TPU v7x, 32 devices: a whole 2x2x4 slice. The times are simulated.
32 devices in a mesh: dp: 16 (over z, x, core), sp: 2 (over y).
Axes of the slice: x: 2, y: 2, z: 4, core: 2. Of those that a mesh axis runs over, the one named last changes fastest.
Arguments:
- tokens: bfloat16 [4096, 1024], P(('dp', 'sp')), may hold values from -6 to 6
- seq_start: int32 [4096], P('dp'), may hold values from 0 to 192, as said below
- qkv_weight: bfloat16 [2, 1024, 3072], P(None, 'dp'), may hold values from -0.1875 to 0.1875
- out_weight: bfloat16 [2, 1024, 1024], P(None, 'dp'), may hold values from -0.1875 to 0.1875
- fc1_weight: bfloat16 [2, 1024, 4096], P(None, 'dp'), may hold values from -0.1875 to 0.1875
- fc2_weight: bfloat16 [2, 4096, 1024], P(None, 'dp'), may hold values from -0.09375 to 0.09375
- norm_gain: float32 [2, 3, 1024], replicated, may hold values from 0.5 to 1.5
- norm_bias: float32 [2, 3, 1024], replicated, may hold values from -2.5 to 2.5
- mid_gain: float32 [2, 4096], replicated, may hold values from 0.5 to 1.5
- mid_bias: float32 [2, 4096], replicated, may hold values from -2.5 to 2.5
- head_scale: float32 [2, 16], replicated, may hold values from 0.25 to 1.75
- cotangent: bfloat16 [4096, 1024], P(('dp', 'sp')), may hold values from -6 to 6
Outputs:
- output: bfloat16 [4096, 1024], P(('dp', 'sp'))
- grad_tokens: float32 [4096, 1024], P(('dp', 'sp'))
- grad_qkv: float32 [2, 1024, 3072], P(None, 'dp', 'sp')
- grad_out: float32 [2, 1024, 1024], P(None, 'dp', 'sp')
- grad_fc1: float32 [2, 1024, 4096], P(None, 'dp', 'sp')
- grad_fc2: float32 [2, 4096, 1024], P(None, 'dp', 'sp')
- grad_norm_gain: float32 [2, 3, 1024], replicated
- grad_norm_bias: float32 [2, 3, 1024], replicated
- grad_mid_gain: float32 [2, 4096], replicated
- grad_mid_bias: float32 [2, 4096], replicated
- grad_head_scale: float32 [2, 16], replicated
Inputs may be any that keep to these rules, and one draw needn't show every extreme that they name: Within each dp group of 256 tokens the sequences are aligned runs of 64, 128 or 256 tokens, and seq_start gives each token the index within its group of its sequence's first token. In the first group the first half is one sequence and the last two quarters are sequences of their own.
All inputs are finite; a program needn't handle non-finite values.
Results may differ from a plain program's by a relative error of at most 0.02.
Values may be sent and summed in bfloat16 or wider, within the bound.
No kernel may reach another device: no remote copies, remote signals or barrier semaphores. Data moves between devices by JAX's collectives and lax.ppermute only.
A program may use at most 256 MiB of HBM per device.

v0:
```python
from functools import partial
import math

import jax
import jax.numpy as jnp
from jax import lax
from jax.sharding import PartitionSpec as P

H = 16
HD = 64
LAYERS = 2


norm_eps = 1e-05


def for_sending(array):

    def short(part):
        return part.astype(jnp.bfloat16) if part.dtype == jnp.float32 else part

    return jax.tree.map(short, array)


def norm_forward(values, gain, bias):
    center = values - jnp.mean(values, axis=-1, keepdims=True)
    inverse = lax.rsqrt(jnp.mean(center * center, axis=-1, keepdims=True) + norm_eps)
    normal = center * inverse
    return (normal * gain + bias, normal, inverse)


def norm_backward(upstream, normal, inverse, gain):
    scaled = upstream * gain
    grad_values = inverse * (
        scaled
        - jnp.mean(scaled, axis=-1, keepdims=True)
        - normal * jnp.mean(scaled * normal, axis=-1, keepdims=True)
    )
    return (grad_values, jnp.sum(upstream * normal, axis=0), jnp.sum(upstream, axis=0))


def product(left, right):
    return jnp.dot(left, right, preferred_element_type=jnp.float32)


def block_layout(length):
    block_count = min(4, max(1, length // 512))
    return (block_count, length // block_count)


def score_block(query_block, query_pos, query_start, key_rows, score_scale):
    key_pos = jnp.arange(key_rows.shape[0], dtype=jnp.int32)
    scores = (
        jnp.einsum("qhd,khd->hqk", query_block, key_rows, preferred_element_type=jnp.float32)
        * score_scale
    )
    allowed = (key_pos[None, :] >= query_start[:, None]) & (key_pos[None, :] <= query_pos[:, None])
    return jnp.where(allowed[None], scores, -1e30)


def attend_forward(queries, key_rows, value_rows, starts, score_scale):
    length = queries.shape[0]
    block_count, block_rows = block_layout(length)
    positions = jnp.arange(length, dtype=jnp.int32)
    results, maxima, totals = ([], [], [])
    for block_index in range(block_count):
        row_first = block_index * block_rows
        row_end = row_first + block_rows
        scores = score_block(
            queries[row_first:row_end],
            positions[row_first:row_end],
            starts[row_first:row_end],
            key_rows[:row_end],
            score_scale,
        )
        row_max = jnp.max(scores, axis=-1, keepdims=True)
        exponent = jnp.exp(scores - row_max)
        row_total = jnp.sum(exponent, axis=-1, keepdims=True)
        weights_low = (exponent / row_total).astype(jnp.bfloat16)
        results.append(
            jnp.einsum(
                "hqk,khd->qhd",
                weights_low,
                value_rows[:row_end],
                preferred_element_type=jnp.float32,
            )
        )
        maxima.append(row_max)
        totals.append(row_total)
    return (jnp.concatenate(results, axis=0), maxima, totals)


def attend_backward(queries, key_rows, value_rows, starts, score_scale, grad_out, maxima, totals):
    length, heads_here, head_dim = queries.shape
    block_count, block_rows = block_layout(length)
    positions = jnp.arange(length, dtype=jnp.int32)
    grad_keys = jnp.zeros((length, heads_here, head_dim), jnp.float32)
    grad_values = jnp.zeros((length, heads_here, head_dim), jnp.float32)
    query_grads = []
    for block_index in range(block_count):
        row_first = block_index * block_rows
        row_end = row_first + block_rows
        query_block = queries[row_first:row_end]
        grad_block = grad_out[row_first:row_end]
        scores = score_block(
            query_block,
            positions[row_first:row_end],
            starts[row_first:row_end],
            key_rows[:row_end],
            score_scale,
        )
        weights_full = jnp.exp(scores - maxima[block_index]) / totals[block_index]
        weights_low = weights_full.astype(jnp.bfloat16)
        grad_weights = jnp.einsum(
            "qhd,khd->hqk", grad_block, value_rows[:row_end], preferred_element_type=jnp.float32
        )
        inner = jnp.sum(weights_full * grad_weights, axis=-1, keepdims=True)
        grad_scores = (weights_full * (grad_weights - inner)).astype(jnp.bfloat16)
        query_grads.append(
            jnp.einsum(
                "hqk,khd->qhd", grad_scores, key_rows[:row_end], preferred_element_type=jnp.float32
            )
            * score_scale
        )
        grad_keys = grad_keys.at[:row_end].add(
            jnp.einsum("hqk,qhd->khd", grad_scores, query_block, preferred_element_type=jnp.float32)
            * score_scale
        )
        grad_values = grad_values.at[:row_end].add(
            jnp.einsum("hqk,qhd->khd", weights_low, grad_block, preferred_element_type=jnp.float32)
        )
    return (jnp.concatenate(query_grads, axis=0), grad_keys, grad_values)


def local(
    tokens,
    seq_start,
    qkv_weight,
    out_weight,
    fc1_weight,
    fc2_weight,
    norm_gain,
    norm_bias,
    mid_gain,
    mid_bias,
    head_scale,
    cotangent,
):
    split_count = lax.axis_size("sp")
    split_rank = lax.axis_index("sp")
    local_rows, width_model = tokens.shape
    group_rows = seq_start.shape[0]
    heads_here = H // split_count
    head_width = heads_here * HD
    score_scale = 1.0 / math.sqrt(HD)
    scale_here = lax.dynamic_slice_in_dim(head_scale, split_rank * heads_here, heads_here, axis=1)
    hidden = tokens.astype(jnp.float32)
    kept_layers = []
    kept_matrices = []
    for which_layer in range(LAYERS):
        matrices = (
            lax.all_gather(qkv_weight[which_layer], "dp", axis=0, tiled=True),
            lax.all_gather(out_weight[which_layer], "dp", axis=0, tiled=True),
            lax.all_gather(fc1_weight[which_layer], "dp", axis=0, tiled=True),
            lax.all_gather(fc2_weight[which_layer], "dp", axis=0, tiled=True),
        )
        qkv_full, out_full, up_full, down_full = matrices
        normed, norm_a, inv_a = norm_forward(
            hidden, norm_gain[which_layer, 0], norm_bias[which_layer, 0]
        )
        normed_low = normed.astype(jnp.bfloat16)
        project = (
            product(normed_low, qkv_full)
            .astype(jnp.bfloat16)
            .reshape(local_rows, 3, split_count, head_width)
        )
        by_heads = lax.all_to_all(project, "sp", split_axis=2, concat_axis=0, tiled=True)
        queries = by_heads[:, 0, 0].reshape(group_rows, heads_here, HD)
        key_rows = by_heads[:, 1, 0].reshape(group_rows, heads_here, HD)
        value_rows = by_heads[:, 2, 0].reshape(group_rows, heads_here, HD)
        attended, maxima, totals = attend_forward(
            queries, key_rows, value_rows, seq_start, score_scale
        )
        scaled = (
            (attended * scale_here[which_layer][None, :, None])
            .astype(jnp.bfloat16)
            .reshape(group_rows, 1, head_width)
        )
        gathered = lax.all_to_all(scaled, "sp", split_axis=0, concat_axis=1, tiled=True).reshape(
            local_rows, width_model
        )
        branch = product(gathered, out_full)
        branch_norm, norm_z, inv_z = norm_forward(
            branch, norm_gain[which_layer, 1], norm_bias[which_layer, 1]
        )
        middle = hidden + branch_norm
        normed_ff, norm_b, inv_b = norm_forward(
            middle, norm_gain[which_layer, 2], norm_bias[which_layer, 2]
        )
        ff_low = normed_ff.astype(jnp.bfloat16)
        pre_act = product(ff_low, up_full)
        activated = jax.nn.gelu(pre_act, approximate=False)
        mixed, norm_m, inv_m = norm_forward(activated, mid_gain[which_layer], mid_bias[which_layer])
        mixed_low = mixed.astype(jnp.bfloat16)
        hidden = middle + product(mixed_low, down_full)
        kept_layers.append(
            (
                norm_a,
                inv_a,
                normed_low,
                queries,
                key_rows,
                value_rows,
                attended,
                maxima,
                totals,
                gathered,
                norm_z,
                inv_z,
                norm_b,
                inv_b,
                ff_low,
                pre_act,
                norm_m,
                inv_m,
                mixed_low,
            )
        )
        kept_matrices.append(matrices)
    output = hidden.astype(jnp.bfloat16)
    grad_hidden = cotangent.astype(jnp.float32)
    matrix_grads = [None] * LAYERS
    gain_grads = [None] * LAYERS
    bias_grads = [None] * LAYERS
    mid_gain_grads = [None] * LAYERS
    mid_bias_grads = [None] * LAYERS
    scale_grads = [None] * LAYERS
    for which_layer in reversed(range(LAYERS)):
        (
            norm_a,
            inv_a,
            normed_low,
            queries,
            key_rows,
            value_rows,
            attended,
            maxima,
            totals,
            gathered,
            norm_z,
            inv_z,
            norm_b,
            inv_b,
            ff_low,
            pre_act,
            norm_m,
            inv_m,
            mixed_low,
        ) = kept_layers[which_layer]
        qkv_full, out_full, up_full, down_full = (
            lax.all_gather(qkv_weight[which_layer], "dp", axis=0, tiled=True),
            lax.all_gather(out_weight[which_layer], "dp", axis=0, tiled=True),
            lax.all_gather(fc1_weight[which_layer], "dp", axis=0, tiled=True),
            lax.all_gather(fc2_weight[which_layer], "dp", axis=0, tiled=True),
        )
        grad_final = grad_hidden.astype(jnp.bfloat16)
        grad_mixed = product(grad_final, down_full.T)
        grad_act, mid_gain_grad, mid_bias_grad = norm_backward(
            grad_mixed, norm_m, inv_m, mid_gain[which_layer]
        )
        gelu_value, gelu_pull = jax.vjp(partial(jax.nn.gelu, approximate=False), pre_act)
        grad_pre = gelu_pull(grad_act)[0].astype(jnp.bfloat16)
        grad_ff_in = product(grad_pre, up_full.T)
        grad_mid_in, gain_two, bias_two = norm_backward(
            grad_ff_in, norm_b, inv_b, norm_gain[which_layer, 2]
        )
        grad_middle = grad_hidden + grad_mid_in
        grad_branch_full, gain_one, bias_one = norm_backward(
            grad_middle, norm_z, inv_z, norm_gain[which_layer, 1]
        )
        grad_branch = grad_branch_full.astype(jnp.bfloat16)
        grad_gathered = (
            product(grad_branch, out_full.T)
            .astype(jnp.bfloat16)
            .reshape(local_rows, split_count, head_width)
        )
        grad_heads = lax.all_to_all(
            grad_gathered, "sp", split_axis=1, concat_axis=0, tiled=True
        ).reshape(group_rows, heads_here, HD)
        scale_grad_here = jnp.sum(grad_heads.astype(jnp.float32) * attended, axis=(0, 2))
        grad_attended = (grad_heads * scale_here[which_layer][None, :, None]).astype(jnp.bfloat16)
        grad_queries, grad_keys, grad_values = attend_backward(
            queries, key_rows, value_rows, seq_start, score_scale, grad_attended, maxima, totals
        )
        stacked = jnp.stack(
            [
                grad_queries.reshape(group_rows, head_width),
                grad_keys.reshape(group_rows, head_width),
                grad_values.reshape(group_rows, head_width),
            ],
            axis=1,
        )
        stacked = stacked.astype(jnp.bfloat16).reshape(group_rows, 3, 1, head_width)
        back_rows = lax.all_to_all(stacked, "sp", split_axis=0, concat_axis=2, tiled=True).reshape(
            local_rows, 3 * width_model
        )
        grad_normed = product(back_rows, qkv_full.T)
        grad_input, gain_zero, bias_zero = norm_backward(
            grad_normed, norm_a, inv_a, norm_gain[which_layer, 0]
        )
        grad_hidden = grad_middle + grad_input
        group_inputs = (
            lax.all_gather(normed_low, "sp", axis=0, tiled=True),
            lax.all_gather(gathered, "sp", axis=0, tiled=True),
            lax.all_gather(ff_low, "sp", axis=0, tiled=True),
            lax.all_gather(mixed_low, "sp", axis=0, tiled=True),
        )
        group_columns = (
            lax.all_to_all(
                back_rows.reshape(local_rows, split_count, -1),
                "sp",
                split_axis=1,
                concat_axis=0,
                tiled=True,
            ),
            lax.all_to_all(
                grad_branch.reshape(local_rows, split_count, -1),
                "sp",
                split_axis=1,
                concat_axis=0,
                tiled=True,
            ),
            lax.all_to_all(
                grad_pre.reshape(local_rows, split_count, -1),
                "sp",
                split_axis=1,
                concat_axis=0,
                tiled=True,
            ),
            lax.all_to_all(
                grad_final.reshape(local_rows, split_count, -1),
                "sp",
                split_axis=1,
                concat_axis=0,
                tiled=True,
            ),
        )
        terms = tuple(
            (
                product(group_inputs[which].T, group_columns[which].reshape(group_rows, -1))
                for which in range(4)
            )
        )
        matrix_grads[which_layer] = jax.tree.map(
            lambda part: part.astype(jnp.float32),
            lax.psum_scatter(for_sending(terms), "dp", scatter_dimension=0, tiled=True),
        )
        gain_grads[which_layer] = jnp.stack([gain_zero, gain_one, gain_two])
        bias_grads[which_layer] = jnp.stack([bias_zero, bias_one, bias_two])
        mid_gain_grads[which_layer] = mid_gain_grad
        mid_bias_grads[which_layer] = mid_bias_grad
        scale_grads[which_layer] = lax.dynamic_update_slice(
            jnp.zeros((H,), jnp.float32), scale_grad_here, (split_rank * heads_here,)
        )
    summed = tuple((jnp.stack([pieces[which] for pieces in matrix_grads]) for which in range(4)))
    small_sums = lax.psum(
        (
            jnp.stack(gain_grads),
            jnp.stack(bias_grads),
            jnp.stack(mid_gain_grads),
            jnp.stack(mid_bias_grads),
            jnp.stack(scale_grads),
        ),
        ("dp", "sp"),
    )
    return (
        output,
        grad_hidden,
        summed[0],
        summed[1],
        summed[2],
        summed[3],
        small_sums[0],
        small_sums[1],
        small_sums[2],
        small_sums[3],
        small_sums[4],
    )


def solution(mesh):
    in_specs = (
        P(("dp", "sp"), None),
        P("dp"),
        P(None, "dp", None),
        P(None, "dp", None),
        P(None, "dp", None),
        P(None, "dp", None),
        P(),
        P(),
        P(),
        P(),
        P(),
        P(("dp", "sp"), None),
    )
    out_specs = (
        P(("dp", "sp"), None),
        P(("dp", "sp"), None),
        P(None, "dp", "sp"),
        P(None, "dp", "sp"),
        P(None, "dp", "sp"),
        P(None, "dp", "sp"),
        P(),
        P(),
        P(),
        P(),
        P(),
    )
    return jax.shard_map(local, mesh=mesh, in_specs=in_specs, out_specs=out_specs, check_vma=False)
```

profile of v0, /device:TPU:0, one launch (start us, length us, event | category | flops | bytes accessed | tf_op | source)
XLA Modules:
  0.0 1390.0 jit_solution(9248600503546498401)
XLA Ops:
  16.0 59.0 %all-gather.23.cloned.1.call-done = bf16[1,1024,3072]{2,1,0:T(8,128)(2,1)} async-done(((bf16[1,64,3072]{2,1,0:T(8,128)(2,1)}), bf16[1,1024,3072]{2,1,0:T(8,128)(2,1)}) %all-gather.23.cloned.1.call-update) | async-done | bytes 6291472 | tf_op jit(solution)/shard_map/all_gather | solution.py:162
  75.0 3.8 fusion.26
  84.1 11.4 all-to-all-done
  104.5 5.1 all-to-all-done.1
  110.1 7.9 all-gather.25.cloned.1.call-done
  121.6 72.1 %all-gather.27.cloned.1.call-done = bf16[1,1024,4096]{2,1,0:T(8,128)(2,1)} async-done(((bf16[1,64,4096]{2,1,0:T(8,128)(2,1)}), bf16[1,1024,4096]{2,1,0:T(8,128)(2,1)}) %all-gather.27.cloned.1.call-update) | async-done | bytes 8388624 | tf_op jit(solution)/shard_map/all_gather | solution.py:164
  193.7 9.0 fusion.112
  204.5 64.7 %all-gather.29.cloned.1.call-done = bf16[1,4096,1024]{2,1,0:T(8,128)(2,1)} async-done(((bf16[1,256,1024]{2,1,0:T(8,128)(2,1)}), bf16[1,4096,1024]{2,1,0:T(8,128)(2,1)}) %all-gather.29.cloned.1.call-update) | async-done | bytes 8388624 | tf_op jit(solution)/shard_map/all_gather | solution.py:165
  269.2 5.1 fusion.127
  275.4 55.9 %all-gather.31.cloned.1.call-done = bf16[1,1024,3072]{2,1,0:T(8,128)(2,1)} async-done(((bf16[1,64,3072]{2,1,0:T(8,128)(2,1)}), bf16[1,1024,3072]{2,1,0:T(8,128)(2,1)}) %all-gather.31.cloned.1.call-update) | async-done | bytes 6291472 | tf_op jit(solution)/shard_map/all_gather | solution.py:162
  331.4 4.8 fusion.29
  340.6 13.9 %all_to_all.234 = bf16[128,3,2,512]{3,0,1,2:T(8,128)(2,1)S(1)} all-to-all(bf16[128,3,2,512]{3,0,1,2:T(8,128)(2,1)S(1)} %copy.111), channel_id=1, replica_groups=mesh['dp'=16,'sp'=2] {'sp'}, dimensions={2} | all-to-all | bytes 1572864 | tf_op jit(solution)/shard_map/all_to_all | solution.py:177
  365.7 8.7 all_to_all.235
  383.0 65.8 %all-gather.35.cloned.1.call-done = bf16[1,1024,4096]{2,1,0:T(8,128)(2,1)} async-done(((bf16[1,64,4096]{2,1,0:T(8,128)(2,1)}), bf16[1,1024,4096]{2,1,0:T(8,128)(2,1)}) %all-gather.35.cloned.1.call-update) | async-done | bytes 8388624 | tf_op jit(solution)/shard_map/all_gather | solution.py:164
  448.8 9.0 fusion.109
  459.5 64.3 %all-gather.37.cloned.1.call-done = bf16[1,4096,1024]{2,1,0:T(8,128)(2,1)} async-done(((bf16[1,256,1024]{2,1,0:T(8,128)(2,1)}), bf16[1,4096,1024]{2,1,0:T(8,128)(2,1)}) %all-gather.37.cloned.1.call-update) | async-done | bytes 8388624 | tf_op jit(solution)/shard_map/all_gather | solution.py:165
  523.8 7.6 multiply_reduce_fusion
  534.2 6.8 multiply_reduce_fusion.12
  547.6 4.2 all-to-all-start.4
  552.6 5.2 all-to-all-done.4
  578.9 4.1 pad_maximum_fusion
  583.0 4.4 all-to-all-start.5
  589.2 25.8 %all_gather.67 = bf16[256,1024]{0,1:T(8,128)(2,1)} all-gather(bf16[128,1024]{0,1:T(8,128)(2,1)} %bitcast.329), channel_id=1, replica_groups=mesh['dp'=16,'sp'=2] {'sp'}, dimensions={0}, use_global_device_ids=true | all-gather | bytes 786432 | tf_op jit(solution)/shard_map/all_gather | solution.py:314
  621.1 5.6 multiply_reduce_fusion.14
  627.4 6.9 multiply_reduce_fusion.1
  647.4 3.9 all-to-all-done.6
  669.4 7.3 all-to-all-done.7
  676.8 4.1 all-to-all-start.11
  684.3 6.1 fusion.91
  698.4 8.0 all_gather.66
  711.5 10.7 all_gather.65
  731.1 10.7 all_gather.64
  749.1 3.8 all-to-all-start.13
  753.0 12.1 all_gather.69
  774.3 13.7 all_gather.68
  792.2 9.1 all_to_all.236
  801.3 4.9 convolution_convert_fusion.1
  807.3 7.6 all_to_all.237
  815.0 4.9 convolution_convert_fusion
  821.1 5.5 fusion.60
  830.5 48.1 %reduce-scatter.15.cloned.1.call-done = bf16[64,512]{1,0:T(8,128)(2,1)} async-done(((bf16[1024,512]{1,0:T(8,128)(2,1)}), bf16[64,512]{1,0:T(8,128)(2,1)}) %reduce-scatter.15.cloned.1.call-update) | async-done | bytes 65552 | tf_op jit(solution)/shard_map/reduce_scatter | solution.py:356
  878.5 60.3 %reduce-scatter.13.cloned.1.call-done = bf16[64,512]{1,0:T(8,128)(2,1)} async-done(((bf16[1024,512]{1,0:T(8,128)(2,1)}), bf16[64,512]{1,0:T(8,128)(2,1)}) %reduce-scatter.13.cloned.1.call-update) | async-done | bytes 65552 | tf_op jit(solution)/shard_map/reduce_scatter | solution.py:356
  940.4 67.5 %reduce-scatter.11.cloned.1.call-done = bf16[64,1536]{1,0:T(8,128)(2,1)} async-done(((bf16[1024,1536]{1,0:T(8,128)(2,1)}), bf16[64,1536]{1,0:T(8,128)(2,1)}) %reduce-scatter.11.cloned.1.call-update) | async-done | bytes 196624 | tf_op jit(solution)/shard_map/reduce_scatter | solution.py:356
  1007.9 69.1 %reduce-scatter.9.cloned.1.call-done = bf16[64,1536]{1,0:T(8,128)(2,1)} async-done(((bf16[1024,1536]{1,0:T(8,128)(2,1)}), bf16[64,1536]{1,0:T(8,128)(2,1)}) %reduce-scatter.9.cloned.1.call-update) | async-done | bytes 196624 | tf_op jit(solution)/shard_map/reduce_scatter | solution.py:356
  1078.9 73.4 %reduce-scatter.19.cloned.1.call-done = bf16[64,2048]{1,0:T(8,128)(2,1)} async-done(((bf16[1024,2048]{1,0:T(8,128)(2,1)}), bf16[64,2048]{1,0:T(8,128)(2,1)}) %reduce-scatter.19.cloned.1.call-update) | async-done | bytes 262160 | tf_op jit(solution)/shard_map/reduce_scatter | solution.py:356
  1152.3 75.6 %reduce-scatter.17.cloned.1.call-done = bf16[64,2048]{1,0:T(8,128)(2,1)} async-done(((bf16[1024,2048]{1,0:T(8,128)(2,1)}), bf16[64,2048]{1,0:T(8,128)(2,1)}) %reduce-scatter.17.cloned.1.call-update) | async-done | bytes 262160 | tf_op jit(solution)/shard_map/reduce_scatter | solution.py:356
  1230.0 73.5 %reduce-scatter.21.cloned.1.call-done = bf16[256,512]{1,0:T(8,128)(2,1)} async-done(((bf16[4096,512]{1,0:T(8,128)(2,1)}), bf16[256,512]{1,0:T(8,128)(2,1)}) %reduce-scatter.21.cloned.1.call-update) | async-done | bytes 262160 | tf_op jit(solution)/shard_map/reduce_scatter | solution.py:356
  1303.5 75.7 %reduce-scatter.23.cloned.1.call-done = bf16[256,512]{1,0:T(8,128)(2,1)} async-done(((bf16[4096,512]{1,0:T(8,128)(2,1)}), bf16[256,512]{1,0:T(8,128)(2,1)}) %reduce-scatter.23.cloned.1.call-update) | async-done | bytes 262160 | tf_op jit(solution)/shard_map/reduce_scatter | solution.py:356
  (424 shorter events, 187.3 us)
Async XLA Ops:
  7.2 67.8 %all-gather.23.cloned.1.call-start = ((), (), s32[]{:S(2)}) async-start(), calls=%async_computation.34 | async-start | bytes 6684672 | tf_op jit(solution)/shard_map/all_gather | solution.py:162
  9.4 108.5 %all-gather.25.cloned.1.call-start = ((), (), s32[]{:S(2)}) async-start(), calls=%async_computation.35 | async-start | bytes 2228224 | tf_op jit(solution)/shard_map/all_gather | solution.py:163
  10.2 183.5 %all-gather.27.cloned.1.call-start = ((), (), s32[]{:S(2)}) async-start(), calls=%async_computation.36 | async-start | bytes 8912896 | tf_op jit(solution)/shard_map/all_gather | solution.py:164
  11.4 257.8 %all-gather.29.cloned.1.call-start = ((), (), s32[]{:S(2)}) async-start(), calls=%async_computation.37 | async-start | bytes 8912896 | tf_op jit(solution)/shard_map/all_gather | solution.py:165
  12.5 318.9 %all-gather.31.cloned.1.call-start = ((), (), s32[]{:S(2)}) async-start(), calls=%async_computation.38 | async-start | bytes 6684672 | tf_op jit(solution)/shard_map/all_gather | solution.py:162
  13.1 364.4 %all-gather.33.cloned.1.call-start = ((), (), s32[]{:S(2)}) async-start(), calls=%async_computation.39 | async-start | bytes 2228224 | tf_op jit(solution)/shard_map/all_gather | solution.py:163
  13.7 435.1 %all-gather.35.cloned.1.call-start = ((), (), s32[]{:S(2)}) async-start(), calls=%async_computation.40 | async-start | bytes 8912896 | tf_op jit(solution)/shard_map/all_gather | solution.py:164
  14.4 509.4 %all-gather.37.cloned.1.call-start = ((), (), s32[]{:S(2)}) async-start(), calls=%async_computation.41 | async-start | bytes 8912896 | tf_op jit(solution)/shard_map/all_gather | solution.py:165
  15.4 63.4 %copy-start.66 = (f32[128]{0:T(128)}, f32[128]{0:T(128)S(1)}, u32[]{:S(2)}) copy-start(f32[128]{0:T(128)S(1)} %broadcast_multiply_fusion.23) | copy-start | bytes 1540
  15.6 63.2 %copy-start.82 = (f32[128]{0:T(128)}, f32[128]{0:T(128)S(1)}, u32[]{:S(2)}) copy-start(f32[128]{0:T(128)S(1)} %add_rsqrt_fusion.7) | copy-start | bytes 1540
  15.9 62.9 %copy-start.21 = (bf16[128,1024]{1,0:T(8,128)(2,1)}, bf16[128,1024]{1,0:T(8,128)(2,1)S(1)}, u32[]{:S(2)}) copy-start(bf16[128,1024]{1,0:T(8,128)(2,1)S(1)} %fusion.86) | copy-start | bytes 786436
  80.4 15.0 %all-to-all-start = ((bf16[128,3,2,512]{3,0,1,2:T(8,128)(2,1)}), bf16[128,3,2,512]{3,0,1,2:T(8,128)(2,1)S(1)}, u32[]{:S(2)}, u32[]{:S(2)}) async-start(bf16[128,3,2,512]{3,0,1,2:T(8,128)(2,1)} %copy.103), calls=%async_computation | async-start | bytes 1572864 | tf_op jit(solution)/shard_map/all_to_all | solution.py:177
  84.0 277.8 %copy-start.92 = (f32[8]{0:T(128)}, f32[8]{0:T(128)S(1)}, u32[]{:S(2)}) copy-start(f32[8]{0:T(128)S(1)} %get-tuple-element.207) | copy-start | bytes 100
  100.8 8.8 all-to-all-start.1
  121.2 81.5 %copy-start.68 = (f32[128]{0:T(128)}, f32[128]{0:T(128)S(1)}, u32[]{:S(2)}) copy-start(f32[128]{0:T(128)S(1)} %broadcast_multiply_fusion.21) | copy-start | bytes 1540
  121.4 81.3 %copy-start.79 = (f32[128]{0:T(128)}, f32[128]{0:T(128)S(1)}, u32[]{:S(2)}) copy-start(f32[128]{0:T(128)S(1)} %add_rsqrt_fusion.5) | copy-start | bytes 1540
  121.6 81.1 %copy-start.45 = (bf16[128,1024]{1,0:T(8,128)(2,1)}, bf16[128,1024]{1,0:T(8,128)(2,1)S(1)}, u32[]{:S(2)}) copy-start(bf16[128,1024]{1,0:T(8,128)(2,1)S(1)} %add_convert_fusion.6) | copy-start | bytes 786436
  203.1 71.2 %copy-start.86 = (f32[128]{0:T(128)}, f32[128]{0:T(128)S(1)}, u32[]{:S(2)}) copy-start(f32[128]{0:T(128)S(1)} %add_rsqrt_fusion.4) | copy-start | bytes 1540
  274.3 61.8 %copy-start.4 = (f32[128,1024]{1,0:T(8,128)}, f32[128,1024]{1,0:T(8,128)S(1)}, u32[]{:S(2)}) copy-start(f32[128,1024]{1,0:T(8,128)S(1)} %get-tuple-element.217) | copy-start | bytes 1572868
  274.4 61.8 %copy-start.71 = (f32[128]{0:T(128)}, f32[128]{0:T(128)S(1)}, u32[]{:S(2)}) copy-start(f32[128]{0:T(128)S(1)} %broadcast_multiply_fusion.20) | copy-start | bytes 1540
  379.9 77.8 %copy-start.75 = (f32[128]{0:T(128)}, f32[128]{0:T(128)S(1)}, u32[]{:S(2)}) copy-start(f32[128]{0:T(128)S(1)} %add_rsqrt_fusion.2) | copy-start | bytes 1540
  381.9 152.3 %copy-start.70 = (f32[128]{0:T(128)}, f32[128]{0:T(128)S(1)}, u32[]{:S(2)}) copy-start(f32[128]{0:T(128)S(1)} %broadcast_multiply_fusion.18) | copy-start | bytes 1540
  382.1 152.0 %copy-start.81 = (f32[128]{0:T(128)}, f32[128]{0:T(128)S(1)}, u32[]{:S(2)}) copy-start(f32[128]{0:T(128)S(1)} %add_rsqrt_fusion.1) | copy-start | bytes 1540
  547.6 10.2 all-to-all-start.4
  551.8 249.5 %all-gather.19.cloned.1.call-start = ((), (), s32[]{:S(2)}) async-start(), calls=%async_computation.30 | async-start | bytes 3145728 | tf_op jit(solution)/shard_map/all_gather | solution.py:316
  583.0 33.5 %all-to-all-start.5 = ((bf16[256,3,1,512]{3,1,2,0:T(4,128)(2,1)}), bf16[256,3,1,512]{3,1,2,0:T(4,128)(2,1)}, u32[]{:S(2)}, u32[]{:S(2)}) async-start(bf16[256,3,1,512]{3,1,2,0:T(4,128)(2,1)} %pad_maximum_fusion), calls=%async_computation.5 | async-start | bytes 2097152 | tf_op jit(solution)/shard_map/all_to_all | solution.py:304
  587.4 227.6 %all-gather.21.cloned.1.call-start = ((), (), s32[]{:S(2)}) async-start(), calls=%async_computation.32 | async-start | bytes 3145728 | tf_op jit(solution)/shard_map/all_gather | solution.py:316
  642.5 8.8 all-to-all-start.6
  663.7 13.1 all-to-all-start.7
  676.8 15.0 %all-to-all-start.11 = ((bf16[128,2,512]{2,0,1:T(8,128)(2,1)}), bf16[128,2,512]{2,0,1:T(8,128)(2,1)}, u32[]{:S(2)}, u32[]{:S(2)}) async-start(bf16[128,2,512]{2,0,1:T(8,128)(2,1)} %bitcast.308), calls=%async_computation.14 | async-start | bytes 524288 | tf_op jit(solution)/shard_map/all_to_all | solution.py:326
  680.9 146.8 %all-reduce.3.cloned.1.call-start = ((), (), s32[]{:S(2)}) async-start(), calls=%async_computation.42 | async-start | bytes 264192 | tf_op jit(solution)/shard_map/psum | solution.py:366
  691.7 186.8 %reduce-scatter.15.cloned.1.call-start = ((), (), s32[]{:S(2)}) async-start(), calls=%async_computation.27 | async-start | bytes 1114112 | tf_op jit(solution)/shard_map/reduce_scatter | solution.py:356
  694.9 11.6 all-to-all-start.10
  698.4 240.4 %reduce-scatter.13.cloned.1.call-start = ((), (), s32[]{:S(2)}) async-start(), calls=%async_computation.26 | async-start | bytes 1114112 | tf_op jit(solution)/shard_map/reduce_scatter | solution.py:356
  707.9 14.3 %all-to-all-start.9 = ((bf16[128,2,1536]{0,2,1:T(8,128)(2,1)}), bf16[128,2,1536]{0,2,1:T(8,128)(2,1)S(1)}, u32[]{:S(2)}, u32[]{:S(2)}) async-start(bf16[128,2,1536]{0,2,1:T(8,128)(2,1)} %bitcast.81), calls=%async_computation.10 | async-start | bytes 1572864 | tf_op jit(solution)/shard_map/all_to_all | solution.py:319
  711.5 296.4 %reduce-scatter.11.cloned.1.call-start = ((), (), s32[]{:S(2)}) async-start(), calls=%async_computation.25 | async-start | bytes 3342336 | tf_op jit(solution)/shard_map/reduce_scatter | solution.py:356
  727.3 14.5 %all-to-all-start.8 = ((bf16[128,2,1536]{0,2,1:T(8,128)(2,1)}), bf16[128,2,1536]{0,2,1:T(8,128)(2,1)S(1)}, u32[]{:S(2)}, u32[]{:S(2)}) async-start(bf16[128,2,1536]{0,2,1:T(8,128)(2,1)} %bitcast.75), calls=%async_computation.8 | async-start | bytes 1572864 | tf_op jit(solution)/shard_map/all_to_all | solution.py:319
  731.0 345.9 %reduce-scatter.9.cloned.1.call-start = ((), (), s32[]{:S(2)}) async-start(), calls=%async_computation.24 | async-start | bytes 3342336 | tf_op jit(solution)/shard_map/reduce_scatter | solution.py:356
  749.1 16.0 %all-to-all-start.13 = ((bf16[128,2,2048]{2,0,1:T(8,128)(2,1)}), bf16[128,2,2048]{2,0,1:T(8,128)(2,1)S(1)}, u32[]{:S(2)}, u32[]{:S(2)}) async-start(bf16[128,2,2048]{2,0,1:T(8,128)(2,1)} %bitcast.314), calls=%async_computation.18 | async-start | bytes 2097152 | tf_op jit(solution)/shard_map/all_to_all | solution.py:333
  752.9 399.4 %reduce-scatter.19.cloned.1.call-start = ((), (), s32[]{:S(2)}) async-start(), calls=%async_computation.29 | async-start | bytes 4456448 | tf_op jit(solution)/shard_map/reduce_scatter | solution.py:356
  770.7 17.3 %all-to-all-start.12 = ((bf16[128,2,2048]{2,0,1:T(8,128)(2,1)}), bf16[128,2,2048]{2,0,1:T(8,128)(2,1)S(1)}, u32[]{:S(2)}, u32[]{:S(2)}) async-start(bf16[128,2,2048]{2,0,1:T(8,128)(2,1)} %bitcast.315), calls=%async_computation.16 | async-start | bytes 2097152 | tf_op jit(solution)/shard_map/all_to_all | solution.py:333
  774.3 453.6 %reduce-scatter.17.cloned.1.call-start = ((), (), s32[]{:S(2)}) async-start(), calls=%async_computation.28 | async-start | bytes 4456448 | tf_op jit(solution)/shard_map/reduce_scatter | solution.py:356
  791.3 512.2 %reduce-scatter.21.cloned.1.call-start = ((), (), s32[]{:S(2)}) async-start(), calls=%async_computation.31 | async-start | bytes 4456448 | tf_op jit(solution)/shard_map/reduce_scatter | solution.py:356
  806.2 573.0 %reduce-scatter.23.cloned.1.call-start = ((), (), s32[]{:S(2)}) async-start(), calls=%async_computation.33 | async-start | bytes 4456448 | tf_op jit(solution)/shard_map/reduce_scatter | solution.py:356
  1076.9 306.1 %copy-start.1 = (f32[2,16]{1,0:T(2,128)S(1)}, f32[2,16]{1,0:T(2,128)}, u32[]{:S(2)}) copy-start(f32[2,16]{1,0:T(2,128)} %param.38) | copy-start | bytes 388
  1076.9 304.3 %copy-start.63 = (f32[2,4096]{1,0:T(2,128)S(1)}, f32[2,4096]{1,0:T(2,128)}, u32[]{:S(2)}) copy-start(f32[2,4096]{1,0:T(2,128)} %get-tuple-element.245) | copy-start | bytes 98308
  1076.9 304.9 %copy-start.62 = (f32[2,4096]{1,0:T(2,128)S(1)}, f32[2,4096]{1,0:T(2,128)}, u32[]{:S(2)}) copy-start(f32[2,4096]{1,0:T(2,128)} %get-tuple-element.246) | copy-start | bytes 98308
  1077.0 305.5 %copy-start.89 = (f32[2,16]{1,0:T(2,128)S(1)}, f32[2,16]{1,0:T(2,128)}, u32[]{:S(2)}) copy-start(f32[2,16]{1,0:T(2,128)} %get-tuple-element.247) | copy-start | bytes 388
  (81 other events, 442.6 us)
Sparse Core Ops, SparseCore 0:
  10.9 64.1 all-gather.22
  77.8 40.1 all-gather.24
  120.7 72.9 all-gather.26
  196.3 72.8 all-gather.28
  271.4 59.9 all-gather.30
  333.4 40.1 all-gather.32
  375.7 73.0 all-gather.34
  450.9 72.8 all-gather.36
  554.8 32.1 all-gather.18
  590.0 39.1 all-gather.20
  691.9 122.2 all-reduce.2
  817.6 60.8 reduce-scatter.14
  882.2 56.6 reduce-scatter.12
  942.5 65.3 reduce-scatter.10
  1011.5 65.3 reduce-scatter.8
  1080.7 71.6 reduce-scatter.18
  1156.0 71.8 reduce-scatter.16
  1231.6 71.8 reduce-scatter.20
  1307.3 71.8 reduce-scatter.22
where the time goes:
time: 1400 us; the launch traced here: 1390 us
  waiting for transfers between devices  969 us (69%)
  matrix products  129 us (9%)
  blocking collectives  120 us (9%)
  local copies, waits for them, and re-layouts  70.3 us (5%)
  starting transfers between devices  46.2 us (3%)
  other arithmetic  39.1 us (3%)
  between operations  16.1 us (1%)
    reduce_scatter x8, waiting for transfers between devices, local(): lax.psum_scatter(for_sending(terms), 'dp', scatter_dimension=0, tiled=True)  543 us
    all_gather x2, waiting for transfers between devices, local(): lax.all_gather(fc1_weight[which_layer], 'dp', axis=0, tiled=True)  138 us
    all_gather x2, waiting for transfers between devices, local(): lax.all_gather(fc2_weight[which_layer], 'dp', axis=0, tiled=True)  129 us
    all_gather x2, waiting for transfers between devices, local(): lax.all_gather(qkv_weight[which_layer], 'dp', axis=0, tiled=True)  115 us
    dot_general x24, matrix products, product(): return jnp.dot(left, right, preferred_element_type=jnp.float32)  106 us
    all_gather x2, blocking collectives, local(): lax.all_gather(gathered, 'sp', axis=0, tiled=True)  33.8 us
  transfers between devices with their start and end apart: 31, of which 20 were waited for; matrix products, arithmetic and copies ran while one was open for 14% of the time, Pallas kernels for 0%

commit v1 on v0

--- a/solution.py
+++ b/solution.py
@@ -4,7 +4,7 @@
 import jax
 import jax.numpy as jnp
 from jax import lax
-from jax.sharding import PartitionSpec as P
+from jax.sharding import Mesh, PartitionSpec as P
 
 H = 16
 HD = 64
@@ -132,7 +132,7 @@
     return (jnp.concatenate(query_grads, axis=0), grad_keys, grad_values)
 
 
-def local(
+def local_any(
     tokens,
     seq_start,
     qkv_weight,
@@ -388,32 +388,421 @@
     )
 
 
+SWAP = ((0, 1), (1, 0))
+
+
+def swap(array, axis):
+    return lax.ppermute(array, axis, SWAP)
+
+
+def shift(array, axis, count, step):
+    return lax.ppermute(array, axis, [(i, (i + step) % count) for i in range(count)])
+
+
+def gather_rows(part):
+    pair = jnp.concatenate([part, swap(part, "y")], axis=0)
+    return jnp.concatenate([pair, swap(pair, "c")], axis=0)
+
+
+def reduce_rows(partial_sum):
+    half = partial_sum.shape[0] // 2
+    mine = partial_sum[:half] + swap(partial_sum[half:].astype(jnp.bfloat16), "c").astype(
+        jnp.float32
+    )
+    half = half // 2
+    return mine[:half] + swap(mine[half:].astype(jnp.bfloat16), "y").astype(jnp.float32)
+
+
+def sum_four(values):
+    values = values + swap(values, "c")
+    return values + swap(values, "y")
+
+
+def from_there(array, axis_name, axis):
+    blocks = 2 if axis_name == "c" else 4
+    there = jnp.split(swap(array, axis_name), blocks, axis=axis)
+    order = (1, 0) if axis_name == "c" else (1, 0, 3, 2)
+    return jnp.concatenate([there[which] for which in order], axis=axis)
+
+
+def sum_rows(values):
+    values = values + from_there(values, "c", values.ndim - 1)
+    return values + from_there(values, "y", values.ndim - 1)
+
+
+def reorder(array, order, axis):
+    return jnp.concatenate(
+        [lax.dynamic_index_in_dim(array, which, axis, keepdims=True) for which in order], axis=axis
+    )
+
+
+def local_four(
+    tokens,
+    seq_start,
+    qkv_weight,
+    out_weight,
+    fc1_weight,
+    fc2_weight,
+    norm_gain,
+    norm_bias,
+    mid_gain,
+    mid_bias,
+    head_scale,
+    cotangent,
+):
+    nz, nx = lax.axis_size("z"), lax.axis_size("x")
+    iz, ix, ic, iy = (lax.axis_index(name) for name in ("z", "x", "c", "y"))
+    rows, width = tokens.shape
+    group_rows = seq_start.shape[0]
+    hidden_width = fc1_weight.shape[2]
+    chips = nz * nx
+    quarter = 2 * iy + ic
+    quarter_there = 2 * iy + 1 - ic
+    unit_quarter = 2 * ic + iy
+    unit_quarter_there = 2 * (1 - ic) + iy
+    chip_rows = width // chips
+    core_rows = chip_rows // 2
+    heads_here = H // 4
+    head_width = width // 4
+    score_scale = 1.0 / math.sqrt(HD)
+    f32, bf16 = jnp.float32, jnp.bfloat16
+
+    far = [((iz - k // nx) % nz, (ix - k % nx) % nx) for k in range(chips)]
+    relative = [a * nx + b for a, b in far]
+    absolute = [((iz - k // nx) % nz) * nx + (ix - k % nx) % nx for k in range(chips)]
+
+    def to_relative(values):
+        blocks = values.reshape(values.shape[0], chips, -1)
+        return reorder(blocks, relative, 1).reshape(values.shape)
+
+    def to_absolute(values):
+        blocks = values.reshape(values.shape[0], chips, -1)
+        return reorder(blocks, absolute, 1).reshape(values.shape)
+
+    def core_order(own, other):
+        first = jnp.where(ic == 0, own, other)
+        second = jnp.where(ic == 0, other, own)
+        return jnp.concatenate([first, second], axis=0)
+
+    def pieces(which_layer):
+        def columns(weight, parts, blocks, which):
+            view = weight.reshape(weight.shape[0], parts, blocks, -1)
+            return lax.dynamic_index_in_dim(view, which, 2, keepdims=False).reshape(
+                weight.shape[0], -1
+            )
+
+        qkv, out = qkv_weight[which_layer], out_weight[which_layer]
+        up, down = fc1_weight[which_layer], fc2_weight[which_layer]
+        own = jnp.concatenate([columns(qkv, 3, 4, quarter), columns(out, 1, 4, quarter)], axis=1)
+        send = jnp.concatenate(
+            [columns(qkv, 3, 4, quarter_there), columns(out, 1, 4, quarter_there)], axis=1
+        )
+        first = core_order(own, swap(send, "c"))
+        own = columns(up, chips, 4, unit_quarter)
+        send = columns(up, chips, 4, unit_quarter_there)
+        second = core_order(own, swap(send, "c"))
+        third = lax.dynamic_slice_in_dim(down, iy * (down.shape[0] // 2), down.shape[0] // 2, 0)
+        return first, second, third
+
+    def gather_chips(part):
+        got = []
+        for step in range(nz):
+            here = part if step == 0 else shift(part, "z", nz, step)
+            got.append(here)
+            for side in range(1, nx):
+                got.append(shift(here, "x", nx, side))
+        return got
+
+    def scatter_chips(blocks):
+        held = blocks[:, 0].astype(f32)
+        for side in range(1, nx):
+            there = blocks[:, side].astype(bf16)
+            held = held + lax.ppermute(
+                there, "x", [(i, (i - side) % nx) for i in range(nx)]
+            ).astype(f32)
+        total = held[0]
+        for step in range(1, nz):
+            total = total + lax.ppermute(
+                held[step].astype(bf16), "z", [(i, (i - step) % nz) for i in range(nz)]
+            ).astype(f32)
+        return total
+
+    first0, second0, third0 = pieces(0)
+    first1, second1, third1 = pieces(1)
+    got0 = gather_chips(first0)
+    got0b = gather_chips(jnp.stack([second0, third0]))
+    got1 = gather_chips(jnp.stack([first1, second1, third1]))
+    firsts = [jnp.concatenate(got0, axis=0), jnp.concatenate([g[0] for g in got1], axis=0)]
+    seconds = [
+        jnp.concatenate([g[0] for g in got0b], axis=0),
+        jnp.concatenate([g[1] for g in got1], axis=0),
+    ]
+    thirds = [
+        reorder(jnp.stack([g[1] for g in got0b]), absolute, 0).reshape(-1, width),
+        reorder(jnp.stack([g[2] for g in got1]), absolute, 0).reshape(-1, width),
+    ]
+
+    def out_rows(block):
+        view = block.reshape(nz, nx * chip_rows, head_width)
+
+        def rows_of(which):
+            return lax.dynamic_index_in_dim(view, (iz - which) % nz, 0, keepdims=False)
+
+        own = rows_of(quarter)
+        own_y = rows_of(2 * (1 - iy) + ic)
+        there = rows_of(quarter_there)
+        there_y = rows_of(2 * (1 - iy) + 1 - ic)
+        other, other_y = swap((there, there_y), "c")
+        mine = jnp.where(ic == 0, jnp.stack([own, other]), jnp.stack([other, own]))
+        mine_y = jnp.where(ic == 0, jnp.stack([own_y, other_y]), jnp.stack([other_y, own_y]))
+        from_y = swap(mine_y, "y")
+        both = jnp.where(iy == 0, jnp.stack([mine, from_y]), jnp.stack([from_y, mine]))
+        both = both.reshape(4, nx, chip_rows, head_width)
+        both = reorder(both, [(ix - k) % nx for k in range(nx)], 1)
+        return both.transpose(1, 2, 0, 3).reshape(nx * chip_rows, width)
+
+    qkv_mats = [block[:, : 3 * head_width] for block in firsts]
+    out_mats = [out_rows(block[:, 3 * head_width :]) for block in firsts]
+    up_mats, down_mats = seconds, thirds
+
+    own_pos = iy * rows + jnp.arange(rows, dtype=jnp.int32)
+    there_pos = (1 - iy) * rows + jnp.arange(rows, dtype=jnp.int32)
+    pos = jnp.concatenate([own_pos, there_pos])
+    starts = jnp.concatenate(
+        [
+            lax.dynamic_slice_in_dim(seq_start, iy * rows, rows),
+            lax.dynamic_slice_in_dim(seq_start, (1 - iy) * rows, rows),
+        ]
+    )
+    starts = jnp.stack([starts, swap(starts, "c")])
+    allowed = (pos[None, None, :] >= starts[:, :, None]) & (
+        pos[None, None, :] <= pos[None, :, None]
+    )
+    allowed = allowed[:, None]
+    scale_here = lax.dynamic_slice_in_dim(head_scale, quarter * heads_here, heads_here, axis=1)
+
+    def mine_of(vector):
+        view = vector.reshape(chips, 4, -1)
+        return lax.dynamic_index_in_dim(view, unit_quarter, 1, keepdims=False).reshape(-1)
+
+    def split_heads(values):
+        return values.reshape(2, group_rows, heads_here, HD)
+
+    hidden = tokens.astype(f32)
+    kept = []
+    for which in range(LAYERS):
+        normed, norm_a, inv_a = norm_forward(hidden, norm_gain[which, 0], norm_bias[which, 0])
+        a_full = gather_rows(to_relative(normed.astype(bf16)))
+        project = product(a_full, qkv_mats[which]).astype(bf16)
+        queries = split_heads(project[:, :head_width])
+        key_rows = split_heads(project[:, head_width : 2 * head_width])
+        value_rows = split_heads(project[:, 2 * head_width :])
+        scores = (
+            jnp.einsum("gqhd,gkhd->ghqk", queries, key_rows, preferred_element_type=f32)
+            * score_scale
+        )
+        scores = jnp.where(allowed, scores, -1e30)
+        row_max = jnp.max(scores, axis=-1, keepdims=True)
+        exponent = jnp.exp(scores - row_max)
+        weights = exponent / jnp.sum(exponent, axis=-1, keepdims=True)
+        weights_low = weights.astype(bf16)
+        attended = jnp.einsum("ghqk,gkhd->gqhd", weights_low, value_rows, preferred_element_type=f32)
+        scaled = (attended * scale_here[which][None, None, :, None]).astype(bf16)
+        scaled = scaled.reshape(2 * group_rows, head_width)
+        y_all = gather_four(scaled, ic, iy)
+        branch = reduce_rows(product(scaled, out_mats[which]))
+        branch_norm, norm_z, inv_z = norm_forward(branch, norm_gain[which, 1], norm_bias[which, 1])
+        middle = hidden + branch_norm
+        normed_ff, norm_b, inv_b = norm_forward(middle, norm_gain[which, 2], norm_bias[which, 2])
+        b_full = gather_rows(to_relative(normed_ff.astype(bf16)))
+        pre_act = product(b_full, up_mats[which])
+        activated = jax.nn.gelu(pre_act, approximate=False)
+        gain_m, bias_m = mine_of(mid_gain[which]), mine_of(mid_bias[which])
+        mean_here = jnp.mean(activated, axis=-1)
+        center = activated - mean_here[:, None]
+        spread_here = jnp.mean(center * center, axis=-1)
+        mean_all = sum_rows(mean_here) * 0.25
+        spread_all = sum_rows(spread_here + (mean_here - mean_all) ** 2) * 0.25
+        inv_m = lax.rsqrt(spread_all + norm_eps)[:, None]
+        norm_m = (activated - mean_all[:, None]) * inv_m
+        mixed_low = (norm_m * gain_m + bias_m).astype(bf16)
+        hidden = middle + reduce_rows(product(mixed_low, down_mats[which]))
+        kept.append(
+            (
+                norm_a, inv_a, a_full, queries, key_rows, value_rows, weights, weights_low, attended,
+                y_all, norm_z, inv_z, norm_b, inv_b, b_full, pre_act, norm_m, inv_m, mixed_low, gain_m,
+            )
+        )
+    output = hidden.astype(bf16)
+    grad_hidden = cotangent.astype(f32)
+    matrix_grads, vector_grads = [None] * LAYERS, [None] * LAYERS
+    for which in reversed(range(LAYERS)):
+        (
+            norm_a, inv_a, a_full, queries, key_rows, value_rows, weights, weights_low, attended,
+            y_all, norm_z, inv_z, norm_b, inv_b, b_full, pre_act, norm_m, inv_m, mixed_low, gain_m,
+        ) = kept[which]
+        final_full = gather_rows(grad_hidden.astype(bf16))
+        grad_mixed = product(final_full, down_mats[which].T)
+        down_term = product(mixed_low.T, final_full)
+        mid_gain_grad = jnp.sum(grad_mixed * norm_m, axis=0)
+        mid_bias_grad = jnp.sum(grad_mixed, axis=0)
+        scaled_grad = grad_mixed * gain_m
+        sums = sum_rows(
+            jnp.stack([jnp.sum(scaled_grad, axis=-1), jnp.sum(scaled_grad * norm_m, axis=-1)])
+        ) / hidden_width
+        grad_act = inv_m * (scaled_grad - sums[0][:, None] - norm_m * sums[1][:, None])
+        gelu_value, gelu_pull = jax.vjp(partial(jax.nn.gelu, approximate=False), pre_act)
+        grad_pre = gelu_pull(grad_act)[0].astype(bf16)
+        grad_ff_in = to_absolute(reduce_rows(product(grad_pre, up_mats[which].T)))
+        up_term = product(b_full.T, grad_pre)
+        grad_mid_in, gain_two, bias_two = norm_backward(
+            grad_ff_in, norm_b, inv_b, norm_gain[which, 2]
+        )
+        grad_middle = grad_hidden + grad_mid_in
+        grad_branch, gain_one, bias_one = norm_backward(
+            grad_middle, norm_z, inv_z, norm_gain[which, 1]
+        )
+        branch_full = gather_rows(grad_branch.astype(bf16))
+        columns_z = lax.dynamic_slice_in_dim(branch_full, quarter * head_width, head_width, 1)
+        out_term = product(y_all.T, columns_z)
+        grad_scaled = product(branch_full, out_mats[which].T).astype(bf16)
+        grad_heads = split_heads(grad_scaled)
+        scale_grad = jnp.sum(grad_heads.astype(f32) * attended, axis=(0, 1, 3))
+        grad_attended = (grad_heads * scale_here[which][None, None, :, None]).astype(bf16)
+        grad_weights = jnp.einsum(
+            "gqhd,gkhd->ghqk", grad_attended, value_rows, preferred_element_type=f32
+        )
+        inner = jnp.sum(weights * grad_weights, axis=-1, keepdims=True)
+        grad_scores = (weights * (grad_weights - inner)).astype(bf16)
+        grad_queries = jnp.einsum(
+            "ghqk,gkhd->gqhd", grad_scores, key_rows, preferred_element_type=f32
+        ) * score_scale
+        grad_keys = jnp.einsum(
+            "ghqk,gqhd->gkhd", grad_scores, queries, preferred_element_type=f32
+        ) * score_scale
+        grad_values = jnp.einsum(
+            "ghqk,gqhd->gkhd", weights_low, grad_attended, preferred_element_type=f32
+        )
+        grad_project = jnp.concatenate(
+            [
+                part.astype(bf16).reshape(2 * group_rows, head_width)
+                for part in (grad_queries, grad_keys, grad_values)
+            ],
+            axis=1,
+        )
+        grad_normed = to_absolute(reduce_rows(product(grad_project, qkv_mats[which].T)))
+        qkv_term = product(a_full.T, grad_project)
+        grad_input, gain_zero, bias_zero = norm_backward(
+            grad_normed, norm_a, inv_a, norm_gain[which, 0]
+        )
+        grad_hidden = grad_middle + grad_input
+
+        down_blocks = reorder(down_term.astype(bf16).reshape(chips, -1, width), relative, 0)
+        up_blocks = up_term.astype(bf16).reshape(chips, chip_rows, -1)
+        ff_sum = scatter_chips(
+            jnp.stack([up_blocks, down_blocks], axis=1).reshape(nz, nx, 2, chip_rows, -1)
+        )
+        out_blocks = reorder(out_term.astype(bf16).reshape(chips, chip_rows, -1), relative, 0)
+        qkv_blocks = qkv_term.astype(bf16).reshape(chips, chip_rows, -1)
+        at_sum = scatter_chips(
+            jnp.concatenate([qkv_blocks, out_blocks], axis=2).reshape(nz, nx, chip_rows, -1)
+        )
+
+        def core_swap_rows(values):
+            own = lax.dynamic_slice_in_dim(values, ic * core_rows, core_rows, 0)
+            there = lax.dynamic_slice_in_dim(values, (1 - ic) * core_rows, core_rows, 0)
+            other = swap(there.astype(bf16), "c").astype(f32)
+            return jnp.where(ic == 0, jnp.stack([own, other]), jnp.stack([other, own]))
+
+        def y_pair(keep, send):
+            other = swap(send.astype(bf16), "y").astype(f32)
+            return jnp.where(iy == 0, jnp.stack([keep, other]), jnp.stack([other, keep]))
+
+        at_rows = core_swap_rows(at_sum)
+        qkv_rows = at_rows[:, :, : 3 * head_width].reshape(2, core_rows, 3, head_width)
+        q_rows, k_rows, v_rows = (
+            qkv_rows[:, :, part].transpose(1, 0, 2).reshape(core_rows, -1) for part in range(3)
+        )
+        out_part = at_rows[:, :, 3 * head_width :].transpose(1, 0, 2).reshape(core_rows, -1)
+        moved = swap(jnp.where(iy == 0, v_rows, q_rows).astype(bf16), "y").astype(f32)
+        grad_qkv = jnp.where(
+            iy == 0,
+            jnp.concatenate([q_rows, moved, k_rows], axis=1),
+            jnp.concatenate([k_rows, moved, v_rows], axis=1),
+        )
+        grad_out = out_part
+        half_chips = chips // 2
+        up_rows = core_swap_rows(ff_sum[0]).reshape(2, core_rows, chips, -1)
+        up_keep = lax.dynamic_slice_in_dim(up_rows, iy * half_chips, half_chips, 2)
+        up_send = lax.dynamic_slice_in_dim(up_rows, (1 - iy) * half_chips, half_chips, 2)
+        up_both = y_pair(up_keep, up_send)
+        grad_up = up_both.transpose(2, 3, 1, 0, 4).reshape(core_rows, -1)
+        half_width = width // 2
+        down_keep = lax.dynamic_slice_in_dim(ff_sum[1], iy * half_width, half_width, 1)
+        down_send = lax.dynamic_slice_in_dim(ff_sum[1], (1 - iy) * half_width, half_width, 1)
+        grad_down = y_pair(down_keep, down_send).reshape(-1, half_width)
+        matrix_grads[which] = (grad_qkv, grad_out, grad_up, grad_down)
+
+        def spread_units(vector):
+            view = jnp.zeros((chips, 4, hidden_width // chips // 4), f32)
+            return lax.dynamic_update_slice(
+                view, vector.reshape(chips, 1, -1), (0, unit_quarter, 0)
+            ).reshape(-1)
+
+        scale_full = lax.dynamic_update_slice(
+            jnp.zeros((128,), f32), scale_grad, (quarter * heads_here,)
+        )
+        vector = jnp.concatenate(
+            [
+                gain_zero, gain_one, gain_two, bias_zero, bias_one, bias_two,
+                spread_units(mid_gain_grad), spread_units(mid_bias_grad), scale_full,
+            ]
+        )
+        vector = sum_four(vector)
+        vector = vector + swap(vector, "x")
+        for bit in (1, 2):
+            vector = vector + lax.ppermute(vector, "z", [(i, i ^ bit) for i in range(nz)])
+        vector_grads[which] = vector
+
+    summed = [jnp.stack([grads[which] for grads in matrix_grads]) for which in range(4)]
+    vectors = jnp.stack(vector_grads)
+    ends = [0, 3 * width, 6 * width, 6 * width + hidden_width, 6 * width + 2 * hidden_width]
+    return (
+        output,
+        grad_hidden,
+        summed[0],
+        summed[1],
+        summed[2],
+        summed[3],
+        vectors[:, ends[0] : ends[1]].reshape(LAYERS, 3, width),
+        vectors[:, ends[1] : ends[2]].reshape(LAYERS, 3, width),
+        vectors[:, ends[2] : ends[3]],
+        vectors[:, ends[3] : ends[4]],
+        vectors[:, ends[4] : ends[4] + H],
+    )
+
+
+def gather_four(part, ic, iy):
+    other = from_there(part, "c", 0)
+    pair = jnp.where(
+        ic == 0, jnp.concatenate([part, other], axis=1), jnp.concatenate([other, part], axis=1)
+    )
+    there = from_there(pair, "y", 0)
+    return jnp.where(
+        iy == 0, jnp.concatenate([pair, there], axis=1), jnp.concatenate([there, pair], axis=1)
+    )
+
+
 def solution(mesh):
-    in_specs = (
-        P(("dp", "sp"), None),
-        P("dp"),
-        P(None, "dp", None),
-        P(None, "dp", None),
-        P(None, "dp", None),
-        P(None, "dp", None),
-        P(),
-        P(),
-        P(),
-        P(),
-        P(),
-        P(("dp", "sp"), None),
-    )
-    out_specs = (
-        P(("dp", "sp"), None),
-        P(("dp", "sp"), None),
-        P(None, "dp", "sp"),
-        P(None, "dp", "sp"),
-        P(None, "dp", "sp"),
-        P(None, "dp", "sp"),
-        P(),
-        P(),
-        P(),
-        P(),
-        P(),
-    )
-    return jax.shard_map(local, mesh=mesh, in_specs=in_specs, out_specs=out_specs, check_vma=False)
+    dp, sp = mesh.shape["dp"], mesh.shape["sp"]
+    if sp == 2 and dp == 16:
+        mesh = Mesh(mesh.devices.reshape(4, dp // 8, 2, 2), ("z", "x", "c", "y"))
+        rows, every, cols, body = ("z", "x", "c"), ("z", "x", "c", "y"), "y", local_four
+    else:
+        rows, every, cols, body = "dp", ("dp", "sp"), "sp", local_any
+    weight = P(None, rows, None)
+    in_specs = (P(every, None), P(rows), weight, weight, weight, weight)
+    in_specs = in_specs + (P(),) * 5 + (P(every, None),)
+    grad = P(None, rows, cols)
+    out_specs = (P(every, None), P(every, None), grad, grad, grad, grad) + (P(),) * 5
+    return jax.shard_map(body, mesh=mesh, in_specs=in_specs, out_specs=out_specs, check_vma=False)

time: 1400 us -> 777 us (0.56)
  waiting for transfers between devices: 969 us -> 266 us
  starting transfers between devices: 46.2 us -> 174 us
  blocking collectives: 120 us -> 0 us
  local copies, waits for them, and re-layouts: 70.3 us -> 168 us
  matrix products: 129 us -> 71.6 us
  other arithmetic: 39.1 us -> 81.1 us
    reduce_scatter x8 -> x0, waiting for transfers between devices: 543 us -> none  [local(): lax.psum_scatter(for_sending(terms), 'dp', scatter_dimension=0, tiled=True)]
    all_gather x10 -> x0, waiting for transfers between devices: 390 us -> none  [the longest x2 138 us: local(): lax.all_gather(fc1_weight[which_layer], 'dp', axis=0, tiled=True)]
    ppermute x0 -> x116, waiting for transfers between devices: none -> 266 us  [the longest x75 109 us: swap(): return lax.ppermute(array, axis, SWAP)]
    ppermute x0 -> x116, starting transfers between devices: none -> 174 us  [the longest x4 55.4 us: local_four(): lax.ppermute(vector, 'z', [(i, i ^ bit) for i in range(nz)])]
    all_gather x6 -> x0, blocking collectives: 81 us -> none  [the longest x2 33.8 us: local(): lax.all_gather(gathered, 'sp', axis=0, tiled=True)]
    unnamed x210 -> x523, local copies, waits for them, and re-layouts: 22.6 us -> 88.4 us
    dot_general x24, matrix products: 106 us -> 53 us  [product(): return jnp.dot(left, right, preferred_element_type=jnp.float32)]
    all_to_all x12 -> x0, starting transfers between devices: 45.4 us -> none  [the longest x2 8.13 us: local(): lax.all_to_all(stacked, 'sp', split_axis=0, concat_axis=2, tiled=True)]
  transfers between devices with their start and end apart: 31 -> 116, of which waited for: 20 -> 50; matrix products, arithmetic and copies ran while one was open for 14% -> 33% of each run, Pallas kernels for 0% -> 0%
where the time goes in v1:
time: 777 us; the launch traced here: 766 us
  waiting for transfers between devices  266 us (34%)
  starting transfers between devices  174 us (22%)
  local copies, waits for them, and re-layouts  168 us (22%)
  other arithmetic  81.1 us (10%)
  matrix products  71.6 us (9%)
    ppermute x75, waiting for transfers between devices, swap(): return lax.ppermute(array, axis, SWAP)  109 us
    unnamed x523, local copies, waits for them, and re-layouts  88.4 us
    ppermute x21, waiting for transfers between devices, shift(): lax.ppermute(array, axis, [(i, (i + step) % count) for i in range(count)])  75.1 us
    ppermute x4, starting transfers between devices, local_four(): lax.ppermute(vector, 'z', [(i, i ^ bit) for i in range(nz)])  55.4 us
    ppermute x21, starting transfers between devices, shift(): lax.ppermute(array, axis, [(i, (i + step) % count) for i in range(count)])  53.6 us
    dot_general x24, matrix products, product(): return jnp.dot(left, right, preferred_element_type=jnp.float32)  53 us
    ppermute x75, starting transfers between devices, swap(): return lax.ppermute(array, axis, SWAP)  43.8 us
    ppermute x12, waiting for transfers between devices, scatter_chips(): lax.ppermute(held[step].astype(bf16), 'z', [(i, (i - step) % nz) for i in...  43 us
  transfers between devices with their start and end apart: 116, of which 50 were waited for; matrix products, arithmetic and copies ran while one was open for 33% of the time, Pallas kernels for 0%

profile of v1, /device:TPU:0, one launch (start us, length us, event | category | flops | bytes accessed | tf_op | source)
XLA Modules:
  0.0 765.9 jit_solution(2505599094155029676)
XLA Ops:
  14.7 3.0 collective-permute-start.56
  59.9 7.3 collective-permute-start.37
  68.8 14.2 %collective-permute-done.8 = bf16[128,1024]{1,0:T(8,128)(2,1)S(1)} collective-permute-done((bf16[128,1024]{1,0:T(8,128)(2,1)S(1)}, bf16[128,1024]{1,0:T(8,128)(2,1)S(1)}, u32[]{:S(2)}, u32[]{:S(2)}) %collective-permute-start.8) | collective-permute-done | bytes 262176 | tf_op jit(solution)/shard_map/ppermute | solution.py:399
  86.3 3.3 collective-permute-start.39
  89.6 11.6 %collective-permute-done.9 = bf16[128,1024]{1,0:T(8,128)(2,1)S(1)} collective-permute-done((bf16[128,1024]{1,0:T(8,128)(2,1)S(1)}, bf16[128,1024]{1,0:T(8,128)(2,1)S(1)}, u32[]{:S(2)}, u32[]{:S(2)}) %collective-permute-start.9) | collective-permute-done | bytes 262176 | tf_op jit(solution)/shard_map/ppermute | solution.py:399
  101.2 6.7 collective-permute-start.20
  109.8 11.5 %collective-permute-done.20 = bf16[2,128,1024]{2,1,0:T(8,128)(2,1)S(1)} collective-permute-done((bf16[2,128,1024]{2,1,0:T(8,128)(2,1)S(1)}, bf16[2,128,1024]{2,1,0:T(8,128)(2,1)S(1)}, u32[]{:S(2)}, u32[]{:S(2)}) %collective-permute-start.20) | collective-permute-done | bytes 524320 | tf_op jit(solution)/shard_map/ppermute | solution.py:399
  125.6 3.8 fusion.254
  131.0 2.8 multiply_convert_fusion.7
  135.4 16.3 %collective-permute-start.22 = (bf16[2,128,1024]{2,1,0:T(8,128)(2,1)S(1)}, bf16[2,128,1024]{2,1,0:T(8,128)(2,1)S(1)}, u32[]{:S(2)}, u32[]{:S(2)}) collective-permute-start(bf16[2,128,1024]{2,1,0:T(8,128)(2,1)S(1)} %copy-done.68), channel_id=1, source_target_pairs={{0,16},{8,24},{16,0},{24,8},{1,17},{9,25},{17,1},{25,9},{2,18},{10... | collective-permute-start | bytes 1572872 | tf_op jit(solution)/shard_map/ppermute | solution.py:399
  160.6 3.3 collective-permute-done.13
  165.5 10.2 %collective-permute-done.22 = bf16[2,128,1024]{2,1,0:T(8,128)(2,1)S(1)} collective-permute-done((bf16[2,128,1024]{2,1,0:T(8,128)(2,1)S(1)}, bf16[2,128,1024]{2,1,0:T(8,128)(2,1)S(1)}, u32[]{:S(2)}, u32[]{:S(2)}) %collective-permute-start.22) | collective-permute-done | bytes 524320 | tf_op jit(solution)/shard_map/ppermute | solution.py:399
  184.0 10.6 %collective-permute-done.41 = bf16[3,128,1024]{2,1,0:T(8,128)(2,1)} collective-permute-done((bf16[3,128,1024]{2,1,0:T(8,128)(2,1)}, bf16[3,128,1024]{2,1,0:T(8,128)(2,1)}, u32[]{:S(2)}, u32[]{:S(2)}) %collective-permute-start.41) | collective-permute-done | bytes 786464 | tf_op jit(solution)/shard_map/ppermute | solution.py:399
  198.1 3.6 collective-permute-done.23
  203.2 9.8 %collective-permute-done.25 = bf16[2,128,1024]{2,1,0:T(8,128)(2,1)S(1)} collective-permute-done((bf16[2,128,1024]{2,1,0:T(8,128)(2,1)S(1)}, bf16[2,128,1024]{2,1,0:T(8,128)(2,1)S(1)}, u32[]{:S(2)}, u32[]{:S(2)}) %collective-permute-start.25) | collective-permute-done | bytes 524320 | tf_op jit(solution)/shard_map/ppermute | solution.py:399
  223.8 6.2 collective-permute-done.15
  245.0 7.3 fusion.217
  272.2 6.2 collective-permute-done.31
  284.3 4.4 collective-permute-done.32
  328.9 11.6 %fusion.210 = (f32[512]{0:T(512)S(1)}, f32[512,1024]{1,0:T(8,128)S(1)}, f32[512,1024]{1,0:T(8,128)S(1)}, f32[512,1024]{1,0:T(8,128)S(1)}) fusion(bf16[512,1024]{1,0:T(8,128)(2,1)S(1)} %constant_dynamic-update-slice_fusion.23, bf16[1024,1024]{1,0:T(8,128)(2,1)S(1)} %copy-done.149), kind=kOutput, calls=%fused_computation.782 | convolution fusion | flops 1107820032 | bytes 9439232 | tf_op jit(solution)/shard_map/dot_general | solution.py:43
  353.2 9.5 %collective-permute-done.85 = bf16[512,512]{0,1:T(8,128)(2,1)S(1)} collective-permute-done((bf16[512,512]{0,1:T(8,128)(2,1)S(1)}, bf16[512,512]{0,1:T(8,128)(2,1)S(1)}, u32[]{:S(2)}, u32[]{:S(2)}) %collective-permute-start.85) | collective-permute-done | bytes 524320 | tf_op jit(solution)/shard_map/ppermute | solution.py:395
  378.7 4.2 collective-permute-done.61
  388.8 3.0 multiply_reduce_fusion.11
  403.4 4.3 convolution_convert_fusion.1
  425.9 5.9 collective-permute-done.65
  439.0 7.2 collective-permute-done.66
  449.0 3.7 collective-permute-done.112
  453.3 3.7 collective-permute-done.113
  457.0 26.4 %collective-permute-start.114 = (f32[14464]{0:T(1024)S(1)}, f32[14464]{0:T(1024)S(1)}, u32[]{:S(2)}, u32[]{:S(2)}) collective-permute-start(f32[14464]{0:T(1024)S(1)} %add.906), channel_id=1, source_target_pairs={{0,8},{8,0},{16,24},{24,16},{1,9},{9,1},{17,25},{25,17},{2,10},{10... | collective-permute-start | bytes 173576 | tf_op jit(solution)/shard_map/ppermute | solution.py:764
  485.5 3.5 collective-permute-start.115
  501.9 6.0 collective-permute-done.71
  526.9 2.8 convolution_convert_fusion.3
  558.7 16.4 %collective-permute-done.98 = bf16[4,2,128,1024]{3,2,1,0:T(8,128)(2,1)} collective-permute-done((bf16[4,2,128,1024]{3,2,1,0:T(8,128)(2,1)}, bf16[4,2,128,1024]{3,2,1,0:T(8,128)(2,1)}, u32[]{:S(2)}, u32[]{:S(2)}) %collective-permute-start.98) | collective-permute-done | bytes 2097184 | tf_op jit(solution)/shard_map/ppermute | solution.py:520
  575.1 5.4 fusion.198
  589.2 3.1 collective-permute-start.99
  601.3 18.7 %collective-permute-done.92 = bf16[4,2,128,1024]{3,2,0,1:T(8,128)(2,1)} collective-permute-done((bf16[4,2,128,1024]{3,2,0,1:T(8,128)(2,1)}, bf16[4,2,128,1024]{3,2,0,1:T(8,128)(2,1)}, u32[]{:S(2)}, u32[]{:S(2)}) %collective-permute-start.92) | collective-permute-done | bytes 2097184 | tf_op jit(solution)/shard_map/ppermute | solution.py:520
  620.0 2.9 fusion.205
  623.7 3.7 collective-permute-done.107
  628.1 15.2 %collective-permute-done.108 = f32[14464]{0:T(1024)S(1)} collective-permute-done((f32[14464]{0:T(1024)S(1)}, f32[14464]{0:T(1024)S(1)}, u32[]{:S(2)}, u32[]{:S(2)}) %collective-permute-start.108) | collective-permute-done | bytes 57888 | tf_op jit(solution)/shard_map/ppermute | solution.py:395
  648.1 3.1 collective-permute-start.93
  654.1 9.4 %collective-permute-done.93 = bf16[2,128,1024]{2,1,0:T(8,128)(2,1)S(1)} collective-permute-done((bf16[2,128,1024]{2,1,0:T(8,128)(2,1)S(1)}, bf16[2,128,1024]{2,1,0:T(8,128)(2,1)S(1)}, u32[]{:S(2)}, u32[]{:S(2)}) %collective-permute-start.93) | collective-permute-done | bytes 524320 | tf_op jit(solution)/shard_map/ppermute | solution.py:525
  663.5 23.5 %collective-permute-start.110 = (f32[14464]{0:T(1024)S(1)}, f32[14464]{0:T(1024)S(1)}, u32[]{:S(2)}, u32[]{:S(2)}) collective-permute-start(f32[14464]{0:T(1024)S(1)} %add.902), channel_id=1, source_target_pairs={{0,16},{8,24},{16,0},{24,8},{1,17},{9,25},{17,1},{25,9},{2,18},{10... | collective-permute-start | bytes 173576 | tf_op jit(solution)/shard_map/ppermute | solution.py:764
  687.1 10.3 %collective-permute-done.94 = bf16[2,128,1024]{2,1,0:T(8,128)(2,1)S(1)} collective-permute-done((bf16[2,128,1024]{2,1,0:T(8,128)(2,1)S(1)}, bf16[2,128,1024]{2,1,0:T(8,128)(2,1)S(1)}, u32[]{:S(2)}, u32[]{:S(2)}) %collective-permute-start.94) | collective-permute-done | bytes 524320 | tf_op jit(solution)/shard_map/ppermute | solution.py:525
  700.0 3.0 fusion.206
  716.9 3.0 collective-permute-done.103
  721.7 3.3 collective-permute-done.97
  728.9 3.5 collective-permute-done.80
  734.0 19.8 %collective-permute-done.88 = bf16[128,1024]{1,0:T(8,128)(2,1)} collective-permute-done((bf16[128,1024]{1,0:T(8,128)(2,1)}, bf16[128,1024]{1,0:T(8,128)(2,1)}, u32[]{:S(2)}, u32[]{:S(2)}) %collective-permute-start.88) | collective-permute-done | bytes 262176 | tf_op jit(solution)/shard_map/ppermute | solution.py:525
  (1117 shorter events, 382.3 us)
Async XLA Ops:
  7.1 32.6 %collective-permute-start.34 = (bf16[64,1024]{1,0:T(8,128)(2,1)}, bf16[64,1024]{1,0:T(8,128)(2,1)}, u32[]{:S(2)}, u32[]{:S(2)}) collective-permute-start(bf16[64,1024]{1,0:T(8,128)(2,1)} %pad_maximum_fusion.33), channel_id=1, source_target_pairs={{0,2},{2,0},{1,3},{3,1},{4,6},{6,4},{5,7},{7,5},{8,10},{10,8},{9,1... | collective-permute-start | bytes 393224 | tf_op jit(solution)/shard_map/ppermute | solution.py:395
  10.9 32.9 %collective-permute-start.35 = (bf16[64,1024]{1,0:T(8,128)(2,1)}, bf16[64,1024]{1,0:T(8,128)(2,1)}, u32[]{:S(2)}, u32[]{:S(2)}) collective-permute-start(bf16[64,1024]{1,0:T(8,128)(2,1)} %bitcast.629), channel_id=1, source_target_pairs={{0,2},{2,0},{1,3},{3,1},{4,6},{6,4},{5,7},{7,5},{8,10},{10,8},{9,1... | collective-permute-start | bytes 393224 | tf_op jit(solution)/shard_map/ppermute | solution.py:395
  13.5 34.5 %collective-permute-start.18 = (bf16[64,1024]{1,0:T(8,128)(2,1)}, bf16[64,1024]{1,0:T(8,128)(2,1)}, u32[]{:S(2)}, u32[]{:S(2)}) collective-permute-start(bf16[64,1024]{1,0:T(8,128)(2,1)} %bitcast.630), channel_id=1, source_target_pairs={{0,2},{2,0},{1,3},{3,1},{4,6},{6,4},{5,7},{7,5},{8,10},{10,8},{9,1... | collective-permute-start | bytes 393224 | tf_op jit(solution)/shard_map/ppermute | solution.py:395
  14.7 22.4 %collective-permute-start.10 = (s32[256]{0:T(256)}, s32[256]{0:T(256)}, u32[]{:S(2)}, u32[]{:S(2)}) collective-permute-start(s32[256]{0:T(256)} %pad_add_fusion.2), channel_id=1, source_target_pairs={{0,2},{2,0},{1,3},{3,1},{4,6},{6,4},{5,7},{7,5},{8,10},{10,8},{9,1... | collective-permute-start | bytes 3080 | tf_op jit(solution)/shard_map/ppermute | solution.py:395
  14.7 39.6 %collective-permute-start.56 = (bf16[128,1024]{1,0:T(8,128)(2,1)S(1)}, bf16[128,1024]{1,0:T(8,128)(2,1)}, u32[]{:S(2)}, u32[]{:S(2)}) collective-permute-start(bf16[128,1024]{1,0:T(8,128)(2,1)S(1)} %copy-done.19), channel_id=1, source_target_pairs={{0,1},{1,0},{2,3},{3,2},{4,5},{5,4},{6,7},{7,6},{8,9},{9,8},{10,11... | collective-permute-start | bytes 786440 | tf_op jit(solution)/shard_map/ppermute | solution.py:395
  39.7 20.2 %collective-permute-start.3 = (bf16[128,1024]{1,0:T(8,128)(2,1)S(1)}, bf16[128,1024]{1,0:T(8,128)(2,1)S(1)}, u32[]{:S(2)}, u32[]{:S(2)}) collective-permute-start(bf16[128,1024]{1,0:T(8,128)(2,1)S(1)} %pad_maximum_fusion.28), channel_id=1, source_target_pairs={{0,4},{4,0},{1,5},{5,1},{2,6},{6,2},{3,7},{7,3},{8,12},{12,8},{9,1... | collective-permute-start | bytes 786440 | tf_op jit(solution)/shard_map/ppermute | solution.py:399
  48.1 19.2 %collective-permute-start.6 = (bf16[128,1024]{1,0:T(8,128)(2,1)S(1)}, bf16[128,1024]{1,0:T(8,128)(2,1)S(1)}, u32[]{:S(2)}, u32[]{:S(2)}) collective-permute-start(bf16[128,1024]{1,0:T(8,128)(2,1)S(1)} %pad_maximum_fusion.28), channel_id=1, source_target_pairs={{0,16},{8,24},{16,0},{24,8},{1,17},{9,25},{17,1},{25,9},{2,18},{10... | collective-permute-start | bytes 786440 | tf_op jit(solution)/shard_map/ppermute | solution.py:399
  52.9 30.2 %collective-permute-start.8 = (bf16[128,1024]{1,0:T(8,128)(2,1)S(1)}, bf16[128,1024]{1,0:T(8,128)(2,1)S(1)}, u32[]{:S(2)}, u32[]{:S(2)}) collective-permute-start(bf16[128,1024]{1,0:T(8,128)(2,1)S(1)} %pad_maximum_fusion.28), channel_id=1, source_target_pairs={{0,24},{8,0},{16,8},{24,16},{1,25},{9,1},{17,9},{25,17},{2,26},{10... | collective-permute-start | bytes 786440 | tf_op jit(solution)/shard_map/ppermute | solution.py:399
  54.4 98.8 %collective-permute-start.36 = (bf16[3,128,1024]{2,1,0:T(8,128)(2,1)}, bf16[3,128,1024]{2,1,0:T(8,128)(2,1)}, u32[]{:S(2)}, u32[]{:S(2)}) collective-permute-start(bf16[3,128,1024]{2,1,0:T(8,128)(2,1)} %pad_maximum_fusion.9), channel_id=1, source_target_pairs={{0,4},{4,0},{1,5},{5,1},{2,6},{6,2},{3,7},{7,3},{8,12},{12,8},{9,1... | collective-permute-start | bytes 2359304 | tf_op jit(solution)/shard_map/ppermute | solution.py:399
  56.8 26.7 %collective-permute-start.5 = (bf16[128,1024]{1,0:T(8,128)(2,1)S(1)}, bf16[128,1024]{1,0:T(8,128)(2,1)S(1)}, u32[]{:S(2)}, u32[]{:S(2)}) collective-permute-start(bf16[128,1024]{1,0:T(8,128)(2,1)S(1)} %collective-permute-done.4), channel_id=1, source_target_pairs={{0,4},{4,0},{1,5},{5,1},{2,6},{6,2},{3,7},{7,3},{8,12},{12,8},{9,1... | collective-permute-start | bytes 786440 | tf_op jit(solution)/shard_map/ppermute | solution.py:399
  59.9 95.2 %collective-permute-start.37 = (bf16[3,128,1024]{2,1,0:T(8,128)(2,1)}, bf16[3,128,1024]{2,1,0:T(8,128)(2,1)}, u32[]{:S(2)}, u32[]{:S(2)}) collective-permute-start(bf16[3,128,1024]{2,1,0:T(8,128)(2,1)} %pad_maximum_fusion.9), channel_id=1, source_target_pairs={{0,8},{8,16},{16,24},{24,0},{1,9},{9,17},{17,25},{25,1},{2,10},{10... | collective-permute-start | bytes 2359304 | tf_op jit(solution)/shard_map/ppermute | solution.py:399
  67.3 19.0 %collective-permute-start.7 = (bf16[128,1024]{1,0:T(8,128)(2,1)S(1)}, bf16[128,1024]{1,0:T(8,128)(2,1)S(1)}, u32[]{:S(2)}, u32[]{:S(2)}) collective-permute-start(bf16[128,1024]{1,0:T(8,128)(2,1)S(1)} %collective-permute-done.6), channel_id=1, source_target_pairs={{0,4},{4,0},{1,5},{5,1},{2,6},{6,2},{3,7},{7,3},{8,12},{12,8},{9,1... | collective-permute-start | bytes 786440 | tf_op jit(solution)/shard_map/ppermute | solution.py:399
  83.0 25.0 %collective-permute-start.19 = (bf16[2,128,1024]{2,1,0:T(8,128)(2,1)S(1)}, bf16[2,128,1024]{2,1,0:T(8,128)(2,1)S(1)}, u32[]{:S(2)}, u32[]{:S(2)}) collective-permute-start(bf16[2,128,1024]{2,1,0:T(8,128)(2,1)S(1)} %pad_maximum_fusion.14), channel_id=1, source_target_pairs={{0,4},{4,0},{1,5},{5,1},{2,6},{6,2},{3,7},{7,3},{8,12},{12,8},{9,1... | collective-permute-start | bytes 1572872 | tf_op jit(solution)/shard_map/ppermute | solution.py:399
  86.3 97.1 %collective-permute-start.39 = (bf16[3,128,1024]{2,1,0:T(8,128)(2,1)}, bf16[3,128,1024]{2,1,0:T(8,128)(2,1)}, u32[]{:S(2)}, u32[]{:S(2)}) collective-permute-start(bf16[3,128,1024]{2,1,0:T(8,128)(2,1)} %pad_maximum_fusion.9), channel_id=1, source_target_pairs={{0,16},{8,24},{16,0},{24,8},{1,17},{9,25},{17,1},{25,9},{2,18},{10... | collective-permute-start | bytes 2359304 | tf_op jit(solution)/shard_map/ppermute | solution.py:399
  101.2 20.1 %collective-permute-start.20 = (bf16[2,128,1024]{2,1,0:T(8,128)(2,1)S(1)}, bf16[2,128,1024]{2,1,0:T(8,128)(2,1)S(1)}, u32[]{:S(2)}, u32[]{:S(2)}) collective-permute-start(bf16[2,128,1024]{2,1,0:T(8,128)(2,1)S(1)} %pad_maximum_fusion.14), channel_id=1, source_target_pairs={{0,8},{8,16},{16,24},{24,0},{1,9},{9,17},{17,25},{25,1},{2,10},{10... | collective-permute-start | bytes 1572872 | tf_op jit(solution)/shard_map/ppermute | solution.py:399
  133.8 18.9 %collective-permute-start.12 = (bf16[256,256]{1,0:T(8,128)(2,1)S(1)}, bf16[256,256]{1,0:T(8,128)(2,1)S(1)}, u32[]{:S(2)}, u32[]{:S(2)}) collective-permute-start(bf16[256,256]{1,0:T(8,128)(2,1)S(1)} %copy-done.98), channel_id=1, source_target_pairs={{0,2},{2,0},{1,3},{3,1},{4,6},{6,4},{5,7},{7,5},{8,10},{10,8},{9,1... | collective-permute-start | bytes 393224 | tf_op jit(solution)/shard_map/ppermute | solution.py:395
  135.4 40.3 %collective-permute-start.22 = (bf16[2,128,1024]{2,1,0:T(8,128)(2,1)S(1)}, bf16[2,128,1024]{2,1,0:T(8,128)(2,1)S(1)}, u32[]{:S(2)}, u32[]{:S(2)}) collective-permute-start(bf16[2,128,1024]{2,1,0:T(8,128)(2,1)S(1)} %copy-done.68), channel_id=1, source_target_pairs={{0,16},{8,24},{16,0},{24,8},{1,17},{9,25},{17,1},{25,9},{2,18},{10... | collective-permute-start | bytes 1572872 | tf_op jit(solution)/shard_map/ppermute | solution.py:399
  152.7 25.8 %collective-permute-start.24 = (bf16[2,128,1024]{2,1,0:T(8,128)(2,1)S(1)}, bf16[2,128,1024]{2,1,0:T(8,128)(2,1)S(1)}, u32[]{:S(2)}, u32[]{:S(2)}) collective-permute-start(bf16[2,128,1024]{2,1,0:T(8,128)(2,1)S(1)} %copy-done.68), channel_id=1, source_target_pairs={{0,24},{8,0},{16,8},{24,16},{1,25},{9,1},{17,9},{25,17},{2,26},{10... | collective-permute-start | bytes 1572872 | tf_op jit(solution)/shard_map/ppermute | solution.py:399
  153.2 25.8 %collective-permute-start.76 = (bf16[512,256]{0,1:T(8,128)(2,1)S(1)}, bf16[512,256]{0,1:T(8,128)(2,1)S(1)}, u32[]{:S(2)}, u32[]{:S(2)}) collective-permute-start(bf16[512,256]{0,1:T(8,128)(2,1)S(1)} %bitcast.674), channel_id=1, source_target_pairs={{0,2},{2,0},{1,3},{3,1},{4,6},{6,4},{5,7},{7,5},{8,10},{10,8},{9,1... | collective-permute-start | bytes 786440 | tf_op jit(solution)/shard_map/ppermute | solution.py:395
  163.9 30.8 %collective-permute-start.41 = (bf16[3,128,1024]{2,1,0:T(8,128)(2,1)}, bf16[3,128,1024]{2,1,0:T(8,128)(2,1)}, u32[]{:S(2)}, u32[]{:S(2)}) collective-permute-start(bf16[3,128,1024]{2,1,0:T(8,128)(2,1)} %pad_maximum_fusion.9), channel_id=1, source_target_pairs={{0,24},{8,0},{16,8},{24,16},{1,25},{9,1},{17,9},{25,17},{2,26},{10... | collective-permute-start | bytes 2359304 | tf_op jit(solution)/shard_map/ppermute | solution.py:399
  175.7 19.5 %collective-permute-start.21 = (bf16[2,128,1024]{2,1,0:T(8,128)(2,1)S(1)}, bf16[2,128,1024]{2,1,0:T(8,128)(2,1)S(1)}, u32[]{:S(2)}, u32[]{:S(2)}) collective-permute-start(bf16[2,128,1024]{2,1,0:T(8,128)(2,1)S(1)} %copy-done.70), channel_id=1, source_target_pairs={{0,4},{4,0},{1,5},{5,1},{2,6},{6,2},{3,7},{7,3},{8,12},{12,8},{9,1... | collective-permute-start | bytes 1572872 | tf_op jit(solution)/shard_map/ppermute | solution.py:399
  178.5 23.2 %collective-permute-start.23 = (bf16[2,128,1024]{2,1,0:T(8,128)(2,1)S(1)}, bf16[2,128,1024]{2,1,0:T(8,128)(2,1)S(1)}, u32[]{:S(2)}, u32[]{:S(2)}) collective-permute-start(bf16[2,128,1024]{2,1,0:T(8,128)(2,1)S(1)} %collective-permute-done.22), channel_id=1, source_target_pairs={{0,4},{4,0},{1,5},{5,1},{2,6},{6,2},{3,7},{7,3},{8,12},{12,8},{9,1... | collective-permute-start | bytes 1572872 | tf_op jit(solution)/shard_map/ppermute | solution.py:399
  179.0 33.9 %collective-permute-start.25 = (bf16[2,128,1024]{2,1,0:T(8,128)(2,1)S(1)}, bf16[2,128,1024]{2,1,0:T(8,128)(2,1)S(1)}, u32[]{:S(2)}, u32[]{:S(2)}) collective-permute-start(bf16[2,128,1024]{2,1,0:T(8,128)(2,1)S(1)} %collective-permute-done.24), channel_id=1, source_target_pairs={{0,4},{4,0},{1,5},{5,1},{2,6},{6,2},{3,7},{7,3},{8,12},{12,8},{9,1... | collective-permute-start | bytes 1572872 | tf_op jit(solution)/shard_map/ppermute | solution.py:399
  183.4 69.5 %collective-permute-start.38 = (bf16[3,128,1024]{2,1,0:T(8,128)(2,1)}, bf16[3,128,1024]{2,1,0:T(8,128)(2,1)}, u32[]{:S(2)}, u32[]{:S(2)}) collective-permute-start(bf16[3,128,1024]{2,1,0:T(8,128)(2,1)} %collective-permute-done.37), channel_id=1, source_target_pairs={{0,4},{4,0},{1,5},{5,1},{2,6},{6,2},{3,7},{7,3},{8,12},{12,8},{9,1... | collective-permute-start | bytes 2359304 | tf_op jit(solution)/shard_map/ppermute | solution.py:399
  194.7 67.3 %collective-permute-start.40 = (bf16[3,128,1024]{2,1,0:T(8,128)(2,1)}, bf16[3,128,1024]{2,1,0:T(8,128)(2,1)S(1)}, u32[]{:S(2)}, u32[]{:S(2)}) collective-permute-start(bf16[3,128,1024]{2,1,0:T(8,128)(2,1)} %collective-permute-done.39), channel_id=1, source_target_pairs={{0,4},{4,0},{1,5},{5,1},{2,6},{6,2},{3,7},{7,3},{8,12},{12,8},{9,1... | collective-permute-start | bytes 2359304 | tf_op jit(solution)/shard_map/ppermute | solution.py:399
  195.2 72.2 %collective-permute-start.42 = (bf16[3,128,1024]{2,1,0:T(8,128)(2,1)}, bf16[3,128,1024]{2,1,0:T(8,128)(2,1)S(1)}, u32[]{:S(2)}, u32[]{:S(2)}) collective-permute-start(bf16[3,128,1024]{2,1,0:T(8,128)(2,1)} %collective-permute-done.41), channel_id=1, source_target_pairs={{0,4},{4,0},{1,5},{5,1},{2,6},{6,2},{3,7},{7,3},{8,12},{12,8},{9,1... | collective-permute-start | bytes 2359304 | tf_op jit(solution)/shard_map/ppermute | solution.py:399
  201.7 19.5 %collective-permute-start.14 = (bf16[256,1024]{1,0:T(8,128)(2,1)S(1)}, bf16[256,1024]{1,0:T(8,128)(2,1)S(1)}, u32[]{:S(2)}, u32[]{:S(2)}) collective-permute-start(bf16[256,1024]{1,0:T(8,128)(2,1)S(1)} %slice.1007), channel_id=1, source_target_pairs={{0,2},{2,0},{1,3},{3,1},{4,6},{6,4},{5,7},{7,5},{8,10},{10,8},{9,1... | collective-permute-start | bytes 1572872 | tf_op jit(solution)/shard_map/ppermute | solution.py:395
  213.0 57.7 %collective-permute-start.77 = (bf16[512,512]{0,1:T(8,128)(2,1)}, bf16[512,512]{0,1:T(8,128)(2,1)S(1)}, u32[]{:S(2)}, u32[]{:S(2)}) collective-permute-start(bf16[512,512]{0,1:T(8,128)(2,1)} %maximum_select_fusion.6), channel_id=1, source_target_pairs={{0,1},{1,0},{2,3},{3,2},{4,5},{5,4},{6,7},{7,6},{8,9},{9,8},{10,11... | collective-permute-start | bytes 1572872 | tf_op jit(solution)/shard_map/ppermute | solution.py:395
  446.3 37.0 %collective-permute-start.67 = (bf16[256,1024]{1,0:T(8,128)(2,1)S(1)}, bf16[256,1024]{1,0:T(8,128)(2,1)S(1)}, u32[]{:S(2)}, u32[]{:S(2)}) collective-permute-start(bf16[256,1024]{1,0:T(8,128)(2,1)S(1)} %pad_maximum_fusion.20), channel_id=1, source_target_pairs={{0,2},{2,0},{1,3},{3,1},{4,6},{6,4},{5,7},{7,5},{8,10},{10,8},{9,1... | collective-permute-start | bytes 1572872 | tf_op jit(solution)/shard_map/ppermute | solution.py:395
  457.0 28.6 %collective-permute-start.114 = (f32[14464]{0:T(1024)S(1)}, f32[14464]{0:T(1024)S(1)}, u32[]{:S(2)}, u32[]{:S(2)}) collective-permute-start(f32[14464]{0:T(1024)S(1)} %add.906), channel_id=1, source_target_pairs={{0,8},{8,0},{16,24},{24,16},{1,9},{9,1},{17,25},{25,17},{2,10},{10... | collective-permute-start | bytes 173576 | tf_op jit(solution)/shard_map/ppermute | solution.py:764
  526.2 48.8 %collective-permute-start.98 = (bf16[4,2,128,1024]{3,2,1,0:T(8,128)(2,1)}, bf16[4,2,128,1024]{3,2,1,0:T(8,128)(2,1)}, u32[]{:S(2)}, u32[]{:S(2)}) collective-permute-start(bf16[4,2,128,1024]{3,2,1,0:T(8,128)(2,1)} %bitcast.624), channel_id=1, source_target_pairs={{0,4},{4,0},{1,5},{5,1},{2,6},{6,2},{3,7},{7,3},{8,12},{12,8},{9,1... | collective-permute-start | bytes 6291464 | tf_op jit(solution)/shard_map/ppermute | solution.py:520
  532.5 87.5 %collective-permute-start.92 = (bf16[4,2,128,1024]{3,2,0,1:T(8,128)(2,1)}, bf16[4,2,128,1024]{3,2,0,1:T(8,128)(2,1)}, u32[]{:S(2)}, u32[]{:S(2)}) collective-permute-start(bf16[4,2,128,1024]{3,2,0,1:T(8,128)(2,1)} %fusion.7), channel_id=1, source_target_pairs={{0,4},{4,0},{1,5},{5,1},{2,6},{6,2},{3,7},{7,3},{8,12},{12,8},{9,1... | collective-permute-start | bytes 6291464 | tf_op jit(solution)/shard_map/ppermute | solution.py:520
  548.9 31.6 %collective-permute-start.74 = (bf16[256,1024]{1,0:T(8,128)(2,1)}, bf16[256,1024]{1,0:T(8,128)(2,1)}, u32[]{:S(2)}, u32[]{:S(2)}) collective-permute-start(bf16[256,1024]{1,0:T(8,128)(2,1)} %slice.1000), channel_id=1, source_target_pairs={{0,2},{2,0},{1,3},{3,1},{4,6},{6,4},{5,7},{7,5},{8,10},{10,8},{9,1... | collective-permute-start | bytes 1572872 | tf_op jit(solution)/shard_map/ppermute | solution.py:395
  555.5 142.9 %collective-permute-start.78 = (bf16[4,128,1024]{2,1,0:T(8,128)(2,1)}, bf16[4,128,1024]{2,1,0:T(8,128)(2,1)}, u32[]{:S(2)}, u32[]{:S(2)}) collective-permute-start(bf16[4,128,1024]{2,1,0:T(8,128)(2,1)} %fusion.49), channel_id=1, source_target_pairs={{0,4},{4,0},{1,5},{5,1},{2,6},{6,2},{3,7},{7,3},{8,12},{12,8},{9,1... | collective-permute-start | bytes 3145736 | tf_op jit(solution)/shard_map/ppermute | solution.py:520
  583.5 64.6 %collective-permute-start.100 = (bf16[2,128,1024]{2,1,0:T(8,128)(2,1)}, bf16[2,128,1024]{2,1,0:T(8,128)(2,1)}, u32[]{:S(2)}, u32[]{:S(2)}) collective-permute-start(bf16[2,128,1024]{2,1,0:T(8,128)(2,1)} %get-tuple-element.110), channel_id=1, source_target_pairs={{0,16},{8,24},{16,0},{24,8},{1,17},{9,25},{17,1},{25,9},{2,18},{10... | collective-permute-start | bytes 1572872 | tf_op jit(solution)/shard_map/ppermute | solution.py:525
  585.0 66.2 %collective-permute-start.101 = (bf16[2,128,1024]{2,1,0:T(8,128)(2,1)}, bf16[2,128,1024]{2,1,0:T(8,128)(2,1)}, u32[]{:S(2)}, u32[]{:S(2)}) collective-permute-start(bf16[2,128,1024]{2,1,0:T(8,128)(2,1)} %get-tuple-element.109), channel_id=1, source_target_pairs={{0,8},{8,16},{16,24},{24,0},{1,9},{9,17},{17,25},{25,1},{2,10},{10... | collective-permute-start | bytes 1572872 | tf_op jit(solution)/shard_map/ppermute | solution.py:525
  589.2 62.4 %collective-permute-start.99 = (bf16[2,128,1024]{2,1,0:T(8,128)(2,1)}, bf16[2,128,1024]{2,1,0:T(8,128)(2,1)}, u32[]{:S(2)}, u32[]{:S(2)}) collective-permute-start(bf16[2,128,1024]{2,1,0:T(8,128)(2,1)} %get-tuple-element.108), channel_id=1, source_target_pairs={{0,24},{8,0},{16,8},{24,16},{1,25},{9,1},{17,9},{25,17},{2,26},{10... | collective-permute-start | bytes 1572872 | tf_op jit(solution)/shard_map/ppermute | solution.py:525
  647.5 56.4 %collective-permute-start.86 = (bf16[4,128,1024]{2,1,0:T(8,128)(2,1)S(1)}, bf16[4,128,1024]{2,1,0:T(8,128)(2,1)S(1)}, u32[]{:S(2)}, u32[]{:S(2)}) collective-permute-start(bf16[4,128,1024]{2,1,0:T(8,128)(2,1)S(1)} %copy-done.41), channel_id=1, source_target_pairs={{0,4},{4,0},{1,5},{5,1},{2,6},{6,2},{3,7},{7,3},{8,12},{12,8},{9,1... | collective-permute-start | bytes 3145736 | tf_op jit(solution)/shard_map/ppermute | solution.py:520
  651.2 46.1 %collective-permute-start.94 = (bf16[2,128,1024]{2,1,0:T(8,128)(2,1)S(1)}, bf16[2,128,1024]{2,1,0:T(8,128)(2,1)S(1)}, u32[]{:S(2)}, u32[]{:S(2)}) collective-permute-start(bf16[2,128,1024]{2,1,0:T(8,128)(2,1)S(1)} %get-tuple-element.107), channel_id=1, source_target_pairs={{0,16},{8,24},{16,0},{24,8},{1,17},{9,25},{17,1},{25,9},{2,18},{10... | collective-permute-start | bytes 1572872 | tf_op jit(solution)/shard_map/ppermute | solution.py:525
  651.6 46.2 %collective-permute-start.95 = (bf16[2,128,1024]{2,1,0:T(8,128)(2,1)S(1)}, bf16[2,128,1024]{2,1,0:T(8,128)(2,1)S(1)}, u32[]{:S(2)}, u32[]{:S(2)}) collective-permute-start(bf16[2,128,1024]{2,1,0:T(8,128)(2,1)S(1)} %get-tuple-element.106), channel_id=1, source_target_pairs={{0,8},{8,16},{16,24},{24,0},{1,9},{9,17},{17,25},{25,1},{2,10},{10... | collective-permute-start | bytes 1572872 | tf_op jit(solution)/shard_map/ppermute | solution.py:525
  663.5 42.8 %collective-permute-start.110 = (f32[14464]{0:T(1024)S(1)}, f32[14464]{0:T(1024)S(1)}, u32[]{:S(2)}, u32[]{:S(2)}) collective-permute-start(f32[14464]{0:T(1024)S(1)} %add.902), channel_id=1, source_target_pairs={{0,16},{8,24},{16,0},{24,8},{1,17},{9,25},{17,1},{25,9},{2,18},{10... | collective-permute-start | bytes 173576 | tf_op jit(solution)/shard_map/ppermute | solution.py:764
  706.4 20.5 %collective-permute-start.79 = (bf16[128,1024]{1,0:T(8,128)(2,1)}, bf16[128,1024]{1,0:T(8,128)(2,1)}, u32[]{:S(2)}, u32[]{:S(2)}) collective-permute-start(bf16[128,1024]{1,0:T(8,128)(2,1)} %get-tuple-element.115), channel_id=1, source_target_pairs={{0,24},{8,0},{16,8},{24,16},{1,25},{9,1},{17,9},{25,17},{2,26},{10... | collective-permute-start | bytes 786440 | tf_op jit(solution)/shard_map/ppermute | solution.py:525
  708.4 24.0 %collective-permute-start.80 = (bf16[128,1024]{1,0:T(8,128)(2,1)}, bf16[128,1024]{1,0:T(8,128)(2,1)}, u32[]{:S(2)}, u32[]{:S(2)}) collective-permute-start(bf16[128,1024]{1,0:T(8,128)(2,1)} %get-tuple-element.117), channel_id=1, source_target_pairs={{0,16},{8,24},{16,0},{24,8},{1,17},{9,25},{17,1},{25,9},{2,18},{10... | collective-permute-start | bytes 786440 | tf_op jit(solution)/shard_map/ppermute | solution.py:525
  709.9 22.6 %collective-permute-start.81 = (bf16[128,1024]{1,0:T(8,128)(2,1)}, bf16[128,1024]{1,0:T(8,128)(2,1)}, u32[]{:S(2)}, u32[]{:S(2)}) collective-permute-start(bf16[128,1024]{1,0:T(8,128)(2,1)} %get-tuple-element.116), channel_id=1, source_target_pairs={{0,8},{8,16},{16,24},{24,0},{1,9},{9,17},{17,25},{25,1},{2,10},{10... | collective-permute-start | bytes 786440 | tf_op jit(solution)/shard_map/ppermute | solution.py:525
  712.1 21.9 %collective-permute-start.87 = (bf16[128,1024]{1,0:T(8,128)(2,1)}, bf16[128,1024]{1,0:T(8,128)(2,1)}, u32[]{:S(2)}, u32[]{:S(2)}) collective-permute-start(bf16[128,1024]{1,0:T(8,128)(2,1)} %get-tuple-element.118), channel_id=1, source_target_pairs={{0,24},{8,0},{16,8},{24,16},{1,25},{9,1},{17,9},{25,17},{2,26},{10... | collective-permute-start | bytes 786440 | tf_op jit(solution)/shard_map/ppermute | solution.py:525
  725.1 28.8 %collective-permute-start.88 = (bf16[128,1024]{1,0:T(8,128)(2,1)}, bf16[128,1024]{1,0:T(8,128)(2,1)}, u32[]{:S(2)}, u32[]{:S(2)}) collective-permute-start(bf16[128,1024]{1,0:T(8,128)(2,1)} %get-tuple-element.120), channel_id=1, source_target_pairs={{0,16},{8,24},{16,0},{24,8},{1,17},{9,25},{17,1},{25,9},{2,18},{10... | collective-permute-start | bytes 786440 | tf_op jit(solution)/shard_map/ppermute | solution.py:525
  726.9 27.0 %collective-permute-start.89 = (bf16[128,1024]{1,0:T(8,128)(2,1)S(1)}, bf16[128,1024]{1,0:T(8,128)(2,1)S(1)}, u32[]{:S(2)}, u32[]{:S(2)}) collective-permute-start(bf16[128,1024]{1,0:T(8,128)(2,1)S(1)} %copy-done.85), channel_id=1, source_target_pairs={{0,8},{8,16},{16,24},{24,0},{1,9},{9,17},{17,25},{25,1},{2,10},{10... | collective-permute-start | bytes 786440 | tf_op jit(solution)/shard_map/ppermute | solution.py:525
  733.9 22.3 %collective-permute-start.82 = (bf16[64,1024]{1,0:T(8,128)(2,1)S(1)}, bf16[64,1024]{1,0:T(8,128)(2,1)S(1)}, u32[]{:S(2)}, u32[]{:S(2)}) collective-permute-start(bf16[64,1024]{1,0:T(8,128)(2,1)S(1)} %dynamic-slice_convert_fusion.7), channel_id=1, source_target_pairs={{0,2},{2,0},{1,3},{3,1},{4,6},{6,4},{5,7},{7,5},{8,10},{10,8},{9,1... | collective-permute-start | bytes 393224 | tf_op jit(solution)/shard_map/ppermute | solution.py:395
  (253 other events, 1730.8 us)

commit v2 on v0

--- a/solution.py
+++ b/solution.py
@@ -4,7 +4,9 @@
 import jax
 import jax.numpy as jnp
 from jax import lax
-from jax.sharding import PartitionSpec as P
+from jax.experimental import pallas as pl
+from jax.experimental.pallas import tpu as pltpu
+from jax.sharding import Mesh, PartitionSpec as P
 
 H = 16
 HD = 64
@@ -132,7 +134,7 @@
     return (jnp.concatenate(query_grads, axis=0), grad_keys, grad_values)
 
 
-def local(
+def local_any(
     tokens,
     seq_start,
     qkv_weight,
@@ -388,32 +390,550 @@
     )
 
 
+def contract(left, right, left_axis, right_axis):
+    return lax.dot_general(
+        left, right, (((left_axis,), (right_axis,)), ((), ())), preferred_element_type=jnp.float32
+    )
+
+
+def head_parts(project_ref, head):
+    span = project_ref.shape[1] // 3
+    at = head * HD
+    return (project_ref[:, base + at : base + at + HD] for base in (0, span, 2 * span))
+
+
+def head_weights(queries, key_rows, allowed):
+    scores = contract(queries, key_rows, 1, 1) * (1.0 / math.sqrt(HD))
+    scores = jnp.where(allowed, scores, -1e30)
+    exponent = jnp.exp(scores - jnp.max(scores, axis=-1, keepdims=True))
+    return exponent / jnp.sum(exponent, axis=-1, keepdims=True)
+
+
+def allowed_pairs(starts_ref):
+    length = starts_ref.shape[0]
+    row = lax.broadcasted_iota(jnp.int32, (length, length), 0)
+    col = lax.broadcasted_iota(jnp.int32, (length, length), 1)
+    return (col >= starts_ref[...]) & (col <= row)
+
+
+def attention_forward(scale_ref, project_ref, starts_ref, scaled_ref):
+    allowed = allowed_pairs(starts_ref)
+    for pair in range(scaled_ref.shape[1] // (2 * HD)):
+        parts = []
+        for head in (2 * pair, 2 * pair + 1):
+            queries, key_rows, value_rows = head_parts(project_ref, head)
+            weights = head_weights(queries, key_rows, allowed).astype(jnp.bfloat16)
+            attended = contract(weights, value_rows, 1, 0)
+            parts.append((attended * scale_ref[head]).astype(jnp.bfloat16))
+        at = 2 * HD * pair
+        scaled_ref[:, at : at + 2 * HD] = jnp.concatenate(parts, axis=1)
+
+
+def attention_backward(scale_ref, project_ref, starts_ref, grad_ref, out_ref, scale_grad_ref):
+    allowed = allowed_pairs(starts_ref)
+    span = grad_ref.shape[1]
+    score_scale = 1.0 / math.sqrt(HD)
+    for pair in range(span // (2 * HD)):
+        parts = ([], [], [])
+        sums = []
+        for head in (2 * pair, 2 * pair + 1):
+            queries, key_rows, value_rows = head_parts(project_ref, head)
+            upstream = grad_ref[:, head * HD : head * HD + HD]
+            weights = head_weights(queries, key_rows, allowed)
+            weights_low = weights.astype(jnp.bfloat16)
+            attended = contract(weights_low, value_rows, 1, 0)
+            wide = upstream.astype(jnp.float32)
+            sums.append(jnp.sum(wide * attended, axis=0, keepdims=True))
+            grad_attended = (wide * scale_ref[head]).astype(jnp.bfloat16)
+            grad_weights = contract(grad_attended, value_rows, 1, 1)
+            inner = jnp.sum(weights * grad_weights, axis=-1, keepdims=True)
+            grad_scores = (weights * (grad_weights - inner)).astype(jnp.bfloat16)
+            parts[0].append(contract(grad_scores, key_rows, 1, 0) * score_scale)
+            parts[1].append(contract(grad_scores, queries, 0, 0) * score_scale)
+            parts[2].append(contract(weights_low, grad_attended, 0, 0))
+        at = 2 * HD * pair
+        for which in range(3):
+            both = jnp.concatenate(parts[which], axis=1).astype(jnp.bfloat16)
+            out_ref[:, which * span + at : which * span + at + 2 * HD] = both
+        scale_grad_ref[pair : pair + 1, :] = jnp.concatenate(sums, axis=1)
+
+
+def pack_columns(place_ref, qkv_ref, up_ref, own_ref, there_ref):
+    core, near = place_ref[0], place_ref[1]
+    layers, shard, width = qkv_ref.shape
+    span = width // 2
+    blocks = up_ref.shape[2] // 512
+    for layer in range(layers):
+        for at in range(0, width, 256):
+            parts = [qkv_ref[layer, :, at + HD * i : at + HD * (i + 1)] for i in range(4)]
+            even = jnp.concatenate([parts[0], parts[2]], axis=1)
+            odd = jnp.concatenate([parts[1], parts[3]], axis=1)
+
+            @pl.when(core == 0)
+            def _():
+                own_ref[layer, :, at // 2 : at // 2 + 128] = even
+                there_ref[layer, :, at // 2 : at // 2 + 128] = odd
+
+            @pl.when(core == 1)
+            def _():
+                own_ref[layer, :, at // 2 : at // 2 + 128] = odd
+                there_ref[layer, :, at // 2 : at // 2 + 128] = even
+
+        for out_ref, which in ((own_ref, core), (there_ref, 1 - core)):
+            for part, side in enumerate((near, 1 - near)):
+                for block in range(blocks):
+                    at = span + (part * blocks + block) * 128
+                    source = pl.multiple_of(block * 512 + which * 256 + side * 128, 128)
+                    out_ref[layer, :, at : at + 128] = up_ref[layer, :, pl.ds(source, 128)]
+
+
+def pack_rows(place_ref, own_ref, there_ref, out_ref, down_ref, *units):
+    core, near = place_ref[0], place_ref[1]
+    layers, shard, width = out_ref.shape
+    half = width // 2
+    span = own_ref.shape[2] - 2 * width
+    first, second, up, *downs = units
+    attention, ups = (first, second.at[:, : 2 * width]), (up, second.at[:, 2 * width :])
+    for layer in range(layers):
+        for source_ref, which in ((own_ref, core), (there_ref, 1 - core)):
+            rows = pl.ds(pl.multiple_of(which * shard, shard), shard)
+            attention[layer][rows, :span] = source_ref[layer, :, :span]
+            ups[layer][rows, :] = source_ref[layer, :, span : span + width]
+        attention[layer][:shard, span:] = out_ref[layer, :, :half]
+        attention[layer][shard:, span:] = out_ref[layer, :, half:]
+        for part in range(downs[layer].shape[1] // width):
+            side = near if part == 0 else 1 - near
+            rows = pl.ds(pl.multiple_of(side * 2 * shard, 2 * shard), 2 * shard)
+            downs[layer][:, part * width : part * width + width] = down_ref[layer, rows, :]
+
+
+def term_product(arrays, parts, shape):
+    def body(left_ref, left_there_ref, right_ref, right_there_ref, out_ref):
+        for left_at, right_at, columns, out_at in parts:
+            right = right_ref[:, right_at : right_at + columns]
+            right_there = right_there_ref[:, right_at : right_at + columns]
+            for row in range(0, shape[0], 256):
+                left = left_ref[:, left_at + row : left_at + row + 256]
+                left_there = left_there_ref[:, left_at + row : left_at + row + 256]
+                total = contract(left, right, 0, 0) + contract(left_there, right_there, 0, 0)
+                out_ref[row : row + 256, out_at : out_at + columns] = total.astype(jnp.bfloat16)
+
+    vmem = pl.BlockSpec(memory_space=pltpu.VMEM)
+    return pl.pallas_call(
+        body,
+        out_shape=jax.ShapeDtypeStruct(shape, jnp.bfloat16),
+        in_specs=[vmem] * 4,
+        out_specs=vmem,
+    )(*arrays)
+
+
+def run_small(body, scale, arrays, outs):
+    vmem = pl.BlockSpec(memory_space=pltpu.VMEM)
+    return pl.pallas_call(
+        body,
+        out_shape=[jax.ShapeDtypeStruct(*out) for out in outs],
+        in_specs=[pl.BlockSpec(memory_space=pltpu.SMEM)] + [vmem] * len(arrays),
+        out_specs=[vmem] * len(outs),
+    )(scale, *arrays)
+
+
+SWAP = ((0, 1), (1, 0))
+
+
+def swap(array, axis):
+    return lax.ppermute(array, axis, SWAP)
+
+
+def turn(array):
+    return lax.ppermute(array, ("c", "y"), ((0, 0), (1, 2), (2, 1), (3, 3)))
+
+
+def norm_parts(values):
+    center = values - jnp.mean(values, axis=-1, keepdims=True)
+    inverse = lax.rsqrt(jnp.mean(center * center, axis=-1, keepdims=True) + norm_eps)
+    return center * inverse, inverse
+
+
+def local_chip(
+    tokens,
+    seq_start,
+    qkv_weight,
+    out_weight,
+    fc1_weight,
+    fc2_weight,
+    norm_gain,
+    norm_bias,
+    mid_gain,
+    mid_bias,
+    head_scale,
+    cotangent,
+):
+    nz, nx = lax.axis_size("z"), lax.axis_size("x")
+    iz, ix, ic, iy = (lax.axis_index(name) for name in ("z", "x", "c", "y"))
+    chips = nz * nx
+    rows, width = tokens.shape
+    group_rows = seq_start.shape[0]
+    hidden_width = fc1_weight.shape[2]
+    shard = qkv_weight.shape[1]
+    block = hidden_width // (4 * chips)
+    heads_here = H // 2
+    head_width = width // 2
+    units = hidden_width // 2
+    half_units = units // 2
+    half = width // 2
+    wide = 3 * head_width // 2
+    f32, bf16 = jnp.float32, jnp.bfloat16
+
+    def pick(array, which, axis):
+        return lax.dynamic_index_in_dim(array, which, axis, keepdims=False)
+
+    def cores(own, other, axis=0):
+        first = jnp.where(ic == 0, own, other)
+        second = jnp.where(ic == 0, other, own)
+        return jnp.concatenate([first, second], axis=axis)
+
+    def both_cores(partial_sum):
+        low = lax.optimization_barrier(partial_sum.astype(bf16))
+        return low.astype(f32) + swap(low, "c").astype(f32)
+
+    def ordered(first, second, axis):
+        near = jnp.where(iy == 0, first, second)
+        far = jnp.where(iy == 0, second, first)
+        return jnp.concatenate([near, far], axis=axis)
+
+    def gather(array):
+        return lax.all_gather(array, ("z", "x"), axis=0, tiled=True)
+
+    def scatter(array):
+        return lax.psum_scatter(
+            array.astype(bf16), ("z", "x"), scatter_dimension=0, tiled=True
+        ).astype(f32)
+
+    def step_x(array):
+        split = array.reshape(nz, nx, -1, array.shape[1])
+        there = swap(pick(split, 1 - ix, 1).astype(bf16), "x")
+        return pick(split, ix, 1).astype(f32) + there.astype(f32)
+
+    def step_z(array):
+        total = pick(array, iz, 0)
+        for step in range(1, nz):
+            there = pick(array, (iz + step) % nz, 0).astype(bf16)
+            ring = [(i, (i + step) % nz) for i in range(nz)]
+            total = total + lax.ppermute(there, "z", ring).astype(f32)
+        return total
+
+    def steps(array):
+        return step_z(step_x(array))
+
+    def tie(value, *others):
+        return lax.optimization_barrier((value,) + others)
+
+    def z_pieces(array):
+        return [array] + [
+            lax.ppermute(array, "z", [(i, (i + step) % nz) for i in range(nz)])
+            for step in range(1, nz)
+        ]
+
+    def join(pieces):
+        held = jnp.zeros((nz, nx) + pieces[0].shape, pieces[0].dtype)
+        for step, piece in enumerate(pieces):
+            for at_x, part in ((ix, piece), (1 - ix, swap(piece, "x"))):
+                at = ((iz - step) % nz, at_x, 0, 0)
+                held = lax.dynamic_update_slice(held, part[None, None], at)
+        return held.reshape(-1, pieces[0].shape[1])
+
+    place = jnp.stack([ic, iy]).astype(jnp.int32)
+    narrow = (LAYERS, shard, 3 * head_width + units)
+    own, there = run_small(
+        pack_columns, place, (qkv_weight, fc1_weight), [(narrow, bf16), (narrow, bf16)]
+    )
+    wides = (4 * head_width, 4 * head_width + width, width, width, 2 * width)
+    packed = run_small(
+        pack_rows,
+        place,
+        (own, swap(there, "c"), out_weight, fc2_weight),
+        [((2 * shard, columns), bf16) for columns in wides],
+    )
+    got = []
+    for unit in (packed[0], packed[2], packed[3]):
+        if got:
+            unit, got[-1][1] = tie(unit, got[-1][1])
+        got.append(z_pieces(unit))
+    late = packed[1]
+    late, *got[0] = tie(late, *got[0])
+    late = gather(late)
+    got = [join(pieces) for pieces in got]
+    last_down = gather(packed[4])
+    last_up = late[:, 4 * head_width :]
+    ups = [(got[1], swap(got[1], "y")), (last_up, swap(last_up, "y"))]
+    downs = [(got[2], swap(got[2], "y")), (last_down[:, :width], last_down[:, width:])]
+    attention_mats = [got[0], late]
+
+    def matrices(which):
+        packed = attention_mats[which]
+        qkv = packed[:, : 3 * head_width]
+        out = packed[:, 3 * head_width : 4 * head_width].reshape(chips, 2, shard, half)
+        out = jnp.concatenate(
+            [out[:, 0].reshape(head_width, half), out[:, 1].reshape(head_width, half)], axis=1
+        )
+        return qkv, out, ups[which], downs[which]
+
+    def mine_of(vector):
+        mine = pick(vector.reshape(chips, 2, 2, block), ic, 1)
+        return ordered(mine[:, 0].reshape(-1), mine[:, 1].reshape(-1), 0)
+
+    def slice_of(values, first, size):
+        return lax.dynamic_slice_in_dim(values, first, size, 1)
+
+    turned = turn(tokens)
+    hidden = cores(turned, swap(turned, "c")).astype(f32)
+    starts = jnp.where(ic == iy, seq_start, swap(seq_start, "c"))
+    starts = starts[:, None]
+
+    cotangent_late, attention_mats[0] = tie(cotangent, attention_mats[0])
+    mats = [matrices(which) for which in range(LAYERS)]
+    kept = []
+    for which in range(LAYERS):
+        qkv_mat, out_mat, up_mat, down_mat = mats[which]
+        scale_here = pick(head_scale[which].reshape(heads_here, 2), ic, 1)
+        if which == 1:
+            hidden, far_up = tie(hidden, up_mat[1])
+            up_mat = (up_mat[0], far_up)
+            mats[1] = (qkv_mat, out_mat, up_mat, down_mat)
+        norm_a, inv_a = norm_parts(hidden)
+        a_low = (norm_a * norm_gain[which, 0] + norm_bias[which, 0]).astype(bf16)
+        project = product(a_low, qkv_mat).astype(bf16)
+        (scaled,) = run_small(
+            attention_forward, scale_here, (project, starts), [((group_rows, head_width), bf16)]
+        )
+        branch = both_cores(product(scaled, out_mat))
+        if which == 0:
+            branch, far_up, far_down = tie(branch, up_mat[1], down_mat[1])
+            up_mat, down_mat = (up_mat[0], far_up), (down_mat[0], far_down)
+            mats[0] = (qkv_mat, out_mat, up_mat, down_mat)
+        norm_z, inv_z = norm_parts(branch)
+        middle = hidden + norm_z * norm_gain[which, 1] + norm_bias[which, 1]
+        norm_b, inv_b = norm_parts(middle)
+        b_low = (norm_b * norm_gain[which, 2] + norm_bias[which, 2]).astype(bf16)
+        pre_act = jnp.concatenate([product(b_low, part) for part in up_mat], axis=1)
+        below = 0.5 * (1.0 + lax.erf(pre_act * (1.0 / math.sqrt(2.0))))
+        activated = pre_act * below
+        mean_here = jnp.mean(activated, axis=-1)
+        center = activated - mean_here[:, None]
+        stats = jnp.stack([mean_here, jnp.mean(center * center, axis=-1)])
+        stats_there = swap(stats, "c")
+        mean_all = 0.5 * (stats[0] + stats_there[0])
+        apart = 0.5 * (stats[0] - stats_there[0])
+        spread = 0.5 * (stats[1] + stats_there[1]) + apart * apart
+        inv_m = lax.rsqrt(spread + norm_eps)[:, None]
+        norm_m = (activated - mean_all[:, None]) * inv_m
+        gain_m, bias_m = mine_of(mid_gain[which]), mine_of(mid_bias[which])
+        mixed_low = (norm_m * gain_m + bias_m).astype(bf16)
+        if which == 1:
+            last = kept[0]
+            mixed_low, there_a, there_h = tie(mixed_low, last[-3], last[-1])
+            kept[0] = last[:-3] + (there_a, last[-2], there_h)
+        near, far = mixed_low[:, :half_units], mixed_low[:, half_units:]
+        hidden = middle + both_cores(product(near, down_mat[0]) + product(far, down_mat[1]))
+        attention_in = jnp.concatenate([a_low, scaled], axis=1)
+        hidden_in = jnp.concatenate([b_low, mixed_low], axis=1)
+        hidden_there = swap(jnp.concatenate([b_low, far, near], axis=1), "y")
+        attention_there = swap(attention_in, "y")
+        kept.append(
+            (
+                norm_a, inv_a, project, scale_here, norm_z, inv_z, norm_b, inv_b, pre_act, below, norm_m, inv_m, gain_m,
+                attention_in, attention_there, hidden_in, hidden_there,
+            )
+        )
+    output = lax.dynamic_slice_in_dim(hidden.astype(bf16), ic * rows, rows, 0)
+    turned = turn(cotangent_late)
+    grad_hidden = cores(turned, swap(turned, "c")).astype(f32)
+
+    def natural(values):
+        return ordered(values[:half_units], values[half_units:], 0)
+
+    vectors, pending = [None] * LAYERS, [None] * LAYERS
+    for which in reversed(range(LAYERS)):
+        qkv_mat, out_mat, up_mat, down_mat = mats[which]
+        (
+            norm_a, inv_a, project, scale_here, norm_z, inv_z, norm_b, inv_b, pre_act, below, norm_m, inv_m, gain_m,
+            attention_in, attention_there, hidden_in, hidden_there,
+        ) = kept[which]
+        final_low = grad_hidden.astype(bf16)
+        grad_mixed = jnp.concatenate([product(final_low, part.T) for part in down_mat], axis=1)
+        mid_gain_grad = jnp.sum(grad_mixed * norm_m, axis=0)
+        mid_bias_grad = jnp.sum(grad_mixed, axis=0)
+        scaled_grad = grad_mixed * gain_m
+        sums = jnp.stack([jnp.sum(scaled_grad, axis=-1), jnp.sum(scaled_grad * norm_m, axis=-1)])
+        sums = (sums + swap(sums, "c")) / hidden_width
+        grad_act = inv_m * (scaled_grad - sums[0][:, None] - norm_m * sums[1][:, None])
+        slope = below + pre_act * jnp.exp(-0.5 * pre_act * pre_act) * (1.0 / math.sqrt(2 * math.pi))
+        grad_pre = (grad_act * slope).astype(bf16)
+        if which == 0:
+            grad_pre, at_there = tie(grad_pre, at_there)
+            later = finish_attention(at_there)
+        near, far = grad_pre[:, :half_units], grad_pre[:, half_units:]
+
+        def unit_columns(side):
+            first = side * (half_units // 2)
+            return (
+                slice_of(near, first, half_units // 2),
+                slice_of(far, first, half_units // 2),
+                slice_of(final_low, side * half, half),
+            )
+
+        keep_n, keep_f, keep_c = unit_columns(iy)
+        send_n, send_f, send_c = unit_columns(1 - iy)
+        ff_there = swap(jnp.concatenate([send_f, send_n, send_c], axis=1), "y")
+        ff_out = jnp.concatenate([keep_n, keep_f, keep_c], axis=1)
+        grad_ff_in = both_cores(product(near, up_mat[0].T) + product(far, up_mat[1].T))
+        grad_mid_in, gain_two, bias_two = norm_backward(
+            grad_ff_in, norm_b, inv_b, norm_gain[which, 2]
+        )
+        grad_middle = grad_hidden + grad_mid_in
+        grad_branch, gain_one, bias_one = norm_backward(
+            grad_middle, norm_z, inv_z, norm_gain[which, 1]
+        )
+        branch_low = grad_branch.astype(bf16)
+        if which == 0:
+            branch_low, later = tie(branch_low, later)
+            later = step_x(later)
+        grad_heads = product(branch_low, out_mat.T).astype(bf16)
+        grad_project, scale_grad = run_small(
+            attention_backward,
+            scale_here,
+            (project, starts, grad_heads),
+            [((group_rows, 3 * head_width), bf16), ((heads_here // 2, 2 * HD), f32)],
+        )
+        scale_grad = jnp.sum(scale_grad.reshape(heads_here, HD), axis=1)
+        grad_normed = both_cores(product(grad_project, qkv_mat.T))
+        grad_input, gain_zero, bias_zero = norm_backward(
+            grad_normed, norm_a, inv_a, norm_gain[which, 0]
+        )
+
+        at_out = jnp.concatenate(
+            [slice_of(grad_project, iy * wide, wide), slice_of(branch_low, iy * half, half)], axis=1
+        )
+        at_there = jnp.concatenate(
+            [
+                slice_of(grad_project, (1 - iy) * wide, wide),
+                slice_of(branch_low, (1 - iy) * half, half),
+            ],
+            axis=1,
+        )
+        at_there = swap(at_there, "y")
+        if which == 1:
+            grad_input, ff_there, hidden_there, attention_there = tie(
+                grad_input, ff_there, hidden_there, attention_there
+            )
+        ff_term = term_product(
+            (hidden_in, hidden_there, ff_out, ff_there),
+            ((0, 0, width, 0), (width, width, half, width), (2 * width, width, half, width + half)),
+            (width, 2 * width),
+        )
+        grad_hidden = grad_middle + grad_input
+        if which == 1:
+            grad_hidden, ff_term = tie(grad_hidden, ff_term)
+            ff_rows = scatter(ff_term)
+        else:
+            ff_rows = jnp.concatenate(
+                [steps(ff_term[:, :width]), steps(ff_term[:, width:])], axis=1
+            )
+
+        def attention_term(there, here=at_out, ins=attention_in, ins_there=attention_there):
+            split = half // 2
+            out_term = term_product(
+                (ins[:, width:], ins_there[:, width:], here[:, wide:], there[:, wide:]),
+                ((0, 0, half, 0),),
+                (head_width, half),
+            ).reshape(chips, shard, half)
+            out_term = jnp.concatenate([out_term[..., :split], out_term[..., split:]], axis=1)
+            qkv_term = term_product((ins, ins_there, here, there), ((0, 0, wide, 0),), (width, wide))
+            return jnp.concatenate([qkv_term, out_term.reshape(-1, split)], axis=1)
+
+        if which == 1:
+            finish_attention = attention_term
+        else:
+            grad_hidden, later = tie(grad_hidden, later)
+            at_rows_last = step_z(later)
+            at_rows = step_x(attention_term(at_there))
+        pending[which] = ff_rows
+        shared = jnp.concatenate([gain_zero, gain_one, gain_two, bias_zero, bias_one, bias_two])
+        vectors[which] = jnp.concatenate(
+            [0.5 * shared, natural(mid_gain_grad), natural(mid_bias_grad), jnp.pad(scale_grad, (0, 128 - heads_here))]
+        )
+
+    vector = jnp.stack(vectors)
+    vector = vector + swap(vector, "y")
+    vector, at_rows, output = tie(vector, at_rows, output)
+    at_rows = step_z(at_rows)
+    vector = vector + swap(vector, "x")
+    matrix_grads = []
+    for at_rows, ff_rows in ((at_rows, pending[0]), (at_rows_last, pending[1])):
+        grad_out = at_rows[:, wide:].reshape(2, shard, half // 2)
+        grad_out = jnp.concatenate([grad_out[0], grad_out[1]], axis=1)
+        down_near, down_far = ff_rows[:, width : width + half], ff_rows[:, width + half :]
+        grad_down = jnp.concatenate(
+            [jnp.where(iy == 0, down_near, down_far), jnp.where(iy == 0, down_far, down_near)], axis=0
+        )
+        mixed_rows = jnp.concatenate([at_rows[:, :wide], ff_rows[:, :width]], axis=1)
+        mixed_rows = mixed_rows.reshape(2, shard, -1)
+        own = pick(mixed_rows, ic, 0)
+        other = swap(pick(mixed_rows, 1 - ic, 0).astype(bf16), "c").astype(f32)
+        columns = cores(own[None], other[None])
+        grad_qkv = columns[:, :, :wide].reshape(2, shard, wide // HD, HD)
+        grad_qkv = grad_qkv.transpose(1, 2, 0, 3).reshape(shard, 2 * wide)
+        near, far = columns[:, :, wide : wide + half], columns[:, :, wide + half :]
+        grad_up = jnp.stack(
+            [jnp.where(iy == 0, near, far), jnp.where(iy == 0, far, near)], axis=2
+        ).reshape(2, shard, 2, chips // 2, block)
+        grad_up = grad_up.transpose(1, 3, 0, 2, 4).reshape(shard, 2 * width)
+        matrix_grads.append((grad_qkv, grad_out, grad_up, grad_down))
+
+    grad_tokens = turn(lax.dynamic_slice_in_dim(grad_hidden, ic * rows, rows, 0))
+    output = turn(output)
+    for bit in (1, 2):
+        vector = vector + lax.ppermute(vector, "z", [(i, i ^ bit) for i in range(nz)])
+    there = swap(vector, "c")
+    shared = vector[:, : 6 * width] + there[:, : 6 * width]
+
+    def spread_units(first):
+        view = (LAYERS, 2, chips, 1, block)
+        own, other = (part[:, first : first + units] for part in (vector, there))
+        own, other = own.reshape(view), other.reshape(view)
+        return cores(own, other, 3).transpose(0, 2, 3, 1, 4).reshape(LAYERS, hidden_width)
+
+    scale_at = 6 * width + 2 * units
+    own, other = (
+        part[:, scale_at : scale_at + heads_here].reshape(LAYERS, heads_here, 1)
+        for part in (vector, there)
+    )
+    summed = [jnp.stack([grads[which] for grads in matrix_grads]) for which in range(4)]
+    return (
+        output,
+        grad_tokens,
+        summed[0],
+        summed[1],
+        summed[2],
+        summed[3],
+        shared[:, : 3 * width].reshape(LAYERS, 3, width),
+        shared[:, 3 * width :].reshape(LAYERS, 3, width),
+        spread_units(6 * width),
+        spread_units(6 * width + units),
+        cores(own, other, 2).reshape(LAYERS, H),
+    )
+
+
 def solution(mesh):
-    in_specs = (
-        P(("dp", "sp"), None),
-        P("dp"),
-        P(None, "dp", None),
-        P(None, "dp", None),
-        P(None, "dp", None),
-        P(None, "dp", None),
-        P(),
-        P(),
-        P(),
-        P(),
-        P(),
-        P(("dp", "sp"), None),
-    )
-    out_specs = (
-        P(("dp", "sp"), None),
-        P(("dp", "sp"), None),
-        P(None, "dp", "sp"),
-        P(None, "dp", "sp"),
-        P(None, "dp", "sp"),
-        P(None, "dp", "sp"),
-        P(),
-        P(),
-        P(),
-        P(),
-        P(),
-    )
-    return jax.shard_map(local, mesh=mesh, in_specs=in_specs, out_specs=out_specs, check_vma=False)
+    dp, sp = mesh.shape["dp"], mesh.shape["sp"]
+    if sp == 2 and dp == 16:
+        mesh = Mesh(mesh.devices.reshape(4, dp // 8, 2, 2), ("z", "x", "c", "y"))
+        rows, every, cols, body = ("z", "x", "c"), ("z", "x", "c", "y"), "y", local_chip
+    else:
+        rows, every, cols, body = "dp", ("dp", "sp"), "sp", local_any
+    weight = P(None, rows, None)
+    in_specs = (P(every, None), P(rows), weight, weight, weight, weight)
+    in_specs = in_specs + (P(),) * 5 + (P(every, None),)
+    grad = P(None, rows, cols)
+    out_specs = (P(every, None), P(every, None), grad, grad, grad, grad) + (P(),) * 5
+    return jax.shard_map(body, mesh=mesh, in_specs=in_specs, out_specs=out_specs, check_vma=False)

time: 1400 us -> 707 us (0.51)
  waiting for transfers between devices: 969 us -> 275 us
  blocking collectives: 120 us -> 0 us
  starting transfers between devices: 46.2 us -> 154 us
  matrix products: 129 us -> 50 us
  Pallas kernels: 0 us -> 59.2 us
  other arithmetic: 39.1 us -> 84.5 us
    reduce_scatter x8 -> x1, waiting for transfers between devices: 543 us -> 0.01 us  [scatter(): lax.psum_scatter(array.astype(bf16), ('z', 'x'), scatter_dimension=0, til...]
    all_gather x10 -> x2, waiting for transfers between devices: 390 us -> 0.02 us  [gather(): return lax.all_gather(array, ('z', 'x'), axis=0, tiled=True)]
    ppermute x0 -> x75, waiting for transfers between devices: none -> 275 us  [the longest x48 157 us: swap(): return lax.ppermute(array, axis, SWAP)]
    ppermute x0 -> x75, starting transfers between devices: none -> 153 us  [the longest x48 80.4 us: swap(): return lax.ppermute(array, axis, SWAP)]
    all_gather x6 -> x0, blocking collectives: 81 us -> none  [the longest x2 33.8 us: local(): lax.all_gather(gathered, 'sp', axis=0, tiled=True)]
    pallas_call x0 -> x12, Pallas kernels: none -> 59.2 us  [the longest x6 32.2 us: run_small(): pl.pallas_call(body, out_shape=[jax.ShapeDtypeStruct(*out) for out in out...]
    dot_general x24, matrix products: 106 us -> 50 us  [product(): return jnp.dot(left, right, preferred_element_type=jnp.float32)]
    all_to_all x12 -> x0, starting transfers between devices: 45.4 us -> none  [the longest x2 8.13 us: local(): lax.all_to_all(stacked, 'sp', split_axis=0, concat_axis=2, tiled=True)]
  transfers between devices with their start and end apart: 31 -> 78, of which waited for: 20 -> 24; matrix products, arithmetic and copies ran while one was open for 14% -> 26% of each run, Pallas kernels for 0% -> 8%
where the time goes in v2:
time: 707 us; the launch traced here: 704 us
  waiting for transfers between devices  275 us (39%)
  starting transfers between devices  154 us (22%)
  other arithmetic  84.5 us (12%)
  local copies, waits for them, and re-layouts  64.6 us (9%)
  Pallas kernels  59.2 us (8%)
  matrix products  50 us (7%)
  between operations  16.4 us (2%)
    ppermute x48, waiting for transfers between devices, swap(): return lax.ppermute(array, axis, SWAP)  157 us
    ppermute x48, starting transfers between devices, swap(): return lax.ppermute(array, axis, SWAP)  80.4 us
    ppermute x9, waiting for transfers between devices, z_pieces(): lax.ppermute(array, 'z', [(i, (i + step) % nz) for i in range(nz)])  73.1 us
    dot_general x24, matrix products, product(): return jnp.dot(left, right, preferred_element_type=jnp.float32)  50 us
    ppermute x9, starting transfers between devices, z_pieces(): lax.ppermute(array, 'z', [(i, (i + step) % nz) for i in range(nz)])  36.4 us
    pallas_call x6, Pallas kernels, run_small(): pl.pallas_call(body, out_shape=[jax.ShapeDtypeStruct(*out) for out in out...  32.2 us
    ppermute x12, waiting for transfers between devices, step_z(): total = total + lax.ppermute(there, 'z', ring).astype(f32)  29.2 us
    pallas_call x6, Pallas kernels, term_product(): pl.pallas_call(body, out_shape=jax.ShapeDtypeStruct(shape, jnp.bfloat16),...  27 us
  transfers between devices with their start and end apart: 78, of which 24 were waited for; matrix products, arithmetic and copies ran while one was open for 26% of the time, Pallas kernels for 8%

profile of v2, /device:TPU:0, one launch (start us, length us, event | category | flops | bytes accessed | tf_op | source)
XLA Modules:
  0.0 703.6 jit_solution(14868862787569521021)
XLA Ops:
  9.4 4.8 shard_map.203
  14.2 3.5 collective-permute-start.2
  21.0 3.4 shard_map.204
  29.9 11.5 %collective-permute-done.3 = bf16[128,2048]{1,0:T(8,128)(2,1)} collective-permute-done((bf16[128,2048]{1,0:T(8,128)(2,1)}, bf16[128,2048]{1,0:T(8,128)(2,1)}, u32[]{:S(2)}, u32[]{:S(2)}) %collective-permute-start.3) | collective-permute-done | bytes 524320 | tf_op jit(solution)/shard_map/ppermute | solution.py:633
  41.4 21.9 %collective-permute-done.4 = bf16[128,2048]{1,0:T(8,128)(2,1)} collective-permute-done((bf16[128,2048]{1,0:T(8,128)(2,1)}, bf16[128,2048]{1,0:T(8,128)(2,1)}, u32[]{:S(2)}, u32[]{:S(2)}) %collective-permute-start.4) | collective-permute-done | bytes 524320 | tf_op jit(solution)/shard_map/ppermute | solution.py:633
  67.9 11.7 %collective-permute-start.13 = (bf16[128,1024]{1,0:T(8,128)(2,1)S(1)}, bf16[128,1024]{1,0:T(8,128)(2,1)S(1)}, u32[]{:S(2)}, u32[]{:S(2)}) collective-permute-start(bf16[128,1024]{1,0:T(8,128)(2,1)S(1)} %copy-done.63), channel_id=1, source_target_pairs={{0,8},{8,16},{16,24},{24,0},{1,9},{9,17},{17,25},{25,1},{2,10},{10... | collective-permute-start | bytes 786440 | tf_op jit(solution)/shard_map/ppermute | solution.py:633
  86.5 4.1 collective-permute-done.13
  94.4 16.3 %collective-permute-done.15 = bf16[128,1024]{1,0:T(8,128)(2,1)S(1)} collective-permute-done((bf16[128,1024]{1,0:T(8,128)(2,1)S(1)}, bf16[128,1024]{1,0:T(8,128)(2,1)S(1)}, u32[]{:S(2)}, u32[]{:S(2)}) %collective-permute-start.15) | collective-permute-done | bytes 262176 | tf_op jit(solution)/shard_map/ppermute | solution.py:633
  111.2 9.7 %collective-permute-done.14 = bf16[128,1024]{1,0:T(8,128)(2,1)S(1)} collective-permute-done((bf16[128,1024]{1,0:T(8,128)(2,1)S(1)}, bf16[128,1024]{1,0:T(8,128)(2,1)S(1)}, u32[]{:S(2)}, u32[]{:S(2)}) %collective-permute-start.14) | collective-permute-done | bytes 262176 | tf_op jit(solution)/shard_map/ppermute | solution.py:544
  124.3 16.6 %collective-permute-done.16 = bf16[128,1024]{1,0:T(8,128)(2,1)S(1)} collective-permute-done((bf16[128,1024]{1,0:T(8,128)(2,1)S(1)}, bf16[128,1024]{1,0:T(8,128)(2,1)S(1)}, u32[]{:S(2)}, u32[]{:S(2)}) %collective-permute-start.16) | collective-permute-done | bytes 262176 | tf_op jit(solution)/shard_map/ppermute | solution.py:544
  142.7 20.2 %collective-permute-done.18 = bf16[128,1024]{1,0:T(8,128)(2,1)S(1)} collective-permute-done((bf16[128,1024]{1,0:T(8,128)(2,1)S(1)}, bf16[128,1024]{1,0:T(8,128)(2,1)S(1)}, u32[]{:S(2)}, u32[]{:S(2)}) %collective-permute-start.18) | collective-permute-done | bytes 262176 | tf_op jit(solution)/shard_map/ppermute | solution.py:544
  162.9 8.7 %collective-permute-start.21 = (bf16[128,1024]{1,0:T(8,128)(2,1)S(1)}, bf16[128,1024]{1,0:T(8,128)(2,1)S(1)}, u32[]{:S(2)}, u32[]{:S(2)}) collective-permute-start(bf16[128,1024]{1,0:T(8,128)(2,1)S(1)} %copy-done.62), channel_id=1, source_target_pairs={{0,8},{8,16},{16,24},{24,0},{1,9},{9,17},{17,25},{25,1},{2,10},{10... | collective-permute-start | bytes 786440 | tf_op jit(solution)/shard_map/ppermute | solution.py:633
  173.0 11.6 %collective-permute-done.21 = bf16[128,1024]{1,0:T(8,128)(2,1)S(1)} collective-permute-done((bf16[128,1024]{1,0:T(8,128)(2,1)S(1)}, bf16[128,1024]{1,0:T(8,128)(2,1)S(1)}, u32[]{:S(2)}, u32[]{:S(2)}) %collective-permute-start.21) | collective-permute-done | bytes 262176 | tf_op jit(solution)/shard_map/ppermute | solution.py:633
  184.6 6.1 collective-permute-start.23
  195.1 4.4 collective-permute-done.23
  199.6 3.4 collective-permute-done.25
  206.2 3.1 collective-permute-done.24
  209.4 2.7 collective-permute-done.26
  217.1 4.8 shard_map.205.left_ref
  226.7 45.1 %collective-permute-start.29 = (bf16[128,1024]{1,0:T(8,128)(2,1)S(1)}, bf16[128,1024]{1,0:T(8,128)(2,1)}, u32[]{:S(2)}, u32[]{:S(2)}) collective-permute-start(bf16[128,1024]{1,0:T(8,128)(2,1)S(1)} %collective-permute-done.28), channel_id=1, source_target_pairs={{0,2},{2,0},{1,3},{3,1},{4,6},{6,4},{5,7},{7,5},{8,10},{10,8},{9,1... | collective-permute-start | bytes 786440 | tf_op jit(solution)/shard_map/ppermute | solution.py:544
  281.9 2.7 fusion.173
  299.6 40.0 %collective-permute-done.32 = bf16[1024,1024]{1,0:T(8,128)(2,1)} collective-permute-done((bf16[1024,1024]{1,0:T(8,128)(2,1)S(1)}, bf16[1024,1024]{1,0:T(8,128)(2,1)}, u32[]{:S(2)}, u32[]{:S(2)}) %collective-permute-start.32) | collective-permute-done | bytes 2097184 | tf_op jit(solution)/shard_map/ppermute | solution.py:544
  341.0 3.8 fusion.11.project_ref
  344.8 4.8 shard_map.206.left_ref
  362.0 12.8 %multiply_reduce_fusion.18 = f32[256]{0:T(256)S(1)} fusion(f32[256,1024]{1,0:T(8,128)S(1)} %get-tuple-element.144, f32[256]{0:T(256)S(1)} %broadcast_multiply_fusion.16), kind=kLoop, calls=%fused_computation.138 | loop fusion | flops 786176 | bytes 1050624 | tf_op jit(solution)/shard_map/reduce_sum | solution.py:553
  407.2 7.3 %shard_map.207 = (bf16[256,1536]{1,0:T(8,128)(2,1)}, f32[4,128]{1,0:T(4,128)}) custom-call(f32[8]{0:T(128)} %fusion.123.scale_ref, bf16[256,1536]{1,0:T(8,128)(2,1)} %fusion.11.project_ref, s32[256,1]{1,0:T(8,128)} %copy.57.starts_ref, bf16[256,512]{1,0:T(8,128)(2,1)} %convolution_convert_fusion.3.grad_ref), custom_call_target="tpu_custom_call" | custom-call | tf_op jit(solution)/shard_map/pallas_call | solution.py:532
  414.5 4.1 fusion.44
  429.0 23.0 %collective-permute-done.38.right_there_ref = bf16[256,1536]{1,0:T(8,128)(2,1)} collective-permute-done((bf16[256,1536]{1,0:T(8,128)(2,1)}, bf16[256,1536]{1,0:T(8,128)(2,1)}, u32[]{:S(2)}, u32[]{:S(2)}) %collective-permute-start.38) | collective-permute-done | bytes 786464 | tf_op jit(solution)/shard_map/ppermute | solution.py:544
  452.2 7.1 %shard_map.208 = bf16[1024,2048]{1,0:T(8,128)(2,1)} custom-call(bf16[256,3072]{1,0:T(8,128)(2,1)} %get-tuple-element.214.left_ref, bf16[256,3072]{1,0:T(8,128)(2,1)} %collective-permute-done.41.left_there_ref, bf16[256,1536]{1,0:T(8,128)(2,1)} %pad_maximum_fusion.18.right_ref, bf16[256,1536]{1,0:T(8,128)(2,1)} %collective-permute-done.38.right_there_ref), custom_call_target="tpu_custom_call" | custom-call | tf_op jit(solution)/shard_map/pallas_call | solution.py:522
  466.4 3.2 fusion.25
  481.8 4.1 shard_map.209
  496.2 7.2 %shard_map.211 = (bf16[256,1536]{1,0:T(8,128)(2,1)}, f32[4,128]{1,0:T(4,128)}) custom-call(f32[8]{0:T(128)} %fusion.122.scale_ref, bf16[256,1536]{1,0:T(8,128)(2,1)} %fusion.8.project_ref, s32[256,1]{1,0:T(8,128)} %copy.57.starts_ref, bf16[256,512]{1,0:T(8,128)(2,1)} %convolution_convert_fusion.2.grad_ref), custom_call_target="tpu_custom_call" | custom-call | tf_op jit(solution)/shard_map/pallas_call | solution.py:532
  503.5 4.0 fusion.41
  514.3 3.8 collective-permute-start.52
  519.0 6.9 shard_map.214
  525.9 2.7 fusion.152
  535.3 2.6 fusion.65
  543.7 4.0 shard_map.212
  554.3 19.7 %collective-permute-done.58 = bf16[4,128,1024]{2,1,0:T(8,128)(2,1)} collective-permute-done((bf16[4,128,1024]{2,1,0:T(8,128)(2,1)}, bf16[4,128,1024]{2,1,0:T(8,128)(2,1)}, u32[]{:S(2)}, u32[]{:S(2)}) %collective-permute-start.58) | collective-permute-done | bytes 1048608 | tf_op jit(solution)/shard_map/ppermute | solution.py:544
  577.1 19.4 %collective-permute-done.67 = bf16[4,128,1024]{2,1,0:T(8,128)(2,1)} collective-permute-done((bf16[4,128,1024]{2,1,0:T(8,128)(2,1)}, bf16[4,128,1024]{2,1,0:T(8,128)(2,1)}, u32[]{:S(2)}, u32[]{:S(2)}) %collective-permute-start.67) | collective-permute-done | bytes 1048608 | tf_op jit(solution)/shard_map/ppermute | solution.py:544
  596.5 2.7 collective-permute-start.61
  606.5 8.8 %collective-permute-start.69 = (bf16[128,1024]{1,0:T(8,128)(2,1)S(1)}, bf16[128,1024]{1,0:T(8,128)(2,1)S(1)}, u32[]{:S(2)}, u32[]{:S(2)}) collective-permute-start(bf16[128,1024]{1,0:T(8,128)(2,1)S(1)} %get-tuple-element.154), channel_id=1, source_target_pairs={{0,16},{8,24},{16,0},{24,8},{1,17},{9,25},{17,1},{25,9},{2,18},{10... | collective-permute-start | bytes 786440 | tf_op jit(solution)/shard_map/ppermute | solution.py:622
  615.3 16.1 %collective-permute-done.60 = bf16[128,1024]{1,0:T(8,128)(2,1)S(1)} collective-permute-done((bf16[128,1024]{1,0:T(8,128)(2,1)S(1)}, bf16[128,1024]{1,0:T(8,128)(2,1)S(1)}, u32[]{:S(2)}, u32[]{:S(2)}) %collective-permute-start.60) | collective-permute-done | bytes 262176 | tf_op jit(solution)/shard_map/ppermute | solution.py:622
  632.4 11.6 %collective-permute-done.69 = bf16[128,1024]{1,0:T(8,128)(2,1)S(1)} collective-permute-done((bf16[128,1024]{1,0:T(8,128)(2,1)S(1)}, bf16[128,1024]{1,0:T(8,128)(2,1)S(1)}, u32[]{:S(2)}, u32[]{:S(2)}) %collective-permute-start.69) | collective-permute-done | bytes 262176 | tf_op jit(solution)/shard_map/ppermute | solution.py:622
  646.4 2.9 collective-permute-start.55
  651.4 12.1 %collective-permute-done.72 = f32[2,10368]{1,0:T(2,128)S(1)} collective-permute-done((f32[2,10368]{1,0:T(2,128)S(1)}, f32[2,10368]{1,0:T(2,128)S(1)}, u32[]{:S(2)}, u32[]{:S(2)}) %collective-permute-start.72) | collective-permute-done | bytes 82976 | tf_op jit(solution)/shard_map/ppermute | solution.py:896
  663.6 7.3 %collective-permute-start.73 = (f32[2,10368]{1,0:T(2,128)S(1)}, f32[2,10368]{1,0:T(2,128)S(1)}, u32[]{:S(2)}, u32[]{:S(2)}) collective-permute-start(f32[2,10368]{1,0:T(2,128)S(1)} %add.651), channel_id=1, source_target_pairs={{0,16},{8,24},{16,0},{24,8},{1,17},{9,25},{17,1},{25,9},{2,18},{10... | collective-permute-start | bytes 248840 | tf_op jit(solution)/shard_map/ppermute | solution.py:896
  671.9 3.9 collective-permute-done.73
  (591 shorter events, 225.0 us)
Async XLA Ops:
  7.2 280.3 %all-gather.3.cloned.1.call-start = ((), (), s32[]{:S(2)}) async-start(), calls=%async_computation.1 | async-start | bytes 7077888 | tf_op jit(solution)/shard_map/all_gather | solution.py:605
  7.2 56.3 %collective-permute-start = (bf16[128,1024]{1,0:T(8,128)(2,1)}, bf16[128,1024]{1,0:T(8,128)(2,1)S(1)}, u32[]{:S(2)}, u32[]{:S(2)}) collective-permute-start(bf16[128,1024]{1,0:T(8,128)(2,1)} %param.12), channel_id=1, source_target_pairs={{0,0},{1,2},{2,1},{3,3},{4,4},{5,6},{6,5},{7,7},{8,8},{9,10},{10,9... | collective-permute-start | bytes 786440 | tf_op jit(solution)/shard_map/ppermute | solution.py:548
  17.7 46.8 %collective-permute-start.10 = (s32[256]{0:T(256)}, s32[256]{0:T(256)S(1)}, u32[]{:S(2)}, u32[]{:S(2)}) collective-permute-start(s32[256]{0:T(256)} %param.13), channel_id=1, source_target_pairs={{0,2},{2,0},{1,3},{3,1},{4,6},{6,4},{5,7},{7,5},{8,10},{10,8},{9,1... | collective-permute-start | bytes 3080 | tf_op jit(solution)/shard_map/ppermute | solution.py:544
  25.9 37.4 %collective-permute-start.4 = (bf16[128,2048]{1,0:T(8,128)(2,1)}, bf16[128,2048]{1,0:T(8,128)(2,1)}, u32[]{:S(2)}, u32[]{:S(2)}) collective-permute-start(bf16[128,2048]{1,0:T(8,128)(2,1)} %get-tuple-element.62), channel_id=1, source_target_pairs={{0,16},{8,24},{16,0},{24,8},{1,17},{9,25},{17,1},{25,9},{2,18},{10... | collective-permute-start | bytes 1572872 | tf_op jit(solution)/shard_map/ppermute | solution.py:633
  28.5 34.8 %collective-permute-start.5 = (bf16[128,2048]{1,0:T(8,128)(2,1)}, bf16[128,2048]{1,0:T(8,128)(2,1)}, u32[]{:S(2)}, u32[]{:S(2)}) collective-permute-start(bf16[128,2048]{1,0:T(8,128)(2,1)} %get-tuple-element.62), channel_id=1, source_target_pairs={{0,24},{8,0},{16,8},{24,16},{1,25},{9,1},{17,9},{25,17},{2,26},{10... | collective-permute-start | bytes 1572872 | tf_op jit(solution)/shard_map/ppermute | solution.py:633
  63.4 288.8 %all-gather.5.cloned.1.call-start = ((), (), s32[]{:S(2)}) async-start(), calls=%async_computation.2 | async-start | bytes 4718592 | tf_op jit(solution)/shard_map/all_gather | solution.py:605
  66.4 24.2 %collective-permute-start.12 = (bf16[128,1024]{1,0:T(8,128)(2,1)S(1)}, bf16[128,1024]{1,0:T(8,128)(2,1)S(1)}, u32[]{:S(2)}, u32[]{:S(2)}) collective-permute-start(bf16[128,1024]{1,0:T(8,128)(2,1)S(1)} %copy-done.63), channel_id=1, source_target_pairs={{0,4},{4,0},{1,5},{5,1},{2,6},{6,2},{3,7},{7,3},{8,12},{12,8},{9,1... | collective-permute-start | bytes 786440 | tf_op jit(solution)/shard_map/ppermute | solution.py:544
  67.9 22.7 %collective-permute-start.13 = (bf16[128,1024]{1,0:T(8,128)(2,1)S(1)}, bf16[128,1024]{1,0:T(8,128)(2,1)S(1)}, u32[]{:S(2)}, u32[]{:S(2)}) collective-permute-start(bf16[128,1024]{1,0:T(8,128)(2,1)S(1)} %copy-done.63), channel_id=1, source_target_pairs={{0,8},{8,16},{16,24},{24,0},{1,9},{9,17},{17,25},{25,1},{2,10},{10... | collective-permute-start | bytes 786440 | tf_op jit(solution)/shard_map/ppermute | solution.py:633
  79.7 31.0 %collective-permute-start.15 = (bf16[128,1024]{1,0:T(8,128)(2,1)S(1)}, bf16[128,1024]{1,0:T(8,128)(2,1)S(1)}, u32[]{:S(2)}, u32[]{:S(2)}) collective-permute-start(bf16[128,1024]{1,0:T(8,128)(2,1)S(1)} %copy-done.63), channel_id=1, source_target_pairs={{0,16},{8,24},{16,0},{24,8},{1,17},{9,25},{17,1},{25,9},{2,18},{10... | collective-permute-start | bytes 786440 | tf_op jit(solution)/shard_map/ppermute | solution.py:633
  81.2 41.4 %collective-permute-start.17 = (bf16[128,1024]{1,0:T(8,128)(2,1)S(1)}, bf16[128,1024]{1,0:T(8,128)(2,1)S(1)}, u32[]{:S(2)}, u32[]{:S(2)}) collective-permute-start(bf16[128,1024]{1,0:T(8,128)(2,1)S(1)} %copy-done.63), channel_id=1, source_target_pairs={{0,24},{8,0},{16,8},{24,16},{1,25},{9,1},{17,9},{25,17},{2,26},{10... | collective-permute-start | bytes 786440 | tf_op jit(solution)/shard_map/ppermute | solution.py:633
  82.0 108.7 %collective-permute-start.6 = (bf16[128,2048]{1,0:T(8,128)(2,1)}, bf16[128,2048]{1,0:T(8,128)(2,1)S(1)}, u32[]{:S(2)}, u32[]{:S(2)}) collective-permute-start(bf16[128,2048]{1,0:T(8,128)(2,1)} %get-tuple-element.62), channel_id=1, source_target_pairs={{0,4},{4,0},{1,5},{5,1},{2,6},{6,2},{3,7},{7,3},{8,12},{12,8},{9,1... | collective-permute-start | bytes 1572872 | tf_op jit(solution)/shard_map/ppermute | solution.py:544
  90.6 103.3 %collective-permute-start.7 = (bf16[128,2048]{1,0:T(8,128)(2,1)}, bf16[128,2048]{1,0:T(8,128)(2,1)S(1)}, u32[]{:S(2)}, u32[]{:S(2)}) collective-permute-start(bf16[128,2048]{1,0:T(8,128)(2,1)} %collective-permute-done.3), channel_id=1, source_target_pairs={{0,4},{4,0},{1,5},{5,1},{2,6},{6,2},{3,7},{7,3},{8,12},{12,8},{9,1... | collective-permute-start | bytes 1572872 | tf_op jit(solution)/shard_map/ppermute | solution.py:544
  90.6 30.2 %collective-permute-start.14 = (bf16[128,1024]{1,0:T(8,128)(2,1)S(1)}, bf16[128,1024]{1,0:T(8,128)(2,1)S(1)}, u32[]{:S(2)}, u32[]{:S(2)}) collective-permute-start(bf16[128,1024]{1,0:T(8,128)(2,1)S(1)} %collective-permute-done.13), channel_id=1, source_target_pairs={{0,4},{4,0},{1,5},{5,1},{2,6},{6,2},{3,7},{7,3},{8,12},{12,8},{9,1... | collective-permute-start | bytes 786440 | tf_op jit(solution)/shard_map/ppermute | solution.py:544
  110.7 92.3 %collective-permute-start.8 = (bf16[128,2048]{1,0:T(8,128)(2,1)}, bf16[128,2048]{1,0:T(8,128)(2,1)S(1)}, u32[]{:S(2)}, u32[]{:S(2)}) collective-permute-start(bf16[128,2048]{1,0:T(8,128)(2,1)} %collective-permute-done.4), channel_id=1, source_target_pairs={{0,4},{4,0},{1,5},{5,1},{2,6},{6,2},{3,7},{7,3},{8,12},{12,8},{9,1... | collective-permute-start | bytes 1572872 | tf_op jit(solution)/shard_map/ppermute | solution.py:544
  120.8 20.1 %collective-permute-start.16 = (bf16[128,1024]{1,0:T(8,128)(2,1)S(1)}, bf16[128,1024]{1,0:T(8,128)(2,1)S(1)}, u32[]{:S(2)}, u32[]{:S(2)}) collective-permute-start(bf16[128,1024]{1,0:T(8,128)(2,1)S(1)} %collective-permute-done.15), channel_id=1, source_target_pairs={{0,4},{4,0},{1,5},{5,1},{2,6},{6,2},{3,7},{7,3},{8,12},{12,8},{9,1... | collective-permute-start | bytes 786440 | tf_op jit(solution)/shard_map/ppermute | solution.py:544
  122.6 49.7 %collective-permute-start.20 = (bf16[128,1024]{1,0:T(8,128)(2,1)S(1)}, bf16[128,1024]{1,0:T(8,128)(2,1)S(1)}, u32[]{:S(2)}, u32[]{:S(2)}) collective-permute-start(bf16[128,1024]{1,0:T(8,128)(2,1)S(1)} %copy-done.62), channel_id=1, source_target_pairs={{0,4},{4,0},{1,5},{5,1},{2,6},{6,2},{3,7},{7,3},{8,12},{12,8},{9,1... | collective-permute-start | bytes 786440 | tf_op jit(solution)/shard_map/ppermute | solution.py:544
  141.0 22.0 %collective-permute-start.18 = (bf16[128,1024]{1,0:T(8,128)(2,1)S(1)}, bf16[128,1024]{1,0:T(8,128)(2,1)S(1)}, u32[]{:S(2)}, u32[]{:S(2)}) collective-permute-start(bf16[128,1024]{1,0:T(8,128)(2,1)S(1)} %collective-permute-done.17), channel_id=1, source_target_pairs={{0,4},{4,0},{1,5},{5,1},{2,6},{6,2},{3,7},{7,3},{8,12},{12,8},{9,1... | collective-permute-start | bytes 786440 | tf_op jit(solution)/shard_map/ppermute | solution.py:544
  162.9 21.7 %collective-permute-start.21 = (bf16[128,1024]{1,0:T(8,128)(2,1)S(1)}, bf16[128,1024]{1,0:T(8,128)(2,1)S(1)}, u32[]{:S(2)}, u32[]{:S(2)}) collective-permute-start(bf16[128,1024]{1,0:T(8,128)(2,1)S(1)} %copy-done.62), channel_id=1, source_target_pairs={{0,8},{8,16},{16,24},{24,0},{1,9},{9,17},{17,25},{25,1},{2,10},{10... | collective-permute-start | bytes 786440 | tf_op jit(solution)/shard_map/ppermute | solution.py:633
  172.4 39.9 %collective-permute-start.9 = (bf16[128,2048]{1,0:T(8,128)(2,1)}, bf16[128,2048]{1,0:T(8,128)(2,1)S(1)}, u32[]{:S(2)}, u32[]{:S(2)}) collective-permute-start(bf16[128,2048]{1,0:T(8,128)(2,1)} %collective-permute-done.5), channel_id=1, source_target_pairs={{0,4},{4,0},{1,5},{5,1},{2,6},{6,2},{3,7},{7,3},{8,12},{12,8},{9,1... | collective-permute-start | bytes 1572872 | tf_op jit(solution)/shard_map/ppermute | solution.py:544
  193.9 83.2 %collective-permute-start.19 = (bf16[1024,1024]{1,0:T(8,128)(2,1)}, bf16[1024,1024]{1,0:T(8,128)(2,1)}, u32[]{:S(2)}, u32[]{:S(2)}) collective-permute-start(bf16[1024,1024]{1,0:T(8,128)(2,1)} %bitcast.25), channel_id=1, source_target_pairs={{0,1},{1,0},{2,3},{3,2},{4,5},{5,4},{6,7},{7,6},{8,9},{9,8},{10,11... | collective-permute-start | bytes 6291464 | tf_op jit(solution)/shard_map/ppermute | solution.py:544
  212.1 65.0 %collective-permute-start.27 = (bf16[1024,1024]{1,0:T(8,128)(2,1)S(1)}, bf16[1024,1024]{1,0:T(8,128)(2,1)}, u32[]{:S(2)}, u32[]{:S(2)}) collective-permute-start(bf16[1024,1024]{1,0:T(8,128)(2,1)S(1)} %bitcast.284), channel_id=1, source_target_pairs={{0,1},{1,0},{2,3},{3,2},{4,5},{5,4},{6,7},{7,6},{8,9},{9,8},{10,11... | collective-permute-start | bytes 6291464 | tf_op jit(solution)/shard_map/ppermute | solution.py:544
  224.5 51.2 %collective-permute-start.11 = (bf16[256,1024]{1,0:T(8,128)(2,1)}, bf16[256,1024]{1,0:T(8,128)(2,1)}, u32[]{:S(2)}, u32[]{:S(2)}) collective-permute-start(bf16[256,1024]{1,0:T(8,128)(2,1)} %convolution_convert_fusion.1), channel_id=1, source_target_pairs={{0,2},{2,0},{1,3},{3,1},{4,6},{6,4},{5,7},{7,5},{8,10},{10,8},{9,1... | collective-permute-start | bytes 1572872 | tf_op jit(solution)/shard_map/ppermute | solution.py:544
  226.7 47.2 %collective-permute-start.29 = (bf16[128,1024]{1,0:T(8,128)(2,1)S(1)}, bf16[128,1024]{1,0:T(8,128)(2,1)}, u32[]{:S(2)}, u32[]{:S(2)}) collective-permute-start(bf16[128,1024]{1,0:T(8,128)(2,1)S(1)} %collective-permute-done.28), channel_id=1, source_target_pairs={{0,2},{2,0},{1,3},{3,1},{4,6},{6,4},{5,7},{7,5},{8,10},{10,8},{9,1... | collective-permute-start | bytes 786440 | tf_op jit(solution)/shard_map/ppermute | solution.py:544
  272.6 413.8 %reduce-scatter.2.cloned.1.call-start = ((), (), s32[]{:S(2)}) async-start(), calls=%async_computation.3 | async-start | bytes 4718592 | tf_op jit(solution)/shard_map/reduce_scatter | solution.py:608
  273.9 108.6 %collective-permute-start.39 = (bf16[256,1536]{1,0:T(8,128)(2,1)}, bf16[256,1536]{1,0:T(8,128)(2,1)}, u32[]{:S(2)}, u32[]{:S(2)}) collective-permute-start(bf16[256,1536]{1,0:T(8,128)(2,1)} %pad_maximum_fusion.16.left_ref), channel_id=1, source_target_pairs={{0,1},{1,0},{2,3},{3,2},{4,5},{5,4},{6,7},{7,6},{8,9},{9,8},{10,11... | collective-permute-start | bytes 2359304 | tf_op jit(solution)/shard_map/ppermute | solution.py:544
  289.3 50.3 %collective-permute-start.32 = (bf16[1024,1024]{1,0:T(8,128)(2,1)S(1)}, bf16[1024,1024]{1,0:T(8,128)(2,1)}, u32[]{:S(2)}, u32[]{:S(2)}) collective-permute-start(bf16[1024,1024]{1,0:T(8,128)(2,1)S(1)} %slice.420), channel_id=1, source_target_pairs={{0,1},{1,0},{2,3},{3,2},{4,5},{5,4},{6,7},{7,6},{8,9},{9,8},{10,11... | collective-permute-start | bytes 6291464 | tf_op jit(solution)/shard_map/ppermute | solution.py:544
  297.3 85.2 %collective-permute-start.40 = (bf16[256,3072]{1,0:T(8,128)(2,1)}, bf16[256,3072]{1,0:T(8,128)(2,1)}, u32[]{:S(2)}, u32[]{:S(2)}) collective-permute-start(bf16[256,3072]{1,0:T(8,128)(2,1)} %get-tuple-element.199), channel_id=1, source_target_pairs={{0,1},{1,0},{2,3},{3,2},{4,5},{5,4},{6,7},{7,6},{8,9},{9,8},{10,11... | collective-permute-start | bytes 4718600 | tf_op jit(solution)/shard_map/ppermute | solution.py:544
  380.7 48.2 %collective-permute-start.42 = (bf16[256,1536]{1,0:T(8,128)(2,1)}, bf16[256,1536]{1,0:T(8,128)(2,1)}, u32[]{:S(2)}, u32[]{:S(2)}) collective-permute-start(bf16[256,1536]{1,0:T(8,128)(2,1)} %pad_maximum_fusion.17.left_ref), channel_id=1, source_target_pairs={{0,1},{1,0},{2,3},{3,2},{4,5},{5,4},{6,7},{7,6},{8,9},{9,8},{10,11... | collective-permute-start | bytes 2359304 | tf_op jit(solution)/shard_map/ppermute | solution.py:544
  384.7 67.3 %collective-permute-start.41 = (bf16[256,3072]{1,0:T(8,128)(2,1)}, bf16[256,3072]{1,0:T(8,128)(2,1)}, u32[]{:S(2)}, u32[]{:S(2)}) collective-permute-start(bf16[256,3072]{1,0:T(8,128)(2,1)} %get-tuple-element.215), channel_id=1, source_target_pairs={{0,1},{1,0},{2,3},{3,2},{4,5},{5,4},{6,7},{7,6},{8,9},{9,8},{10,11... | collective-permute-start | bytes 4718600 | tf_op jit(solution)/shard_map/ppermute | solution.py:544
  396.4 55.6 %collective-permute-start.38 = (bf16[256,1536]{1,0:T(8,128)(2,1)}, bf16[256,1536]{1,0:T(8,128)(2,1)}, u32[]{:S(2)}, u32[]{:S(2)}) collective-permute-start(bf16[256,1536]{1,0:T(8,128)(2,1)} %pad_maximum_fusion.15), channel_id=1, source_target_pairs={{0,1},{1,0},{2,3},{3,2},{4,5},{5,4},{6,7},{7,6},{8,9},{9,8},{10,11... | collective-permute-start | bytes 2359304 | tf_op jit(solution)/shard_map/ppermute | solution.py:544
  422.6 47.1 %collective-permute-start.44 = (bf16[256,1280]{1,0:T(8,128)(2,1)}, bf16[256,1280]{1,0:T(8,128)(2,1)}, u32[]{:S(2)}, u32[]{:S(2)}) collective-permute-start(bf16[256,1280]{1,0:T(8,128)(2,1)} %pad_maximum_fusion.27), channel_id=1, source_target_pairs={{0,1},{1,0},{2,3},{3,2},{4,5},{5,4},{6,7},{7,6},{8,9},{9,8},{10,11... | collective-permute-start | bytes 1966088 | tf_op jit(solution)/shard_map/ppermute | solution.py:544
  487.7 31.3 %collective-permute-start.57 = (bf16[256,1536]{1,0:T(8,128)(2,1)}, bf16[256,1536]{1,0:T(8,128)(2,1)}, u32[]{:S(2)}, u32[]{:S(2)}) collective-permute-start(bf16[256,1536]{1,0:T(8,128)(2,1)} %pad_maximum_fusion.20), channel_id=1, source_target_pairs={{0,1},{1,0},{2,3},{3,2},{4,5},{5,4},{6,7},{7,6},{8,9},{9,8},{10,11... | collective-permute-start | bytes 2359304 | tf_op jit(solution)/shard_map/ppermute | solution.py:544
  508.4 24.5 %collective-permute-start.46 = (bf16[256,1024]{1,0:T(8,128)(2,1)}, bf16[256,1024]{1,0:T(8,128)(2,1)}, u32[]{:S(2)}, u32[]{:S(2)}) collective-permute-start(bf16[256,1024]{1,0:T(8,128)(2,1)} %fusion.41), channel_id=1, source_target_pairs={{0,2},{2,0},{1,3},{3,1},{4,6},{6,4},{5,7},{7,5},{8,10},{10,8},{9,1... | collective-permute-start | bytes 1572872 | tf_op jit(solution)/shard_map/ppermute | solution.py:544
  511.6 27.9 %collective-permute-start.48 = (bf16[256,1280]{1,0:T(8,128)(2,1)}, bf16[256,1280]{1,0:T(8,128)(2,1)}, u32[]{:S(2)}, u32[]{:S(2)}) collective-permute-start(bf16[256,1280]{1,0:T(8,128)(2,1)} %pad_maximum_fusion.30), channel_id=1, source_target_pairs={{0,1},{1,0},{2,3},{3,2},{4,5},{5,4},{6,7},{7,6},{8,9},{9,8},{10,11... | collective-permute-start | bytes 1966088 | tf_op jit(solution)/shard_map/ppermute | solution.py:544
  514.3 35.6 %collective-permute-start.52 = (bf16[4,128,1024]{2,1,0:T(8,128)(2,1)}, bf16[4,128,1024]{2,1,0:T(8,128)(2,1)}, u32[]{:S(2)}, u32[]{:S(2)}) collective-permute-start(bf16[4,128,1024]{2,1,0:T(8,128)(2,1)} %dynamic-slice_bitcast_fusion.2), channel_id=1, source_target_pairs={{0,4},{4,0},{1,5},{5,1},{2,6},{6,2},{3,7},{7,3},{8,12},{12,8},{9,1... | collective-permute-start | bytes 3145736 | tf_op jit(solution)/shard_map/ppermute | solution.py:544
  529.7 44.3 %collective-permute-start.58 = (bf16[4,128,1024]{2,1,0:T(8,128)(2,1)}, bf16[4,128,1024]{2,1,0:T(8,128)(2,1)}, u32[]{:S(2)}, u32[]{:S(2)}) collective-permute-start(bf16[4,128,1024]{2,1,0:T(8,128)(2,1)} %dynamic-slice_bitcast_fusion.1), channel_id=1, source_target_pairs={{0,4},{4,0},{1,5},{5,1},{2,6},{6,2},{3,7},{7,3},{8,12},{12,8},{9,1... | collective-permute-start | bytes 3145736 | tf_op jit(solution)/shard_map/ppermute | solution.py:544
  531.3 65.2 %collective-permute-start.67 = (bf16[4,128,1024]{2,1,0:T(8,128)(2,1)}, bf16[4,128,1024]{2,1,0:T(8,128)(2,1)}, u32[]{:S(2)}, u32[]{:S(2)}) collective-permute-start(bf16[4,128,1024]{2,1,0:T(8,128)(2,1)} %dynamic-slice_bitcast_fusion), channel_id=1, source_target_pairs={{0,4},{4,0},{1,5},{5,1},{2,6},{6,2},{3,7},{7,3},{8,12},{12,8},{9,1... | collective-permute-start | bytes 3145736 | tf_op jit(solution)/shard_map/ppermute | solution.py:544
  549.2 94.9 %collective-permute-start.49 = (bf16[4,128,1024]{2,1,0:T(8,128)(2,1)S(1)}, bf16[4,128,1024]{2,1,0:T(8,128)(2,1)S(1)}, u32[]{:S(2)}, u32[]{:S(2)}) collective-permute-start(bf16[4,128,1024]{2,1,0:T(8,128)(2,1)S(1)} %fusion.69), channel_id=1, source_target_pairs={{0,4},{4,0},{1,5},{5,1},{2,6},{6,2},{3,7},{7,3},{8,12},{12,8},{9,1... | collective-permute-start | bytes 3145736 | tf_op jit(solution)/shard_map/ppermute | solution.py:544
  551.7 49.2 %collective-permute-start.65 = (bf16[128,1024]{1,0:T(8,128)(2,1)S(1)}, bf16[128,1024]{1,0:T(8,128)(2,1)S(1)}, u32[]{:S(2)}, u32[]{:S(2)}) collective-permute-start(bf16[128,1024]{1,0:T(8,128)(2,1)S(1)} %get-tuple-element.162), channel_id=1, source_target_pairs={{0,24},{8,0},{16,8},{24,16},{1,25},{9,1},{17,9},{25,17},{2,26},{10... | collective-permute-start | bytes 786440 | tf_op jit(solution)/shard_map/ppermute | solution.py:622
  553.4 47.7 %collective-permute-start.64 = (bf16[128,1024]{1,0:T(8,128)(2,1)S(1)}, bf16[128,1024]{1,0:T(8,128)(2,1)S(1)}, u32[]{:S(2)}, u32[]{:S(2)}) collective-permute-start(bf16[128,1024]{1,0:T(8,128)(2,1)S(1)} %get-tuple-element.163), channel_id=1, source_target_pairs={{0,16},{8,24},{16,0},{24,8},{1,17},{9,25},{17,1},{25,9},{2,18},{10... | collective-permute-start | bytes 786440 | tf_op jit(solution)/shard_map/ppermute | solution.py:622
  574.0 28.7 %collective-permute-start.63 = (bf16[128,1024]{1,0:T(8,128)(2,1)S(1)}, bf16[128,1024]{1,0:T(8,128)(2,1)S(1)}, u32[]{:S(2)}, u32[]{:S(2)}) collective-permute-start(bf16[128,1024]{1,0:T(8,128)(2,1)S(1)} %get-tuple-element.161), channel_id=1, source_target_pairs={{0,8},{8,16},{16,24},{24,0},{1,9},{9,17},{17,25},{25,1},{2,10},{10... | collective-permute-start | bytes 786440 | tf_op jit(solution)/shard_map/ppermute | solution.py:622
  600.9 30.5 %collective-permute-start.60 = (bf16[128,1024]{1,0:T(8,128)(2,1)S(1)}, bf16[128,1024]{1,0:T(8,128)(2,1)S(1)}, u32[]{:S(2)}, u32[]{:S(2)}) collective-permute-start(bf16[128,1024]{1,0:T(8,128)(2,1)S(1)} %get-tuple-element.160), channel_id=1, source_target_pairs={{0,16},{8,24},{16,0},{24,8},{1,17},{9,25},{17,1},{25,9},{2,18},{10... | collective-permute-start | bytes 786440 | tf_op jit(solution)/shard_map/ppermute | solution.py:622
  601.1 30.4 %collective-permute-start.59 = (bf16[128,1024]{1,0:T(8,128)(2,1)S(1)}, bf16[128,1024]{1,0:T(8,128)(2,1)S(1)}, u32[]{:S(2)}, u32[]{:S(2)}) collective-permute-start(bf16[128,1024]{1,0:T(8,128)(2,1)S(1)} %get-tuple-element.158), channel_id=1, source_target_pairs={{0,8},{8,16},{16,24},{24,0},{1,9},{9,17},{17,25},{25,1},{2,10},{10... | collective-permute-start | bytes 786440 | tf_op jit(solution)/shard_map/ppermute | solution.py:622
  602.7 29.7 %collective-permute-start.70 = (bf16[128,1024]{1,0:T(8,128)(2,1)S(1)}, bf16[128,1024]{1,0:T(8,128)(2,1)S(1)}, u32[]{:S(2)}, u32[]{:S(2)}) collective-permute-start(bf16[128,1024]{1,0:T(8,128)(2,1)S(1)} %get-tuple-element.153), channel_id=1, source_target_pairs={{0,24},{8,0},{16,8},{24,16},{1,25},{9,1},{17,9},{25,17},{2,26},{10... | collective-permute-start | bytes 786440 | tf_op jit(solution)/shard_map/ppermute | solution.py:622
  606.5 37.5 %collective-permute-start.69 = (bf16[128,1024]{1,0:T(8,128)(2,1)S(1)}, bf16[128,1024]{1,0:T(8,128)(2,1)S(1)}, u32[]{:S(2)}, u32[]{:S(2)}) collective-permute-start(bf16[128,1024]{1,0:T(8,128)(2,1)S(1)} %get-tuple-element.154), channel_id=1, source_target_pairs={{0,16},{8,24},{16,0},{24,8},{1,17},{9,25},{17,1},{25,9},{2,18},{10... | collective-permute-start | bytes 786440 | tf_op jit(solution)/shard_map/ppermute | solution.py:622
  646.4 29.6 %collective-permute-start.56 = (bf16[128,1024]{1,0:T(8,128)(2,1)S(1)}, bf16[128,1024]{1,0:T(8,128)(2,1)S(1)}, u32[]{:S(2)}, u32[]{:S(2)}) collective-permute-start(bf16[128,1024]{1,0:T(8,128)(2,1)S(1)} %get-tuple-element.156), channel_id=1, source_target_pairs={{0,24},{8,0},{16,8},{24,16},{1,25},{9,1},{17,9},{25,17},{2,26},{10... | collective-permute-start | bytes 786440 | tf_op jit(solution)/shard_map/ppermute | solution.py:622
  646.4 29.5 %collective-permute-start.55 = (bf16[128,1024]{1,0:T(8,128)(2,1)S(1)}, bf16[128,1024]{1,0:T(8,128)(2,1)S(1)}, u32[]{:S(2)}, u32[]{:S(2)}) collective-permute-start(bf16[128,1024]{1,0:T(8,128)(2,1)S(1)} %get-tuple-element.157), channel_id=1, source_target_pairs={{0,16},{8,24},{16,0},{24,8},{1,17},{9,25},{17,1},{25,9},{2,18},{10... | collective-permute-start | bytes 786440 | tf_op jit(solution)/shard_map/ppermute | solution.py:622
  649.3 26.7 %collective-permute-start.54 = (bf16[128,1024]{1,0:T(8,128)(2,1)S(1)}, bf16[128,1024]{1,0:T(8,128)(2,1)S(1)}, u32[]{:S(2)}, u32[]{:S(2)}) collective-permute-start(bf16[128,1024]{1,0:T(8,128)(2,1)S(1)} %get-tuple-element.155), channel_id=1, source_target_pairs={{0,8},{8,16},{16,24},{24,0},{1,9},{9,17},{17,25},{25,1},{2,10},{10... | collective-permute-start | bytes 786440 | tf_op jit(solution)/shard_map/ppermute | solution.py:622
  (107 other events, 842.3 us)
Sparse Core Ops, SparseCore 0:
  63.5 154.1 all-gather.2
  272.8 72.2 all-gather.4
  466.5 108.5 reduce-scatter.1

commit v3 on v2

--- a/solution.py
+++ b/solution.py
@@ -492,13 +492,15 @@
     layers, shard, width = out_ref.shape
     half = width // 2
     span = own_ref.shape[2] - 2 * width
-    first, second, up, *downs = units
-    attention, ups = (first, second.at[:, : 2 * width]), (up, second.at[:, 2 * width :])
+    first, up, down, second = units
+    attention, ups = (first, second.at[:, : 2 * width]), (up, second.at[:, 2 * width : 4 * width])
+    downs = (down, second.at[:, 4 * width :])
     for layer in range(layers):
         for source_ref, which in ((own_ref, core), (there_ref, 1 - core)):
             rows = pl.ds(pl.multiple_of(which * shard, shard), shard)
             attention[layer][rows, :span] = source_ref[layer, :, :span]
-            ups[layer][rows, :] = source_ref[layer, :, span : span + width]
+            columns = ups[layer].shape[1]
+            ups[layer][rows, :] = source_ref[layer, :, span : span + columns]
         attention[layer][:shard, span:] = out_ref[layer, :, :half]
         attention[layer][shard:, span:] = out_ref[layer, :, half:]
         for part in range(downs[layer].shape[1] // width):
@@ -507,14 +509,17 @@
             downs[layer][:, part * width : part * width + width] = down_ref[layer, rows, :]
 
 
-def term_product(arrays, parts, shape):
-    def body(left_ref, left_there_ref, right_ref, right_there_ref, out_ref):
-        for left_at, right_at, columns, out_at in parts:
+def term_product(lefts, lefts_there, rights, parts, shape):
+    count = len(lefts)
+
+    def body(*refs):
+        right_ref, right_there_ref, out_ref = refs[2 * count :]
+        for which, left_at, right_at, columns, out_at in parts:
             right = right_ref[:, right_at : right_at + columns]
             right_there = right_there_ref[:, right_at : right_at + columns]
             for row in range(0, shape[0], 256):
-                left = left_ref[:, left_at + row : left_at + row + 256]
-                left_there = left_there_ref[:, left_at + row : left_at + row + 256]
+                left = refs[which][:, left_at + row : left_at + row + 256]
+                left_there = refs[count + which][:, left_at + row : left_at + row + 256]
                 total = contract(left, right, 0, 0) + contract(left_there, right_there, 0, 0)
                 out_ref[row : row + 256, out_at : out_at + columns] = total.astype(jnp.bfloat16)
 
@@ -522,9 +527,9 @@
     return pl.pallas_call(
         body,
         out_shape=jax.ShapeDtypeStruct(shape, jnp.bfloat16),
-        in_specs=[vmem] * 4,
+        in_specs=[vmem] * (2 * count + 2),
         out_specs=vmem,
-    )(*arrays)
+    )(*lefts, *lefts_there, *rights)
 
 
 def run_small(body, scale, arrays, outs):
@@ -647,27 +652,25 @@
     own, there = run_small(
         pack_columns, place, (qkv_weight, fc1_weight), [(narrow, bf16), (narrow, bf16)]
     )
-    wides = (4 * head_width, 4 * head_width + width, width, width, 2 * width)
     packed = run_small(
         pack_rows,
         place,
         (own, swap(there, "c"), out_weight, fc2_weight),
-        [((2 * shard, columns), bf16) for columns in wides],
+        [((2 * shard, columns), bf16) for columns in (2 * width, width, width, 6 * width)],
     )
     got = []
-    for unit in (packed[0], packed[2], packed[3]):
+    for unit in (packed[1], packed[2], packed[0]):
         if got:
             unit, got[-1][1] = tie(unit, got[-1][1])
         got.append(z_pieces(unit))
-    late = packed[1]
-    late, *got[0] = tie(late, *got[0])
+    got = [join(pieces) for pieces in got]
+    late, got[0] = tie(packed[3], got[0])
     late = gather(late)
-    got = [join(pieces) for pieces in got]
-    last_down = gather(packed[4])
-    last_up = late[:, 4 * head_width :]
-    ups = [(got[1], swap(got[1], "y")), (last_up, swap(last_up, "y"))]
-    downs = [(got[2], swap(got[2], "y")), (last_down[:, :width], last_down[:, width:])]
-    attention_mats = [got[0], late]
+    up_there, down_there = swap(got[0], "y"), swap(got[1], "y")
+    late_parts = [late[:, width * part : width * (part + 1)] for part in range(2, 6)]
+    ups = [(got[0], up_there), late_parts[:2]]
+    downs = [(got[1], down_there), late_parts[2:]]
+    attention_mats = [got[2], late]
 
     def matrices(which):
         packed = attention_mats[which]
@@ -690,16 +693,11 @@
     starts = jnp.where(ic == iy, seq_start, swap(seq_start, "c"))
     starts = starts[:, None]
 
-    cotangent_late, attention_mats[0] = tie(cotangent, attention_mats[0])
     mats = [matrices(which) for which in range(LAYERS)]
     kept = []
     for which in range(LAYERS):
         qkv_mat, out_mat, up_mat, down_mat = mats[which]
         scale_here = pick(head_scale[which].reshape(heads_here, 2), ic, 1)
-        if which == 1:
-            hidden, far_up = tie(hidden, up_mat[1])
-            up_mat = (up_mat[0], far_up)
-            mats[1] = (qkv_mat, out_mat, up_mat, down_mat)
         norm_a, inv_a = norm_parts(hidden)
         a_low = (norm_a * norm_gain[which, 0] + norm_bias[which, 0]).astype(bf16)
         project = product(a_low, qkv_mat).astype(bf16)
@@ -707,7 +705,10 @@
             attention_forward, scale_here, (project, starts), [((group_rows, head_width), bf16)]
         )
         branch = both_cores(product(scaled, out_mat))
-        if which == 0:
+        if which == 1:
+            branch, *there = tie(branch, *kept[0][-1][:2])
+            kept[0] = kept[0][:-1] + ((*there, kept[0][-1][2]),)
+        else:
             branch, far_up, far_down = tie(branch, up_mat[1], down_mat[1])
             up_mat, down_mat = (up_mat[0], far_up), (down_mat[0], far_down)
             mats[0] = (qkv_mat, out_mat, up_mat, down_mat)
@@ -729,24 +730,19 @@
         norm_m = (activated - mean_all[:, None]) * inv_m
         gain_m, bias_m = mine_of(mid_gain[which]), mine_of(mid_bias[which])
         mixed_low = (norm_m * gain_m + bias_m).astype(bf16)
-        if which == 1:
-            last = kept[0]
-            mixed_low, there_a, there_h = tie(mixed_low, last[-3], last[-1])
-            kept[0] = last[:-3] + (there_a, last[-2], there_h)
         near, far = mixed_low[:, :half_units], mixed_low[:, half_units:]
         hidden = middle + both_cores(product(near, down_mat[0]) + product(far, down_mat[1]))
         attention_in = jnp.concatenate([a_low, scaled], axis=1)
-        hidden_in = jnp.concatenate([b_low, mixed_low], axis=1)
-        hidden_there = swap(jnp.concatenate([b_low, far, near], axis=1), "y")
-        attention_there = swap(attention_in, "y")
+        mixed_there = swap(jnp.concatenate([far, near], axis=1), "y")
+        ins_there = (swap(attention_in, "y"), swap(b_low, "y"), mixed_there)
         kept.append(
             (
                 norm_a, inv_a, project, scale_here, norm_z, inv_z, norm_b, inv_b, pre_act, below, norm_m, inv_m, gain_m,
-                attention_in, attention_there, hidden_in, hidden_there,
+                attention_in, b_low, mixed_low, ins_there,
             )
         )
     output = lax.dynamic_slice_in_dim(hidden.astype(bf16), ic * rows, rows, 0)
-    turned = turn(cotangent_late)
+    turned = turn(cotangent)
     grad_hidden = cores(turned, swap(turned, "c")).astype(f32)
 
     def natural(values):
@@ -757,7 +753,7 @@
         qkv_mat, out_mat, up_mat, down_mat = mats[which]
         (
             norm_a, inv_a, project, scale_here, norm_z, inv_z, norm_b, inv_b, pre_act, below, norm_m, inv_m, gain_m,
-            attention_in, attention_there, hidden_in, hidden_there,
+            attention_in, b_low, mixed_low, ins_there,
         ) = kept[which]
         final_low = grad_hidden.astype(bf16)
         grad_mixed = jnp.concatenate([product(final_low, part.T) for part in down_mat], axis=1)
@@ -769,7 +765,10 @@
         grad_act = inv_m * (scaled_grad - sums[0][:, None] - norm_m * sums[1][:, None])
         slope = below + pre_act * jnp.exp(-0.5 * pre_act * pre_act) * (1.0 / math.sqrt(2 * math.pi))
         grad_pre = (grad_act * slope).astype(bf16)
-        if which == 0:
+        attention_there, b_there, mixed_there = ins_there
+        if which == 1:
+            grad_pre, attention_there, b_there = tie(grad_pre, attention_there, b_there)
+        else:
             grad_pre, at_there = tie(grad_pre, at_there)
             later = finish_attention(at_there)
         near, far = grad_pre[:, :half_units], grad_pre[:, half_units:]
@@ -806,6 +805,17 @@
             [((group_rows, 3 * head_width), bf16), ((heads_here // 2, 2 * HD), f32)],
         )
         scale_grad = jnp.sum(scale_grad.reshape(heads_here, HD), axis=1)
+        grad_project, ff_there, mixed_there = tie(grad_project, ff_there, mixed_there)
+        ff_term = term_product(
+            (b_low, mixed_low),
+            (b_there, mixed_there),
+            (ff_out, ff_there),
+            ((0, 0, 0, width, 0), (1, 0, width, half, width), (1, width, width, half, width + half)),
+            (width, 2 * width),
+        )
+        if which == 1:
+            grad_project, ff_term = tie(grad_project, ff_term)
+            ff_rows = scatter(ff_term)
         grad_normed = both_cores(product(grad_project, qkv_mat.T))
         grad_input, gain_zero, bias_zero = norm_backward(
             grad_normed, norm_a, inv_a, norm_gain[which, 0]
@@ -822,33 +832,18 @@
             axis=1,
         )
         at_there = swap(at_there, "y")
-        if which == 1:
-            grad_input, ff_there, hidden_there, attention_there = tie(
-                grad_input, ff_there, hidden_there, attention_there
-            )
-        ff_term = term_product(
-            (hidden_in, hidden_there, ff_out, ff_there),
-            ((0, 0, width, 0), (width, width, half, width), (2 * width, width, half, width + half)),
-            (width, 2 * width),
-        )
         grad_hidden = grad_middle + grad_input
-        if which == 1:
-            grad_hidden, ff_term = tie(grad_hidden, ff_term)
-            ff_rows = scatter(ff_term)
-        else:
-            ff_rows = jnp.concatenate(
-                [steps(ff_term[:, :width]), steps(ff_term[:, width:])], axis=1
-            )
 
         def attention_term(there, here=at_out, ins=attention_in, ins_there=attention_there):
             split = half // 2
+            rights = (here, there)
             out_term = term_product(
-                (ins[:, width:], ins_there[:, width:], here[:, wide:], there[:, wide:]),
-                ((0, 0, half, 0),),
-                (head_width, half),
+                (ins,), (ins_there,), rights, ((0, width, wide, half, 0),), (head_width, half)
             ).reshape(chips, shard, half)
             out_term = jnp.concatenate([out_term[..., :split], out_term[..., split:]], axis=1)
-            qkv_term = term_product((ins, ins_there, here, there), ((0, 0, wide, 0),), (width, wide))
+            qkv_term = term_product(
+                (ins,), (ins_there,), rights, ((0, 0, 0, wide, 0),), (width, wide)
+            )
             return jnp.concatenate([qkv_term, out_term.reshape(-1, split)], axis=1)
 
         if which == 1:
@@ -856,8 +851,8 @@
         else:
             grad_hidden, later = tie(grad_hidden, later)
             at_rows_last = step_z(later)
-            at_rows = step_x(attention_term(at_there))
-        pending[which] = ff_rows
+        if which == 1:
+            pending[1] = ff_rows
         shared = jnp.concatenate([gain_zero, gain_one, gain_two, bias_zero, bias_one, bias_two])
         vectors[which] = jnp.concatenate(
             [0.5 * shared, natural(mid_gain_grad), natural(mid_bias_grad), jnp.pad(scale_grad, (0, 128 - heads_here))]
@@ -865,9 +860,15 @@
 
     vector = jnp.stack(vectors)
     vector = vector + swap(vector, "y")
-    vector, at_rows, output = tie(vector, at_rows, output)
-    at_rows = step_z(at_rows)
     vector = vector + swap(vector, "x")
+    vector, ff_term = tie(vector, ff_term)
+    up_held, down_held = step_x(ff_term[:, :width]), step_x(ff_term[:, width:])
+    for bit in (1, 2):
+        vector = vector + lax.ppermute(vector, "z", [(i, i ^ bit) for i in range(nz)])
+    at_held = step_x(attention_term(at_there))
+    at_held, output, grad_hidden = tie(at_held, output, grad_hidden)
+    pending[0] = jnp.concatenate([step_z(up_held), step_z(down_held)], axis=1)
+    at_rows = step_z(at_held)
     matrix_grads = []
     for at_rows, ff_rows in ((at_rows, pending[0]), (at_rows_last, pending[1])):
         grad_out = at_rows[:, wide:].reshape(2, shard, half // 2)
@@ -892,8 +893,6 @@
 
     grad_tokens = turn(lax.dynamic_slice_in_dim(grad_hidden, ic * rows, rows, 0))
     output = turn(output)
-    for bit in (1, 2):
-        vector = vector + lax.ppermute(vector, "z", [(i, i ^ bit) for i in range(nz)])
     there = swap(vector, "c")
     shared = vector[:, : 6 * width] + there[:, : 6 * width]
 

time: 707 us -> 659 us (0.932)
  starting transfers between devices: 154 us -> 111 us
  waiting for transfers between devices: 275 us -> 292 us
  other arithmetic: 84.5 us -> 70.8 us
  local copies, waits for them, and re-layouts: 64.6 us -> 54.2 us
    all_gather x2 -> x1, waiting for transfers between devices: 0.02 us -> 55.7 us  [gather(): return lax.all_gather(array, ('z', 'x'), axis=0, tiled=True)]
    ppermute x48 -> x49, waiting for transfers between devices: 157 us -> 109 us  [swap(): return lax.ppermute(array, axis, SWAP)]
    ppermute x48 -> x49, starting transfers between devices: 80.4 us -> 43.1 us  [swap(): return lax.ppermute(array, axis, SWAP)]
    ppermute x12, waiting for transfers between devices: 29.2 us -> 51.2 us  [step_z(): total = total + lax.ppermute(there, 'z', ring).astype(f32)]
    reduce_sum x6, other arithmetic: 15.3 us -> 2.74 us  [norm_parts(): jnp.mean(center * center, axis=-1, keepdims=True) + norm_eps]
    ppermute x2, waiting for transfers between devices: 16.1 us -> 6.73 us  [local_chip(): lax.ppermute(vector, 'z', [(i, i ^ bit) for i in range(nz)])]
    slice x5 -> x0, local copies, waits for them, and re-layouts: 8.51 us -> none  [the longest x2 3.37 us: attention_term(): there[:, wide:]]
    unnamed x166 -> x192, local copies, waits for them, and re-layouts: 10 us -> 14.2 us
  transfers between devices with their start and end apart: 78 -> 78, of which waited for: 24 -> 29; matrix products, arithmetic and copies ran while one was open for 26% -> 23% of each run, Pallas kernels for 8% -> 8%
where the time goes in v3:
time: 659 us; the launch traced here: 653 us
  waiting for transfers between devices  292 us (44%)
  starting transfers between devices  111 us (17%)
  other arithmetic  70.8 us (11%)
  Pallas kernels  60.4 us (9%)
  local copies, waits for them, and re-layouts  54.2 us (8%)
  matrix products  48.4 us (7%)
  between operations  16.8 us (3%)
    ppermute x49, waiting for transfers between devices, swap(): return lax.ppermute(array, axis, SWAP)  109 us
    ppermute x9, waiting for transfers between devices, z_pieces(): lax.ppermute(array, 'z', [(i, (i + step) % nz) for i in range(nz)])  69.3 us
    all_gather x1, waiting for transfers between devices, gather(): return lax.all_gather(array, ('z', 'x'), axis=0, tiled=True)  55.7 us
    ppermute x12, waiting for transfers between devices, step_z(): total = total + lax.ppermute(there, 'z', ring).astype(f32)  51.2 us
    dot_general x24, matrix products, product(): return jnp.dot(left, right, preferred_element_type=jnp.float32)  48.4 us
    ppermute x49, starting transfers between devices, swap(): return lax.ppermute(array, axis, SWAP)  43.1 us
    ppermute x9, starting transfers between devices, z_pieces(): lax.ppermute(array, 'z', [(i, (i + step) % nz) for i in range(nz)])  38 us
    pallas_call x6, Pallas kernels, run_small(): pl.pallas_call(body, out_shape=[jax.ShapeDtypeStruct(*out) for out in out...  32.7 us
  transfers between devices with their start and end apart: 78, of which 29 were waited for; matrix products, arithmetic and copies ran while one was open for 23% of the time, Pallas kernels for 8%

profile of v3, /device:TPU:0, one launch (start us, length us, event | category | flops | bytes accessed | tf_op | source)
XLA Modules:
  0.0 653.2 jit_solution(15920695912014046161)
XLA Ops:
  7.8 4.8 shard_map.203
  16.4 3.4 shard_map.204
  28.4 3.9 collective-permute-done.3
  33.9 9.0 %collective-permute-done.16 = bf16[128,1024]{1,0:T(8,128)(2,1)S(1)} collective-permute-done((bf16[128,1024]{1,0:T(8,128)(2,1)}, bf16[128,1024]{1,0:T(8,128)(2,1)S(1)}, u32[]{:S(2)}, u32[]{:S(2)}) %collective-permute-start.16) | collective-permute-done | bytes 262176 | tf_op jit(solution)/shard_map/ppermute | solution.py:638
  45.2 6.9 %collective-permute-done.17 = bf16[128,1024]{1,0:T(8,128)(2,1)S(1)} collective-permute-done((bf16[128,1024]{1,0:T(8,128)(2,1)S(1)}, bf16[128,1024]{1,0:T(8,128)(2,1)S(1)}, u32[]{:S(2)}, u32[]{:S(2)}) %collective-permute-start.17) | collective-permute-done | bytes 262176 | tf_op jit(solution)/shard_map/ppermute | solution.py:549
  52.2 4.5 collective-permute-done.19
  60.6 3.6 collective-permute-start.33
  69.2 3.7 collective-permute-start.4
  74.8 3.3 collective-permute-start.23
  80.5 7.9 %collective-permute-done.4 = bf16[128,1024]{1,0:T(8,128)(2,1)S(1)} collective-permute-done((bf16[128,1024]{1,0:T(8,128)(2,1)S(1)}, bf16[128,1024]{1,0:T(8,128)(2,1)S(1)}, u32[]{:S(2)}, u32[]{:S(2)}) %collective-permute-start.4) | collective-permute-done | bytes 262176 | tf_op jit(solution)/shard_map/ppermute | solution.py:638
  92.5 14.5 %collective-permute-done.23 = bf16[128,1024]{1,0:T(8,128)(2,1)S(1)} collective-permute-done((bf16[128,1024]{1,0:T(8,128)(2,1)S(1)}, bf16[128,1024]{1,0:T(8,128)(2,1)S(1)}, u32[]{:S(2)}, u32[]{:S(2)}) %collective-permute-start.23) | collective-permute-done | bytes 262176 | tf_op jit(solution)/shard_map/ppermute | solution.py:638
  107.1 16.2 %collective-permute-start.6 = (bf16[128,2048]{1,0:T(8,128)(2,1)S(1)}, bf16[128,2048]{1,0:T(8,128)(2,1)S(1)}, u32[]{:S(2)}, u32[]{:S(2)}) collective-permute-start(bf16[128,2048]{1,0:T(8,128)(2,1)S(1)} %copy-done.62), channel_id=1, source_target_pairs={{0,8},{8,16},{16,24},{24,0},{1,9},{9,17},{17,25},{25,1},{2,10},{10... | collective-permute-start | bytes 1572872 | tf_op jit(solution)/shard_map/ppermute | solution.py:638
  126.2 3.8 collective-permute-start.8
  134.3 4.2 collective-permute-done.26
  138.5 4.2 collective-permute-start.10
  144.9 5.3 collective-permute-done.6
  152.2 28.6 %collective-permute-done.8 = bf16[128,2048]{1,0:T(8,128)(2,1)S(1)} collective-permute-done((bf16[128,2048]{1,0:T(8,128)(2,1)S(1)}, bf16[128,2048]{1,0:T(8,128)(2,1)S(1)}, u32[]{:S(2)}, u32[]{:S(2)}) %collective-permute-start.8) | collective-permute-done | bytes 524320 | tf_op jit(solution)/shard_map/ppermute | solution.py:638
  184.5 19.4 %collective-permute-done.9 = bf16[128,2048]{1,0:T(8,128)(2,1)S(1)} collective-permute-done((bf16[128,2048]{1,0:T(8,128)(2,1)S(1)}, bf16[128,2048]{1,0:T(8,128)(2,1)S(1)}, u32[]{:S(2)}, u32[]{:S(2)}) %collective-permute-start.9) | collective-permute-done | bytes 524320 | tf_op jit(solution)/shard_map/ppermute | solution.py:549
  204.1 20.8 %collective-permute-done.11 = bf16[128,2048]{1,0:T(8,128)(2,1)S(1)} collective-permute-done((bf16[128,2048]{1,0:T(8,128)(2,1)S(1)}, bf16[128,2048]{1,0:T(8,128)(2,1)S(1)}, u32[]{:S(2)}, u32[]{:S(2)}) %collective-permute-start.11) | collective-permute-done | bytes 524320 | tf_op jit(solution)/shard_map/ppermute | solution.py:549
  228.7 4.8 shard_map.205
  262.2 55.7 %all-gather.2.cloned.1.call-done = bf16[1024,6144]{1,0:T(8,128)(2,1)} async-done(((bf16[128,6144]{1,0:T(8,128)(2,1)}), bf16[1024,6144]{1,0:T(8,128)(2,1)}) %all-gather.2.cloned.1.call-update) | async-done | bytes 12582928 | tf_op jit(solution)/shard_map/all_gather | solution.py:610
  320.2 3.8 fusion.11.project_ref
  324.0 5.2 shard_map.206
  333.8 3.3 fusion.28
  361.2 6.5 collective-permute-done.38.refs_2_
  377.9 7.3 %shard_map.207 = (bf16[256,1536]{1,0:T(8,128)(2,1)}, f32[4,128]{1,0:T(4,128)}) custom-call(f32[8]{0:T(128)} %fusion.131.scale_ref, bf16[256,1536]{1,0:T(8,128)(2,1)} %fusion.11.project_ref, s32[256,1]{1,0:T(8,128)} %copy.54.starts_ref, bf16[256,512]{1,0:T(8,128)(2,1)} %convolution_convert_fusion.3.grad_ref), custom_call_target="tpu_custom_call" | custom-call | tf_op jit(solution)/shard_map/pallas_call | solution.py:537
  390.3 16.1 %collective-permute-done.40.refs_5_ = bf16[256,1536]{1,0:T(8,128)(2,1)} collective-permute-done((bf16[256,1536]{1,0:T(8,128)(2,1)}, bf16[256,1536]{1,0:T(8,128)(2,1)}, u32[]{:S(2)}, u32[]{:S(2)}) %collective-permute-start.40) | collective-permute-done | bytes 786464 | tf_op jit(solution)/shard_map/ppermute | solution.py:549
  406.4 6.7 %shard_map.208 = bf16[1024,2048]{1,0:T(8,128)(2,1)} custom-call(bf16[256,1024]{1,0:T(8,128)(2,1)} %copy-done.42, bf16[256,2048]{1,0:T(8,128)(2,1)} %copy-done.15, bf16[256,1024]{1,0:T(8,128)(2,1)} %copy-done.61, bf16[256,2048]{1,0:T(8,128)(2,1)} %collective-permute-done.41.refs_3_, bf16[256,1536]{1,0:T(8,128)(2,1)} %pad_maximum_fusion.16.refs_4_, ...), custom_call_target="tpu_custom_call" | custom-call | tf_op jit(solution)/shard_map/pallas_call | solution.py:527
  413.0 4.0 fusion.53
  437.2 3.1 shard_map.210
  440.2 4.1 shard_map.209
  458.1 7.2 %shard_map.211 = (bf16[256,1536]{1,0:T(8,128)(2,1)}, f32[4,128]{1,0:T(4,128)}) custom-call(f32[8]{0:T(128)} %fusion.130.scale_ref, bf16[256,1536]{1,0:T(8,128)(2,1)} %fusion.8.project_ref, s32[256,1]{1,0:T(8,128)} %copy.54.starts_ref, bf16[256,512]{1,0:T(8,128)(2,1)} %convolution_convert_fusion.2.grad_ref), custom_call_target="tpu_custom_call" | custom-call | tf_op jit(solution)/shard_map/pallas_call | solution.py:537
  469.7 3.0 fusion.50
  476.2 6.9 %shard_map.214 = bf16[1024,2048]{1,0:T(8,128)(2,1)} custom-call(bf16[256,1024]{1,0:T(8,128)(2,1)} %add_convert_fusion.4.refs_0_, bf16[256,2048]{1,0:T(8,128)(2,1)} %copy-done.7, bf16[256,1024]{1,0:T(8,128)(2,1)} %collective-permute-done.32.refs_2_, bf16[256,2048]{1,0:T(8,128)(2,1)} %collective-permute-done.47.refs_3_, ...), custom_call_target="tpu_custom_call" | custom-call | tf_op jit(solution)/shard_map/pallas_call | solution.py:527
  488.0 5.6 collective-permute-done.58
  495.7 3.0 shard_map.213
  499.9 4.0 shard_map.212
  513.2 3.3 collective-permute-done.73
  519.2 3.4 collective-permute-done.74
  529.0 4.6 collective-permute-done.67
  534.8 13.7 %collective-permute-done.66 = bf16[128,1024]{1,0:T(8,128)(2,1)} collective-permute-done((bf16[128,1024]{1,0:T(8,128)(2,1)}, bf16[128,1024]{1,0:T(8,128)(2,1)}, u32[]{:S(2)}, u32[]{:S(2)}) %collective-permute-start.66) | collective-permute-done | bytes 262176 | tf_op jit(solution)/shard_map/ppermute | solution.py:627
  558.5 17.3 %collective-permute-done.69 = bf16[4,128,1024]{2,1,0:T(8,128)(2,1)S(1)} collective-permute-done((bf16[4,128,1024]{2,1,0:T(8,128)(2,1)}, bf16[4,128,1024]{2,1,0:T(8,128)(2,1)S(1)}, u32[]{:S(2)}, u32[]{:S(2)}) %collective-permute-start.69) | collective-permute-done | bytes 1048608 | tf_op jit(solution)/shard_map/ppermute | solution.py:549
  576.4 3.9 collective-permute-start.63
  580.3 6.4 collective-permute-done.55
  586.7 7.5 %collective-permute-start.61 = (bf16[128,1024]{1,0:T(8,128)(2,1)S(1)}, bf16[128,1024]{1,0:T(8,128)(2,1)S(1)}, u32[]{:S(2)}, u32[]{:S(2)}) collective-permute-start(bf16[128,1024]{1,0:T(8,128)(2,1)S(1)} %get-tuple-element.160), channel_id=1, source_target_pairs={{0,8},{8,16},{16,24},{24,0},{1,9},{9,17},{17,25},{25,1},{2,10},{10... | collective-permute-start | bytes 786440 | tf_op jit(solution)/shard_map/ppermute | solution.py:627
  595.2 4.4 collective-permute-start.71
  599.7 9.7 %collective-permute-done.62 = bf16[128,1024]{1,0:T(8,128)(2,1)S(1)} collective-permute-done((bf16[128,1024]{1,0:T(8,128)(2,1)S(1)}, bf16[128,1024]{1,0:T(8,128)(2,1)S(1)}, u32[]{:S(2)}, u32[]{:S(2)}) %collective-permute-start.62) | collective-permute-done | bytes 262176 | tf_op jit(solution)/shard_map/ppermute | solution.py:627
  612.0 16.8 %collective-permute-done.71 = bf16[128,1024]{1,0:T(8,128)(2,1)S(1)} collective-permute-done((bf16[128,1024]{1,0:T(8,128)(2,1)S(1)}, bf16[128,1024]{1,0:T(8,128)(2,1)S(1)}, u32[]{:S(2)}, u32[]{:S(2)}) %collective-permute-start.71) | collective-permute-done | bytes 262176 | tf_op jit(solution)/shard_map/ppermute | solution.py:627
  (609 shorter events, 227.2 us)
Async XLA Ops:
  7.2 310.7 %all-gather.2.cloned.1.call-start = ((), (), s32[]{:S(2)}) async-start(), calls=%async_computation.1 | async-start | bytes 14155776 | tf_op jit(solution)/shard_map/all_gather | solution.py:610
  22.7 20.3 %collective-permute-start.16 = (bf16[128,1024]{1,0:T(8,128)(2,1)}, bf16[128,1024]{1,0:T(8,128)(2,1)S(1)}, u32[]{:S(2)}, u32[]{:S(2)}) collective-permute-start(bf16[128,1024]{1,0:T(8,128)(2,1)} %get-tuple-element.59), channel_id=1, source_target_pairs={{0,16},{8,24},{16,0},{24,8},{1,17},{9,25},{17,1},{25,9},{2,18},{10... | collective-permute-start | bytes 786440 | tf_op jit(solution)/shard_map/ppermute | solution.py:638
  25.3 19.2 %collective-permute-start.18 = (bf16[128,1024]{1,0:T(8,128)(2,1)}, bf16[128,1024]{1,0:T(8,128)(2,1)S(1)}, u32[]{:S(2)}, u32[]{:S(2)}) collective-permute-start(bf16[128,1024]{1,0:T(8,128)(2,1)} %get-tuple-element.59), channel_id=1, source_target_pairs={{0,24},{8,0},{16,8},{24,16},{1,25},{9,1},{17,9},{25,17},{2,26},{10... | collective-permute-start | bytes 786440 | tf_op jit(solution)/shard_map/ppermute | solution.py:638
  26.6 18.4 %collective-permute-start.14 = (bf16[128,1024]{1,0:T(8,128)(2,1)}, bf16[128,1024]{1,0:T(8,128)(2,1)S(1)}, u32[]{:S(2)}, u32[]{:S(2)}) collective-permute-start(bf16[128,1024]{1,0:T(8,128)(2,1)} %get-tuple-element.59), channel_id=1, source_target_pairs={{0,4},{4,0},{1,5},{5,1},{2,6},{6,2},{3,7},{7,3},{8,12},{12,8},{9,1... | collective-permute-start | bytes 786440 | tf_op jit(solution)/shard_map/ppermute | solution.py:549
  56.8 577.9 %reduce-scatter.2.cloned.1.call-start = ((), (), s32[]{:S(2)}) async-start(), calls=%async_computation.2 | async-start | bytes 4718592 | tf_op jit(solution)/shard_map/reduce_scatter | solution.py:613
  66.2 169.6 %collective-permute-start.34 = (bf16[128,1024]{1,0:T(8,128)(2,1)}, bf16[128,1024]{1,0:T(8,128)(2,1)}, u32[]{:S(2)}, u32[]{:S(2)}) collective-permute-start(bf16[128,1024]{1,0:T(8,128)(2,1)} %collective-permute-done.33), channel_id=1, source_target_pairs={{0,2},{2,0},{1,3},{3,1},{4,6},{6,4},{5,7},{7,5},{8,10},{10,8},{9,1... | collective-permute-start | bytes 786440 | tf_op jit(solution)/shard_map/ppermute | solution.py:549
  69.2 19.2 %collective-permute-start.4 = (bf16[128,1024]{1,0:T(8,128)(2,1)S(1)}, bf16[128,1024]{1,0:T(8,128)(2,1)S(1)}, u32[]{:S(2)}, u32[]{:S(2)}) collective-permute-start(bf16[128,1024]{1,0:T(8,128)(2,1)S(1)} %copy-done.73), channel_id=1, source_target_pairs={{0,8},{8,16},{16,24},{24,0},{1,9},{9,17},{17,25},{25,1},{2,10},{10... | collective-permute-start | bytes 786440 | tf_op jit(solution)/shard_map/ppermute | solution.py:638
  73.2 17.3 %collective-permute-start.21 = (bf16[128,1024]{1,0:T(8,128)(2,1)S(1)}, bf16[128,1024]{1,0:T(8,128)(2,1)S(1)}, u32[]{:S(2)}, u32[]{:S(2)}) collective-permute-start(bf16[128,1024]{1,0:T(8,128)(2,1)S(1)} %copy-done.73), channel_id=1, source_target_pairs={{0,4},{4,0},{1,5},{5,1},{2,6},{6,2},{3,7},{7,3},{8,12},{12,8},{9,1... | collective-permute-start | bytes 786440 | tf_op jit(solution)/shard_map/ppermute | solution.py:549
  74.8 32.3 %collective-permute-start.23 = (bf16[128,1024]{1,0:T(8,128)(2,1)S(1)}, bf16[128,1024]{1,0:T(8,128)(2,1)S(1)}, u32[]{:S(2)}, u32[]{:S(2)}) collective-permute-start(bf16[128,1024]{1,0:T(8,128)(2,1)S(1)} %copy-done.73), channel_id=1, source_target_pairs={{0,16},{8,24},{16,0},{24,8},{1,17},{9,25},{17,1},{25,9},{2,18},{10... | collective-permute-start | bytes 786440 | tf_op jit(solution)/shard_map/ppermute | solution.py:638
  78.0 48.2 %collective-permute-start.25 = (bf16[128,1024]{1,0:T(8,128)(2,1)S(1)}, bf16[128,1024]{1,0:T(8,128)(2,1)S(1)}, u32[]{:S(2)}, u32[]{:S(2)}) collective-permute-start(bf16[128,1024]{1,0:T(8,128)(2,1)S(1)} %copy-done.73), channel_id=1, source_target_pairs={{0,24},{8,0},{16,8},{24,16},{1,25},{9,1},{17,9},{25,17},{2,26},{10... | collective-permute-start | bytes 786440 | tf_op jit(solution)/shard_map/ppermute | solution.py:638
  88.4 55.0 %collective-permute-start.5 = (bf16[128,2048]{1,0:T(8,128)(2,1)S(1)}, bf16[128,2048]{1,0:T(8,128)(2,1)S(1)}, u32[]{:S(2)}, u32[]{:S(2)}) collective-permute-start(bf16[128,2048]{1,0:T(8,128)(2,1)S(1)} %copy-done.62), channel_id=1, source_target_pairs={{0,4},{4,0},{1,5},{5,1},{2,6},{6,2},{3,7},{7,3},{8,12},{12,8},{9,1... | collective-permute-start | bytes 1572872 | tf_op jit(solution)/shard_map/ppermute | solution.py:549
  90.5 32.8 %collective-permute-start.22 = (bf16[128,1024]{1,0:T(8,128)(2,1)S(1)}, bf16[128,1024]{1,0:T(8,128)(2,1)S(1)}, u32[]{:S(2)}, u32[]{:S(2)}) collective-permute-start(bf16[128,1024]{1,0:T(8,128)(2,1)S(1)} %collective-permute-done.4), channel_id=1, source_target_pairs={{0,4},{4,0},{1,5},{5,1},{2,6},{6,2},{3,7},{7,3},{8,12},{12,8},{9,1... | collective-permute-start | bytes 786440 | tf_op jit(solution)/shard_map/ppermute | solution.py:549
  107.1 43.1 %collective-permute-start.6 = (bf16[128,2048]{1,0:T(8,128)(2,1)S(1)}, bf16[128,2048]{1,0:T(8,128)(2,1)S(1)}, u32[]{:S(2)}, u32[]{:S(2)}) collective-permute-start(bf16[128,2048]{1,0:T(8,128)(2,1)S(1)} %copy-done.62), channel_id=1, source_target_pairs={{0,8},{8,16},{16,24},{24,0},{1,9},{9,17},{17,25},{25,1},{2,10},{10... | collective-permute-start | bytes 1572872 | tf_op jit(solution)/shard_map/ppermute | solution.py:638
  126.2 54.5 %collective-permute-start.8 = (bf16[128,2048]{1,0:T(8,128)(2,1)S(1)}, bf16[128,2048]{1,0:T(8,128)(2,1)S(1)}, u32[]{:S(2)}, u32[]{:S(2)}) collective-permute-start(bf16[128,2048]{1,0:T(8,128)(2,1)S(1)} %copy-done.62), channel_id=1, source_target_pairs={{0,16},{8,24},{16,0},{24,8},{1,17},{9,25},{17,1},{25,9},{2,18},{10... | collective-permute-start | bytes 1572872 | tf_op jit(solution)/shard_map/ppermute | solution.py:638
  138.5 43.9 %collective-permute-start.10 = (bf16[128,2048]{1,0:T(8,128)(2,1)S(1)}, bf16[128,2048]{1,0:T(8,128)(2,1)S(1)}, u32[]{:S(2)}, u32[]{:S(2)}) collective-permute-start(bf16[128,2048]{1,0:T(8,128)(2,1)S(1)} %copy-done.62), channel_id=1, source_target_pairs={{0,24},{8,0},{16,8},{24,16},{1,25},{9,1},{17,9},{25,17},{2,26},{10... | collective-permute-start | bytes 1572872 | tf_op jit(solution)/shard_map/ppermute | solution.py:638
  143.4 95.7 %collective-permute-start.20 = (bf16[1024,1024]{1,0:T(8,128)(2,1)S(1)}, bf16[1024,1024]{1,0:T(8,128)(2,1)}, u32[]{:S(2)}, u32[]{:S(2)}) collective-permute-start(bf16[1024,1024]{1,0:T(8,128)(2,1)S(1)} %bitcast.282), channel_id=1, source_target_pairs={{0,1},{1,0},{2,3},{3,2},{4,5},{5,4},{6,7},{7,6},{8,9},{9,8},{10,11... | collective-permute-start | bytes 6291464 | tf_op jit(solution)/shard_map/ppermute | solution.py:549
  150.2 33.2 %collective-permute-start.7 = (bf16[128,2048]{1,0:T(8,128)(2,1)S(1)}, bf16[128,2048]{1,0:T(8,128)(2,1)S(1)}, u32[]{:S(2)}, u32[]{:S(2)}) collective-permute-start(bf16[128,2048]{1,0:T(8,128)(2,1)S(1)} %collective-permute-done.6), channel_id=1, source_target_pairs={{0,4},{4,0},{1,5},{5,1},{2,6},{6,2},{3,7},{7,3},{8,12},{12,8},{9,1... | collective-permute-start | bytes 1572872 | tf_op jit(solution)/shard_map/ppermute | solution.py:549
  180.8 58.3 %collective-permute-start.27 = (bf16[1024,1024]{1,0:T(8,128)(2,1)}, bf16[1024,1024]{1,0:T(8,128)(2,1)}, u32[]{:S(2)}, u32[]{:S(2)}) collective-permute-start(bf16[1024,1024]{1,0:T(8,128)(2,1)} %bitcast.34), channel_id=1, source_target_pairs={{0,1},{1,0},{2,3},{3,2},{4,5},{5,4},{6,7},{7,6},{8,9},{9,8},{10,11... | collective-permute-start | bytes 6291464 | tf_op jit(solution)/shard_map/ppermute | solution.py:549
  182.4 21.6 %collective-permute-start.9 = (bf16[128,2048]{1,0:T(8,128)(2,1)S(1)}, bf16[128,2048]{1,0:T(8,128)(2,1)S(1)}, u32[]{:S(2)}, u32[]{:S(2)}) collective-permute-start(bf16[128,2048]{1,0:T(8,128)(2,1)S(1)} %collective-permute-done.8), channel_id=1, source_target_pairs={{0,4},{4,0},{1,5},{5,1},{2,6},{6,2},{3,7},{7,3},{8,12},{12,8},{9,1... | collective-permute-start | bytes 1572872 | tf_op jit(solution)/shard_map/ppermute | solution.py:549
  183.4 41.4 %collective-permute-start.11 = (bf16[128,2048]{1,0:T(8,128)(2,1)S(1)}, bf16[128,2048]{1,0:T(8,128)(2,1)S(1)}, u32[]{:S(2)}, u32[]{:S(2)}) collective-permute-start(bf16[128,2048]{1,0:T(8,128)(2,1)S(1)} %collective-permute-done.10), channel_id=1, source_target_pairs={{0,4},{4,0},{1,5},{5,1},{2,6},{6,2},{3,7},{7,3},{8,12},{12,8},{9,1... | collective-permute-start | bytes 1572872 | tf_op jit(solution)/shard_map/ppermute | solution.py:549
  256.7 81.5 %collective-permute-start.31 = (bf16[256,1536]{1,0:T(8,128)(2,1)}, bf16[256,1536]{1,0:T(8,128)(2,1)}, u32[]{:S(2)}, u32[]{:S(2)}) collective-permute-start(bf16[256,1536]{1,0:T(8,128)(2,1)} %pad_maximum_fusion.13.refs_0_), channel_id=1, source_target_pairs={{0,1},{1,0},{2,3},{3,2},{4,5},{5,4},{6,7},{7,6},{8,9},{9,8},{10,11... | collective-permute-start | bytes 2359304 | tf_op jit(solution)/shard_map/ppermute | solution.py:549
  256.7 81.5 %collective-permute-start.32 = (bf16[256,1024]{1,0:T(8,128)(2,1)}, bf16[256,1024]{1,0:T(8,128)(2,1)}, u32[]{:S(2)}, u32[]{:S(2)}) collective-permute-start(bf16[256,1024]{1,0:T(8,128)(2,1)} %add_convert_fusion.4.refs_0_), channel_id=1, source_target_pairs={{0,1},{1,0},{2,3},{3,2},{4,5},{5,4},{6,7},{7,6},{8,9},{9,8},{10,11... | collective-permute-start | bytes 1572872 | tf_op jit(solution)/shard_map/ppermute | solution.py:549
  259.9 209.6 %collective-permute-start.47 = (bf16[256,2048]{1,0:T(8,128)(2,1)}, bf16[256,2048]{1,0:T(8,128)(2,1)}, u32[]{:S(2)}, u32[]{:S(2)}) collective-permute-start(bf16[256,2048]{1,0:T(8,128)(2,1)} %pad_maximum_fusion.8), channel_id=1, source_target_pairs={{0,1},{1,0},{2,3},{3,2},{4,5},{5,4},{6,7},{7,6},{8,9},{9,8},{10,11... | collective-permute-start | bytes 3145736 | tf_op jit(solution)/shard_map/ppermute | solution.py:549
  332.0 29.2 %collective-permute-start.37 = (bf16[256,1536]{1,0:T(8,128)(2,1)}, bf16[256,1536]{1,0:T(8,128)(2,1)}, u32[]{:S(2)}, u32[]{:S(2)}) collective-permute-start(bf16[256,1536]{1,0:T(8,128)(2,1)} %pad_maximum_fusion.14.refs_0_), channel_id=1, source_target_pairs={{0,1},{1,0},{2,3},{3,2},{4,5},{5,4},{6,7},{7,6},{8,9},{9,8},{10,11... | collective-permute-start | bytes 2359304 | tf_op jit(solution)/shard_map/ppermute | solution.py:549
  352.8 14.9 %collective-permute-start.38 = (bf16[256,1024]{1,0:T(8,128)(2,1)S(1)}, bf16[256,1024]{1,0:T(8,128)(2,1)S(1)}, u32[]{:S(2)}, u32[]{:S(2)}) collective-permute-start(bf16[256,1024]{1,0:T(8,128)(2,1)S(1)} %add_convert_fusion.2.refs_0_), channel_id=1, source_target_pairs={{0,1},{1,0},{2,3},{3,2},{4,5},{5,4},{6,7},{7,6},{8,9},{9,8},{10,11... | collective-permute-start | bytes 1572872 | tf_op jit(solution)/shard_map/ppermute | solution.py:549
  355.8 34.5 %collective-permute-start.41 = (bf16[256,2048]{1,0:T(8,128)(2,1)}, bf16[256,2048]{1,0:T(8,128)(2,1)}, u32[]{:S(2)}, u32[]{:S(2)}) collective-permute-start(bf16[256,2048]{1,0:T(8,128)(2,1)} %pad_maximum_fusion.7), channel_id=1, source_target_pairs={{0,1},{1,0},{2,3},{3,2},{4,5},{5,4},{6,7},{7,6},{8,9},{9,8},{10,11... | collective-permute-start | bytes 3145736 | tf_op jit(solution)/shard_map/ppermute | solution.py:549
  359.0 13.4 %collective-permute-start.50 = (bf16[256,1024]{1,0:T(8,128)(2,1)S(1)}, bf16[256,1024]{1,0:T(8,128)(2,1)S(1)}, u32[]{:S(2)}, u32[]{:S(2)}) collective-permute-start(bf16[256,1024]{1,0:T(8,128)(2,1)S(1)} %fusion.58), channel_id=1, source_target_pairs={{0,2},{2,0},{1,3},{3,1},{4,6},{6,4},{5,7},{7,5},{8,10},{10,8},{9,1... | collective-permute-start | bytes 1572872 | tf_op jit(solution)/shard_map/ppermute | solution.py:549
  371.2 35.2 %collective-permute-start.40 = (bf16[256,1536]{1,0:T(8,128)(2,1)}, bf16[256,1536]{1,0:T(8,128)(2,1)}, u32[]{:S(2)}, u32[]{:S(2)}) collective-permute-start(bf16[256,1536]{1,0:T(8,128)(2,1)} %pad_maximum_fusion.15), channel_id=1, source_target_pairs={{0,1},{1,0},{2,3},{3,2},{4,5},{5,4},{6,7},{7,6},{8,9},{9,8},{10,11... | collective-permute-start | bytes 2359304 | tf_op jit(solution)/shard_map/ppermute | solution.py:549
  418.8 18.4 %collective-permute-start.44 = (bf16[256,1280]{1,0:T(8,128)(2,1)}, bf16[256,1280]{1,0:T(8,128)(2,1)}, u32[]{:S(2)}, u32[]{:S(2)}) collective-permute-start(bf16[256,1280]{1,0:T(8,128)(2,1)} %pad_maximum_fusion.25), channel_id=1, source_target_pairs={{0,1},{1,0},{2,3},{3,2},{4,5},{5,4},{6,7},{7,6},{8,9},{9,8},{10,11... | collective-permute-start | bytes 1966088 | tf_op jit(solution)/shard_map/ppermute | solution.py:549
  449.6 20.0 %collective-permute-start.46 = (bf16[256,1536]{1,0:T(8,128)(2,1)}, bf16[256,1536]{1,0:T(8,128)(2,1)}, u32[]{:S(2)}, u32[]{:S(2)}) collective-permute-start(bf16[256,1536]{1,0:T(8,128)(2,1)} %pad_maximum_fusion.17), channel_id=1, source_target_pairs={{0,1},{1,0},{2,3},{3,2},{4,5},{5,4},{6,7},{7,6},{8,9},{9,8},{10,11... | collective-permute-start | bytes 2359304 | tf_op jit(solution)/shard_map/ppermute | solution.py:549
  467.7 49.8 %collective-permute-start.52 = (bf16[4,128,1024]{2,1,0:T(8,128)(2,1)}, bf16[4,128,1024]{2,1,0:T(8,128)(2,1)}, u32[]{:S(2)}, u32[]{:S(2)}) collective-permute-start(bf16[4,128,1024]{2,1,0:T(8,128)(2,1)} %dynamic-slice_bitcast_fusion.2), channel_id=1, source_target_pairs={{0,4},{4,0},{1,5},{5,1},{2,6},{6,2},{3,7},{7,3},{8,12},{12,8},{9,1... | collective-permute-start | bytes 3145736 | tf_op jit(solution)/shard_map/ppermute | solution.py:549
  474.5 20.5 %collective-permute-start.48 = (bf16[256,1280]{1,0:T(8,128)(2,1)}, bf16[256,1280]{1,0:T(8,128)(2,1)S(1)}, u32[]{:S(2)}, u32[]{:S(2)}) collective-permute-start(bf16[256,1280]{1,0:T(8,128)(2,1)} %pad_maximum_fusion.28), channel_id=1, source_target_pairs={{0,1},{1,0},{2,3},{3,2},{4,5},{5,4},{6,7},{7,6},{8,9},{9,8},{10,11... | collective-permute-start | bytes 1966088 | tf_op jit(solution)/shard_map/ppermute | solution.py:549
  506.1 44.6 %collective-permute-start.49 = (bf16[4,128,1024]{2,1,0:T(8,128)(2,1)}, bf16[4,128,1024]{2,1,0:T(8,128)(2,1)}, u32[]{:S(2)}, u32[]{:S(2)}) collective-permute-start(bf16[4,128,1024]{2,1,0:T(8,128)(2,1)} %fusion.80), channel_id=1, source_target_pairs={{0,4},{4,0},{1,5},{5,1},{2,6},{6,2},{3,7},{7,3},{8,12},{12,8},{9,1... | collective-permute-start | bytes 3145736 | tf_op jit(solution)/shard_map/ppermute | solution.py:549
  510.9 44.1 %collective-permute-start.60 = (bf16[4,128,1024]{2,1,0:T(8,128)(2,1)}, bf16[4,128,1024]{2,1,0:T(8,128)(2,1)}, u32[]{:S(2)}, u32[]{:S(2)}) collective-permute-start(bf16[4,128,1024]{2,1,0:T(8,128)(2,1)} %dynamic-slice_bitcast_fusion.1), channel_id=1, source_target_pairs={{0,4},{4,0},{1,5},{5,1},{2,6},{6,2},{3,7},{7,3},{8,12},{12,8},{9,1... | collective-permute-start | bytes 3145736 | tf_op jit(solution)/shard_map/ppermute | solution.py:549
  525.1 23.5 %collective-permute-start.66 = (bf16[128,1024]{1,0:T(8,128)(2,1)}, bf16[128,1024]{1,0:T(8,128)(2,1)}, u32[]{:S(2)}, u32[]{:S(2)}) collective-permute-start(bf16[128,1024]{1,0:T(8,128)(2,1)} %get-tuple-element.165), channel_id=1, source_target_pairs={{0,16},{8,24},{16,0},{24,8},{1,17},{9,25},{17,1},{25,9},{2,18},{10... | collective-permute-start | bytes 786440 | tf_op jit(solution)/shard_map/ppermute | solution.py:627
  525.1 23.5 %collective-permute-start.65 = (bf16[128,1024]{1,0:T(8,128)(2,1)}, bf16[128,1024]{1,0:T(8,128)(2,1)}, u32[]{:S(2)}, u32[]{:S(2)}) collective-permute-start(bf16[128,1024]{1,0:T(8,128)(2,1)} %get-tuple-element.163), channel_id=1, source_target_pairs={{0,8},{8,16},{16,24},{24,0},{1,9},{9,17},{17,25},{25,1},{2,10},{10... | collective-permute-start | bytes 786440 | tf_op jit(solution)/shard_map/ppermute | solution.py:627
  533.6 42.1 %collective-permute-start.69 = (bf16[4,128,1024]{2,1,0:T(8,128)(2,1)}, bf16[4,128,1024]{2,1,0:T(8,128)(2,1)S(1)}, u32[]{:S(2)}, u32[]{:S(2)}) collective-permute-start(bf16[4,128,1024]{2,1,0:T(8,128)(2,1)} %dynamic-slice_bitcast_fusion), channel_id=1, source_target_pairs={{0,4},{4,0},{1,5},{5,1},{2,6},{6,2},{3,7},{7,3},{8,12},{12,8},{9,1... | collective-permute-start | bytes 3145736 | tf_op jit(solution)/shard_map/ppermute | solution.py:549
  552.4 42.0 %collective-permute-start.53 = (bf16[128,1024]{1,0:T(8,128)(2,1)S(1)}, bf16[128,1024]{1,0:T(8,128)(2,1)S(1)}, u32[]{:S(2)}, u32[]{:S(2)}) collective-permute-start(bf16[128,1024]{1,0:T(8,128)(2,1)S(1)} %copy-done.72), channel_id=1, source_target_pairs={{0,0},{1,2},{2,1},{3,3},{4,4},{5,6},{6,5},{7,7},{8,8},{9,10},{10,9... | collective-permute-start | bytes 786440 | tf_op jit(solution)/shard_map/ppermute | solution.py:553
  553.2 76.5 %collective-permute-start.54 = (f32[128,1024]{1,0:T(8,128)S(1)}, f32[128,1024]{1,0:T(8,128)S(1)}, u32[]{:S(2)}, u32[]{:S(2)}) collective-permute-start(f32[128,1024]{1,0:T(8,128)S(1)} %constant_dynamic-slice_fusion.3), channel_id=1, source_target_pairs={{0,0},{1,2},{2,1},{3,3},{4,4},{5,6},{6,5},{7,7},{8,8},{9,10},{10,9... | collective-permute-start | bytes 1572872 | tf_op jit(solution)/shard_map/ppermute | solution.py:553
  554.1 22.4 %collective-permute-start.57 = (bf16[128,1024]{1,0:T(8,128)(2,1)S(1)}, bf16[128,1024]{1,0:T(8,128)(2,1)S(1)}, u32[]{:S(2)}, u32[]{:S(2)}) collective-permute-start(bf16[128,1024]{1,0:T(8,128)(2,1)S(1)} %get-tuple-element.158), channel_id=1, source_target_pairs={{0,24},{8,0},{16,8},{24,16},{1,25},{9,1},{17,9},{25,17},{2,26},{10... | collective-permute-start | bytes 786440 | tf_op jit(solution)/shard_map/ppermute | solution.py:627
  555.0 25.3 %collective-permute-start.56 = (bf16[128,1024]{1,0:T(8,128)(2,1)S(1)}, bf16[128,1024]{1,0:T(8,128)(2,1)S(1)}, u32[]{:S(2)}, u32[]{:S(2)}) collective-permute-start(bf16[128,1024]{1,0:T(8,128)(2,1)S(1)} %get-tuple-element.159), channel_id=1, source_target_pairs={{0,16},{8,24},{16,0},{24,8},{1,17},{9,25},{17,1},{25,9},{2,18},{10... | collective-permute-start | bytes 786440 | tf_op jit(solution)/shard_map/ppermute | solution.py:627
  576.4 18.8 %collective-permute-start.63 = (bf16[128,1024]{1,0:T(8,128)(2,1)S(1)}, bf16[128,1024]{1,0:T(8,128)(2,1)S(1)}, u32[]{:S(2)}, u32[]{:S(2)}) collective-permute-start(bf16[128,1024]{1,0:T(8,128)(2,1)S(1)} %get-tuple-element.161), channel_id=1, source_target_pairs={{0,24},{8,0},{16,8},{24,16},{1,25},{9,1},{17,9},{25,17},{2,26},{10... | collective-permute-start | bytes 786440 | tf_op jit(solution)/shard_map/ppermute | solution.py:627
  580.3 29.0 %collective-permute-start.62 = (bf16[128,1024]{1,0:T(8,128)(2,1)S(1)}, bf16[128,1024]{1,0:T(8,128)(2,1)S(1)}, u32[]{:S(2)}, u32[]{:S(2)}) collective-permute-start(bf16[128,1024]{1,0:T(8,128)(2,1)S(1)} %get-tuple-element.162), channel_id=1, source_target_pairs={{0,16},{8,24},{16,0},{24,8},{1,17},{9,25},{17,1},{25,9},{2,18},{10... | collective-permute-start | bytes 786440 | tf_op jit(solution)/shard_map/ppermute | solution.py:627
  586.7 24.9 %collective-permute-start.61 = (bf16[128,1024]{1,0:T(8,128)(2,1)S(1)}, bf16[128,1024]{1,0:T(8,128)(2,1)S(1)}, u32[]{:S(2)}, u32[]{:S(2)}) collective-permute-start(bf16[128,1024]{1,0:T(8,128)(2,1)S(1)} %get-tuple-element.160), channel_id=1, source_target_pairs={{0,8},{8,16},{16,24},{24,0},{1,9},{9,17},{17,25},{25,1},{2,10},{10... | collective-permute-start | bytes 786440 | tf_op jit(solution)/shard_map/ppermute | solution.py:627
  594.4 17.5 %collective-permute-start.72 = (bf16[128,1024]{1,0:T(8,128)(2,1)S(1)}, bf16[128,1024]{1,0:T(8,128)(2,1)S(1)}, u32[]{:S(2)}, u32[]{:S(2)}) collective-permute-start(bf16[128,1024]{1,0:T(8,128)(2,1)S(1)} %get-tuple-element.155), channel_id=1, source_target_pairs={{0,24},{8,0},{16,8},{24,16},{1,25},{9,1},{17,9},{25,17},{2,26},{10... | collective-permute-start | bytes 786440 | tf_op jit(solution)/shard_map/ppermute | solution.py:627
  595.2 33.5 %collective-permute-start.71 = (bf16[128,1024]{1,0:T(8,128)(2,1)S(1)}, bf16[128,1024]{1,0:T(8,128)(2,1)S(1)}, u32[]{:S(2)}, u32[]{:S(2)}) collective-permute-start(bf16[128,1024]{1,0:T(8,128)(2,1)S(1)} %get-tuple-element.156), channel_id=1, source_target_pairs={{0,16},{8,24},{16,0},{24,8},{1,17},{9,25},{17,1},{25,9},{2,18},{10... | collective-permute-start | bytes 786440 | tf_op jit(solution)/shard_map/ppermute | solution.py:627
  609.3 19.4 %collective-permute-start.70 = (bf16[128,1024]{1,0:T(8,128)(2,1)S(1)}, bf16[128,1024]{1,0:T(8,128)(2,1)S(1)}, u32[]{:S(2)}, u32[]{:S(2)}) collective-permute-start(bf16[128,1024]{1,0:T(8,128)(2,1)S(1)} %get-tuple-element.154), channel_id=1, source_target_pairs={{0,8},{8,16},{16,24},{24,0},{1,9},{9,17},{17,25},{25,1},{2,10},{10... | collective-permute-start | bytes 786440 | tf_op jit(solution)/shard_map/ppermute | solution.py:627
  611.9 17.9 %collective-permute-start.64 = (bf16[64,1792]{1,0:T(8,128)(2,1)S(1)}, bf16[64,1792]{1,0:T(8,128)(2,1)S(1)}, u32[]{:S(2)}, u32[]{:S(2)}) collective-permute-start(bf16[64,1792]{1,0:T(8,128)(2,1)S(1)} %fusion.124), channel_id=1, source_target_pairs={{0,2},{2,0},{1,3},{3,1},{4,6},{6,4},{5,7},{7,5},{8,10},{10,8},{9,1... | collective-permute-start | bytes 688136 | tf_op jit(solution)/shard_map/ppermute | solution.py:549
  (120 other events, 1000.8 us)
Sparse Core Ops, SparseCore 0:
  56.9 260.9 all-gather.1
  419.2 96.9 reduce-scatter.1

commit v4 on v3

--- a/solution.py
+++ b/solution.py
@@ -509,6 +509,40 @@
             downs[layer][:, part * width : part * width + width] = down_ref[layer, rows, :]
 
 
+def finish_rows(place_ref, *refs):
+    core, near = place_ref[0], place_ref[1]
+    outs = refs[-4:]
+    for layer in range(len(refs[:-4]) // 3):
+        at_ref, ff_ref, there_ref = refs[3 * layer : 3 * layer + 3]
+        qkv_ref, out_ref, up_ref, down_ref = (out.at[layer] for out in outs)
+        shard, half = out_ref.shape
+        span = qkv_ref.shape[1] // 2
+        rows = pl.ds(pl.multiple_of(core * shard, shard), shard)
+        out_ref[:, : half // 2] = at_ref[:shard, span:]
+        out_ref[:, half // 2 :] = at_ref[shard:, span:]
+        for side in range(2):
+            part = near if side == 0 else 1 - near
+            first = pl.multiple_of(2 * half + half * part, half)
+            down_ref[2 * shard * side : 2 * shard * (side + 1), :] = ff_ref[:, pl.ds(first, half)]
+        own = at_ref[rows, :span]
+        other = there_ref[:, :span].astype(jnp.float32)
+        even = jnp.where(core == 0, own, other)
+        odd = jnp.where(core == 0, other, own)
+        for at in range(0, span, HD):
+            both = jnp.concatenate([even[:, at : at + HD], odd[:, at : at + HD]], axis=1)
+            qkv_ref[:, 2 * at : 2 * at + 2 * HD] = both
+        blocks = half // 128
+        for part in range(2):
+            side = near if part == 0 else 1 - near
+            for block in range(blocks):
+                at = half * part + 128 * block
+                to = block * 512 + side * 128
+                mine = pl.ds(pl.multiple_of(to + core * 256, 128), 128)
+                up_ref[:, mine] = ff_ref[rows, at : at + 128]
+                theirs = pl.ds(pl.multiple_of(to + (1 - core) * 256, 128), 128)
+                up_ref[:, theirs] = there_ref[:, span + at : span + at + 128].astype(jnp.float32)
+
+
 def term_product(lefts, lefts_there, rights, parts, shape):
     count = len(lefts)
 
@@ -658,14 +692,13 @@
         (own, swap(there, "c"), out_weight, fc2_weight),
         [((2 * shard, columns), bf16) for columns in (2 * width, width, width, 6 * width)],
     )
+    late = gather(packed[3])
     got = []
     for unit in (packed[1], packed[2], packed[0]):
         if got:
             unit, got[-1][1] = tie(unit, got[-1][1])
         got.append(z_pieces(unit))
     got = [join(pieces) for pieces in got]
-    late, got[0] = tie(packed[3], got[0])
-    late = gather(late)
     up_there, down_there = swap(got[0], "y"), swap(got[1], "y")
     late_parts = [late[:, width * part : width * (part + 1)] for part in range(2, 6)]
     ups = [(got[0], up_there), late_parts[:2]]
@@ -733,7 +766,9 @@
         near, far = mixed_low[:, :half_units], mixed_low[:, half_units:]
         hidden = middle + both_cores(product(near, down_mat[0]) + product(far, down_mat[1]))
         attention_in = jnp.concatenate([a_low, scaled], axis=1)
-        mixed_there = swap(jnp.concatenate([far, near], axis=1), "y")
+        mixed_there = jnp.concatenate([far, near], axis=1)
+        if which == 1:
+            mixed_there = swap(mixed_there, "y")
         ins_there = (swap(attention_in, "y"), swap(b_low, "y"), mixed_there)
         kept.append(
             (
@@ -755,6 +790,10 @@
             norm_a, inv_a, project, scale_here, norm_z, inv_z, norm_b, inv_b, pre_act, below, norm_m, inv_m, gain_m,
             attention_in, b_low, mixed_low, ins_there,
         ) = kept[which]
+        attention_there, b_there, mixed_there = ins_there
+        if which == 0:
+            grad_hidden, mixed_there = tie(grad_hidden, mixed_there)
+            mixed_there = swap(mixed_there, "y")
         final_low = grad_hidden.astype(bf16)
         grad_mixed = jnp.concatenate([product(final_low, part.T) for part in down_mat], axis=1)
         mid_gain_grad = jnp.sum(grad_mixed * norm_m, axis=0)
@@ -765,7 +804,6 @@
         grad_act = inv_m * (scaled_grad - sums[0][:, None] - norm_m * sums[1][:, None])
         slope = below + pre_act * jnp.exp(-0.5 * pre_act * pre_act) * (1.0 / math.sqrt(2 * math.pi))
         grad_pre = (grad_act * slope).astype(bf16)
-        attention_there, b_there, mixed_there = ins_there
         if which == 1:
             grad_pre, attention_there, b_there = tie(grad_pre, attention_there, b_there)
         else:
@@ -863,34 +901,20 @@
     vector = vector + swap(vector, "x")
     vector, ff_term = tie(vector, ff_term)
     up_held, down_held = step_x(ff_term[:, :width]), step_x(ff_term[:, width:])
-    for bit in (1, 2):
-        vector = vector + lax.ppermute(vector, "z", [(i, i ^ bit) for i in range(nz)])
+    vector = sum(z_pieces(vector))
     at_held = step_x(attention_term(at_there))
     at_held, output, grad_hidden = tie(at_held, output, grad_hidden)
     pending[0] = jnp.concatenate([step_z(up_held), step_z(down_held)], axis=1)
     at_rows = step_z(at_held)
-    matrix_grads = []
+    finals = []
     for at_rows, ff_rows in ((at_rows, pending[0]), (at_rows_last, pending[1])):
-        grad_out = at_rows[:, wide:].reshape(2, shard, half // 2)
-        grad_out = jnp.concatenate([grad_out[0], grad_out[1]], axis=1)
-        down_near, down_far = ff_rows[:, width : width + half], ff_rows[:, width + half :]
-        grad_down = jnp.concatenate(
-            [jnp.where(iy == 0, down_near, down_far), jnp.where(iy == 0, down_far, down_near)], axis=0
-        )
-        mixed_rows = jnp.concatenate([at_rows[:, :wide], ff_rows[:, :width]], axis=1)
-        mixed_rows = mixed_rows.reshape(2, shard, -1)
-        own = pick(mixed_rows, ic, 0)
-        other = swap(pick(mixed_rows, 1 - ic, 0).astype(bf16), "c").astype(f32)
-        columns = cores(own[None], other[None])
-        grad_qkv = columns[:, :, :wide].reshape(2, shard, wide // HD, HD)
-        grad_qkv = grad_qkv.transpose(1, 2, 0, 3).reshape(shard, 2 * wide)
-        near, far = columns[:, :, wide : wide + half], columns[:, :, wide + half :]
-        grad_up = jnp.stack(
-            [jnp.where(iy == 0, near, far), jnp.where(iy == 0, far, near)], axis=2
-        ).reshape(2, shard, 2, chips // 2, block)
-        grad_up = grad_up.transpose(1, 3, 0, 2, 4).reshape(shard, 2 * width)
-        matrix_grads.append((grad_qkv, grad_out, grad_up, grad_down))
-
+        send = jnp.concatenate([at_rows[:, :wide], ff_rows[:, :width]], axis=1)
+        send = lax.dynamic_slice_in_dim(send, (1 - ic) * shard, shard, 0).astype(bf16)
+        finals.extend([at_rows, ff_rows, swap(send, "c")])
+    shapes = ((shard, 2 * wide), (shard, half), (shard, 2 * width), (4 * shard, half))
+    summed = run_small(
+        finish_rows, place, finals, [((LAYERS,) + shape, f32) for shape in shapes]
+    )
     grad_tokens = turn(lax.dynamic_slice_in_dim(grad_hidden, ic * rows, rows, 0))
     output = turn(output)
     there = swap(vector, "c")
@@ -907,7 +931,6 @@
         part[:, scale_at : scale_at + heads_here].reshape(LAYERS, heads_here, 1)
         for part in (vector, there)
     )
-    summed = [jnp.stack([grads[which] for grads in matrix_grads]) for which in range(4)]
     return (
         output,
         grad_tokens,

time: 659 us -> 639 us (0.970)
  waiting for transfers between devices: 292 us -> 270 us
  local copies, waits for them, and re-layouts: 54.2 us -> 44.6 us
  starting transfers between devices: 111 us -> 118 us
    ppermute x49, waiting for transfers between devices: 109 us -> 168 us  [swap(): return lax.ppermute(array, axis, SWAP)]
    all_gather x1, waiting for transfers between devices: 55.7 us -> 0.01 us  [gather(): return lax.all_gather(array, ('z', 'x'), axis=0, tiled=True)]
    ppermute x12, waiting for transfers between devices: 51.2 us -> 40 us  [step_z(): total = total + lax.ppermute(there, 'z', ring).astype(f32)]
    ppermute x49, starting transfers between devices: 43.1 us -> 53.3 us  [swap(): return lax.ppermute(array, axis, SWAP)]
    ppermute x9 -> x12, waiting for transfers between devices: 69.3 us -> 62.2 us  [z_pieces(): lax.ppermute(array, 'z', [(i, (i + step) % nz) for i in range(nz)])]
    ppermute x2 -> x0, waiting for transfers between devices: 6.73 us -> none  [local_chip(): lax.ppermute(vector, 'z', [(i, i ^ bit) for i in range(nz)])]
    ppermute x9 -> x12, starting transfers between devices: 38 us -> 42 us  [z_pieces(): lax.ppermute(array, 'z', [(i, (i + step) % nz) for i in range(nz)])]
    pallas_call x6 -> x7, Pallas kernels: 32.7 us -> 36.4 us  [run_small(): pl.pallas_call(body, out_shape=[jax.ShapeDtypeStruct(*out) for out in out...]
  transfers between devices with their start and end apart: 78 -> 79, of which waited for: 29 -> 30; matrix products, arithmetic and copies ran while one was open for 23% -> 23% of each run, Pallas kernels for 8% -> 7%
where the time goes in v4:
time: 639 us; the launch traced here: 632 us
  waiting for transfers between devices  270 us (42%)
  starting transfers between devices  118 us (18%)
  other arithmetic  68.4 us (11%)
  Pallas kernels  64.4 us (10%)
  matrix products  49.2 us (8%)
  local copies, waits for them, and re-layouts  44.6 us (7%)
  between operations  16.7 us (3%)
    ppermute x49, waiting for transfers between devices, swap(): return lax.ppermute(array, axis, SWAP)  168 us
    ppermute x12, waiting for transfers between devices, z_pieces(): lax.ppermute(array, 'z', [(i, (i + step) % nz) for i in range(nz)])  62.2 us
    ppermute x49, starting transfers between devices, swap(): return lax.ppermute(array, axis, SWAP)  53.3 us
    dot_general x24, matrix products, product(): return jnp.dot(left, right, preferred_element_type=jnp.float32)  49.2 us
    ppermute x12, starting transfers between devices, z_pieces(): lax.ppermute(array, 'z', [(i, (i + step) % nz) for i in range(nz)])  42 us
    ppermute x12, waiting for transfers between devices, step_z(): total = total + lax.ppermute(there, 'z', ring).astype(f32)  40 us
    pallas_call x7, Pallas kernels, run_small(): pl.pallas_call(body, out_shape=[jax.ShapeDtypeStruct(*out) for out in out...  36.4 us
    pallas_call x6, Pallas kernels, term_product(): pl.pallas_call(body, out_shape=jax.ShapeDtypeStruct(shape, jnp.bfloat16),...  28 us
  transfers between devices with their start and end apart: 79, of which 30 were waited for; matrix products, arithmetic and copies ran while one was open for 23% of the time, Pallas kernels for 7%

profile of v4, /device:TPU:0, one launch (start us, length us, event | category | flops | bytes accessed | tf_op | source)
XLA Modules:
  0.0 631.7 jit_solution(8116461852512301712)
XLA Ops:
  7.8 4.8 shard_map.203
  16.5 3.5 shard_map.204
  20.7 4.2 collective-permute-start.12
  41.0 8.9 %collective-permute-done.3 = bf16[128,1024]{1,0:T(8,128)(2,1)S(1)} collective-permute-done((bf16[128,1024]{1,0:T(8,128)(2,1)S(1)}, bf16[128,1024]{1,0:T(8,128)(2,1)S(1)}, u32[]{:S(2)}, u32[]{:S(2)}) %collective-permute-start.3) | collective-permute-done | bytes 262176 | tf_op jit(solution)/shard_map/ppermute | solution.py:672
  49.9 6.9 %collective-permute-start.4 = (bf16[128,1024]{1,0:T(8,128)(2,1)S(1)}, bf16[128,1024]{1,0:T(8,128)(2,1)S(1)}, u32[]{:S(2)}, u32[]{:S(2)}) collective-permute-start(bf16[128,1024]{1,0:T(8,128)(2,1)S(1)} %copy-done.76), channel_id=1, source_target_pairs={{0,8},{8,16},{16,24},{24,0},{1,9},{9,17},{17,25},{25,1},{2,10},{10... | collective-permute-start | bytes 786440 | tf_op jit(solution)/shard_map/ppermute | solution.py:672
  60.8 22.5 %collective-permute-done.4 = bf16[128,1024]{1,0:T(8,128)(2,1)S(1)} collective-permute-done((bf16[128,1024]{1,0:T(8,128)(2,1)S(1)}, bf16[128,1024]{1,0:T(8,128)(2,1)S(1)}, u32[]{:S(2)}, u32[]{:S(2)}) %collective-permute-start.4) | collective-permute-done | bytes 262176 | tf_op jit(solution)/shard_map/ppermute | solution.py:672
  85.9 4.7 collective-permute-done.21
  90.6 22.0 %collective-permute-start.23 = (bf16[128,1024]{1,0:T(8,128)(2,1)S(1)}, bf16[128,1024]{1,0:T(8,128)(2,1)S(1)}, u32[]{:S(2)}, u32[]{:S(2)}) collective-permute-start(bf16[128,1024]{1,0:T(8,128)(2,1)S(1)} %copy-done.76), channel_id=1, source_target_pairs={{0,16},{8,24},{16,0},{24,8},{1,17},{9,25},{17,1},{25,9},{2,18},{10... | collective-permute-start | bytes 786440 | tf_op jit(solution)/shard_map/ppermute | solution.py:672
  116.3 7.1 %collective-permute-done.17 = bf16[128,1024]{1,0:T(8,128)(2,1)S(1)} collective-permute-done((bf16[128,1024]{1,0:T(8,128)(2,1)S(1)}, bf16[128,1024]{1,0:T(8,128)(2,1)S(1)}, u32[]{:S(2)}, u32[]{:S(2)}) %collective-permute-start.17) | collective-permute-done | bytes 262176 | tf_op jit(solution)/shard_map/ppermute | solution.py:583
  125.0 4.0 collective-permute-done.19
  137.6 27.6 %collective-permute-done.24 = bf16[128,1024]{1,0:T(8,128)(2,1)S(1)} collective-permute-done((bf16[128,1024]{1,0:T(8,128)(2,1)S(1)}, bf16[128,1024]{1,0:T(8,128)(2,1)S(1)}, u32[]{:S(2)}, u32[]{:S(2)}) %collective-permute-start.24) | collective-permute-done | bytes 262176 | tf_op jit(solution)/shard_map/ppermute | solution.py:583
  169.2 9.5 %collective-permute-done.26 = bf16[128,1024]{1,0:T(8,128)(2,1)S(1)} collective-permute-done((bf16[128,1024]{1,0:T(8,128)(2,1)S(1)}, bf16[128,1024]{1,0:T(8,128)(2,1)S(1)}, u32[]{:S(2)}, u32[]{:S(2)}) %collective-permute-start.26) | collective-permute-done | bytes 262176 | tf_op jit(solution)/shard_map/ppermute | solution.py:583
  183.4 10.7 %collective-permute-done.8 = bf16[128,2048]{1,0:T(8,128)(2,1)S(1)} collective-permute-done((bf16[128,2048]{1,0:T(8,128)(2,1)S(1)}, bf16[128,2048]{1,0:T(8,128)(2,1)S(1)}, u32[]{:S(2)}, u32[]{:S(2)}) %collective-permute-start.8) | collective-permute-done | bytes 524320 | tf_op jit(solution)/shard_map/ppermute | solution.py:672
  196.0 15.6 %collective-permute-done.10 = bf16[128,2048]{1,0:T(8,128)(2,1)S(1)} collective-permute-done((bf16[128,2048]{1,0:T(8,128)(2,1)S(1)}, bf16[128,2048]{1,0:T(8,128)(2,1)S(1)}, u32[]{:S(2)}, u32[]{:S(2)}) %collective-permute-start.10) | collective-permute-done | bytes 524320 | tf_op jit(solution)/shard_map/ppermute | solution.py:672
  213.7 23.9 %collective-permute-done.9 = bf16[128,2048]{1,0:T(8,128)(2,1)S(1)} collective-permute-done((bf16[128,2048]{1,0:T(8,128)(2,1)S(1)}, bf16[128,2048]{1,0:T(8,128)(2,1)S(1)}, u32[]{:S(2)}, u32[]{:S(2)}) %collective-permute-start.9) | collective-permute-done | bytes 524320 | tf_op jit(solution)/shard_map/ppermute | solution.py:583
  237.7 17.3 %collective-permute-done.11 = bf16[128,2048]{1,0:T(8,128)(2,1)S(1)} collective-permute-done((bf16[128,2048]{1,0:T(8,128)(2,1)S(1)}, bf16[128,2048]{1,0:T(8,128)(2,1)S(1)}, u32[]{:S(2)}, u32[]{:S(2)}) %collective-permute-start.11) | collective-permute-done | bytes 524320 | tf_op jit(solution)/shard_map/ppermute | solution.py:583
  258.8 4.8 shard_map.205
  274.1 2.8 fusion.174
  280.3 2.7 fusion.139
  295.0 3.8 fusion.11.project_ref
  298.8 5.0 shard_map.206
  308.7 3.3 fusion.28
  313.1 6.1 collective-permute-done.32.refs_2_
  342.8 5.9 collective-permute-done.38.refs_2_
  360.7 7.2 %shard_map.207 = (bf16[256,1536]{1,0:T(8,128)(2,1)}, f32[4,128]{1,0:T(4,128)}) custom-call(f32[8]{0:T(128)} %fusion.129.scale_ref, bf16[256,1536]{1,0:T(8,128)(2,1)} %fusion.11.project_ref, s32[256,1]{1,0:T(8,128)} %copy.28.starts_ref, bf16[256,512]{1,0:T(8,128)(2,1)} %convolution_convert_fusion.3.grad_ref), custom_call_target="tpu_custom_call" | custom-call | tf_op jit(solution)/shard_map/pallas_call | solution.py:571
  371.3 15.9 %collective-permute-done.40.refs_5_ = bf16[256,1536]{1,0:T(8,128)(2,1)} collective-permute-done((bf16[256,1536]{1,0:T(8,128)(2,1)}, bf16[256,1536]{1,0:T(8,128)(2,1)}, u32[]{:S(2)}, u32[]{:S(2)}) %collective-permute-start.40) | collective-permute-done | bytes 786464 | tf_op jit(solution)/shard_map/ppermute | solution.py:583
  387.1 6.7 %shard_map.208 = bf16[1024,2048]{1,0:T(8,128)(2,1)} custom-call(bf16[256,1024]{1,0:T(8,128)(2,1)} %copy-done.44, bf16[256,2048]{1,0:T(8,128)(2,1)} %copy-done.18, bf16[256,1024]{1,0:T(8,128)(2,1)} %copy-done.64, bf16[256,2048]{1,0:T(8,128)(2,1)} %collective-permute-done.41.refs_3_, bf16[256,1536]{1,0:T(8,128)(2,1)} %pad_maximum_fusion.13.refs_4_, ...), custom_call_target="tpu_custom_call" | custom-call | tf_op jit(solution)/shard_map/pallas_call | solution.py:561
  393.9 4.0 fusion.53
  407.6 3.0 fusion.176
  416.0 2.6 fusion.25
  418.7 3.1 shard_map.210
  421.7 4.0 shard_map.209
  440.8 7.2 %shard_map.211 = (bf16[256,1536]{1,0:T(8,128)(2,1)}, f32[4,128]{1,0:T(4,128)}) custom-call(f32[8]{0:T(128)} %fusion.128.scale_ref, bf16[256,1536]{1,0:T(8,128)(2,1)} %fusion.8.project_ref, s32[256,1]{1,0:T(8,128)} %copy.28.starts_ref, bf16[256,512]{1,0:T(8,128)(2,1)} %convolution_convert_fusion.2.grad_ref), custom_call_target="tpu_custom_call" | custom-call | tf_op jit(solution)/shard_map/pallas_call | solution.py:571
  452.5 5.1 collective-permute-done.46.refs_5_
  457.6 3.2 fusion.50
  463.1 7.0 %shard_map.214 = bf16[1024,2048]{1,0:T(8,128)(2,1)} custom-call(bf16[256,1024]{1,0:T(8,128)(2,1)} %add_convert_fusion.4.refs_0_, bf16[256,2048]{1,0:T(8,128)(2,1)} %copy-done.8, bf16[256,1024]{1,0:T(8,128)(2,1)} %collective-permute-done.32.refs_2_, bf16[256,2048]{1,0:T(8,128)(2,1)} %collective-permute-done.47.refs_3_, ...), custom_call_target="tpu_custom_call" | custom-call | tf_op jit(solution)/shard_map/pallas_call | solution.py:561
  476.7 5.0 collective-permute-done.58
  484.1 4.0 shard_map.212
  488.1 3.1 shard_map.213
  507.6 8.6 %collective-permute-start.70 = (bf16[128,1024]{1,0:T(8,128)(2,1)S(1)}, bf16[128,1024]{1,0:T(8,128)(2,1)S(1)}, u32[]{:S(2)}, u32[]{:S(2)}) collective-permute-start(bf16[128,1024]{1,0:T(8,128)(2,1)S(1)} %get-tuple-element.158), channel_id=1, source_target_pairs={{0,16},{8,24},{16,0},{24,8},{1,17},{9,25},{17,1},{25,9},{2,18},{10... | collective-permute-start | bytes 786440 | tf_op jit(solution)/shard_map/ppermute | solution.py:661
  527.5 3.4 collective-permute-done.70
  535.5 10.7 %collective-permute-done.60 = bf16[4,128,1024]{2,1,0:T(8,128)(2,1)} collective-permute-done((bf16[4,128,1024]{2,1,0:T(8,128)(2,1)}, bf16[4,128,1024]{2,1,0:T(8,128)(2,1)}, u32[]{:S(2)}, u32[]{:S(2)}) %collective-permute-start.60) | collective-permute-done | bytes 1048608 | tf_op jit(solution)/shard_map/ppermute | solution.py:583
  548.1 19.8 %collective-permute-done.64 = bf16[4,128,1024]{2,1,0:T(8,128)(2,1)S(1)} collective-permute-done((bf16[4,128,1024]{2,1,0:T(8,128)(2,1)}, bf16[4,128,1024]{2,1,0:T(8,128)(2,1)S(1)}, u32[]{:S(2)}, u32[]{:S(2)}) %collective-permute-start.64) | collective-permute-done | bytes 1048608 | tf_op jit(solution)/shard_map/ppermute | solution.py:583
  567.9 3.8 collective-permute-start.63
  573.8 3.4 collective-permute-start.67
  579.5 14.1 %collective-permute-done.62 = bf16[128,1024]{1,0:T(8,128)(2,1)S(1)} collective-permute-done((bf16[128,1024]{1,0:T(8,128)(2,1)S(1)}, bf16[128,1024]{1,0:T(8,128)(2,1)S(1)}, u32[]{:S(2)}, u32[]{:S(2)}) %collective-permute-start.62) | collective-permute-done | bytes 262176 | tf_op jit(solution)/shard_map/ppermute | solution.py:661
  595.4 19.6 %collective-permute-done.66 = bf16[128,1024]{1,0:T(8,128)(2,1)S(1)} collective-permute-done((bf16[128,1024]{1,0:T(8,128)(2,1)S(1)}, bf16[128,1024]{1,0:T(8,128)(2,1)S(1)}, u32[]{:S(2)}, u32[]{:S(2)}) %collective-permute-start.66) | collective-permute-done | bytes 262176 | tf_op jit(solution)/shard_map/ppermute | solution.py:661
  619.2 3.9 shard_map.215
  (602 shorter events, 219.1 us)
Async XLA Ops:
  7.2 285.6 %all-gather.2.cloned.1.call-start = ((), (), s32[]{:S(2)}) async-start(), calls=%async_computation.1 | async-start | bytes 14155776 | tf_op jit(solution)/shard_map/all_gather | solution.py:644
  20.0 595.2 %reduce-scatter.2.cloned.1.call-start = ((), (), s32[]{:S(2)}) async-start(), calls=%async_computation.2 | async-start | bytes 4718592 | tf_op jit(solution)/shard_map/reduce_scatter | solution.py:647
  30.7 235.3 %collective-permute-start.34 = (bf16[128,1024]{1,0:T(8,128)(2,1)}, bf16[128,1024]{1,0:T(8,128)(2,1)}, u32[]{:S(2)}, u32[]{:S(2)}) collective-permute-start(bf16[128,1024]{1,0:T(8,128)(2,1)} %collective-permute-done.33), channel_id=1, source_target_pairs={{0,2},{2,0},{1,3},{3,1},{4,6},{6,4},{5,7},{7,5},{8,10},{10,8},{9,1... | collective-permute-start | bytes 786440 | tf_op jit(solution)/shard_map/ppermute | solution.py:583
  35.2 24.0 %collective-permute-start.14 = (bf16[128,1024]{1,0:T(8,128)(2,1)S(1)}, bf16[128,1024]{1,0:T(8,128)(2,1)S(1)}, u32[]{:S(2)}, u32[]{:S(2)}) collective-permute-start(bf16[128,1024]{1,0:T(8,128)(2,1)S(1)} %copy-done.77), channel_id=1, source_target_pairs={{0,4},{4,0},{1,5},{5,1},{2,6},{6,2},{3,7},{7,3},{8,12},{12,8},{9,1... | collective-permute-start | bytes 786440 | tf_op jit(solution)/shard_map/ppermute | solution.py:583
  36.8 77.3 %collective-permute-start.16 = (bf16[128,1024]{1,0:T(8,128)(2,1)S(1)}, bf16[128,1024]{1,0:T(8,128)(2,1)S(1)}, u32[]{:S(2)}, u32[]{:S(2)}) collective-permute-start(bf16[128,1024]{1,0:T(8,128)(2,1)S(1)} %copy-done.77), channel_id=1, source_target_pairs={{0,16},{8,24},{16,0},{24,8},{1,17},{9,25},{17,1},{25,9},{2,18},{10... | collective-permute-start | bytes 786440 | tf_op jit(solution)/shard_map/ppermute | solution.py:672
  39.4 74.7 %collective-permute-start.18 = (bf16[128,1024]{1,0:T(8,128)(2,1)S(1)}, bf16[128,1024]{1,0:T(8,128)(2,1)S(1)}, u32[]{:S(2)}, u32[]{:S(2)}) collective-permute-start(bf16[128,1024]{1,0:T(8,128)(2,1)S(1)} %copy-done.77), channel_id=1, source_target_pairs={{0,24},{8,0},{16,8},{24,16},{1,25},{9,1},{17,9},{25,17},{2,26},{10... | collective-permute-start | bytes 786440 | tf_op jit(solution)/shard_map/ppermute | solution.py:672
  49.9 33.4 %collective-permute-start.4 = (bf16[128,1024]{1,0:T(8,128)(2,1)S(1)}, bf16[128,1024]{1,0:T(8,128)(2,1)S(1)}, u32[]{:S(2)}, u32[]{:S(2)}) collective-permute-start(bf16[128,1024]{1,0:T(8,128)(2,1)S(1)} %copy-done.76), channel_id=1, source_target_pairs={{0,8},{8,16},{16,24},{24,0},{1,9},{9,17},{17,25},{25,1},{2,10},{10... | collective-permute-start | bytes 786440 | tf_op jit(solution)/shard_map/ppermute | solution.py:672
  59.2 56.5 %collective-permute-start.15 = (bf16[128,1024]{1,0:T(8,128)(2,1)S(1)}, bf16[128,1024]{1,0:T(8,128)(2,1)S(1)}, u32[]{:S(2)}, u32[]{:S(2)}) collective-permute-start(bf16[128,1024]{1,0:T(8,128)(2,1)S(1)} %collective-permute-done.3), channel_id=1, source_target_pairs={{0,4},{4,0},{1,5},{5,1},{2,6},{6,2},{3,7},{7,3},{8,12},{12,8},{9,1... | collective-permute-start | bytes 786440 | tf_op jit(solution)/shard_map/ppermute | solution.py:583
  90.6 40.0 %collective-permute-start.23 = (bf16[128,1024]{1,0:T(8,128)(2,1)S(1)}, bf16[128,1024]{1,0:T(8,128)(2,1)S(1)}, u32[]{:S(2)}, u32[]{:S(2)}) collective-permute-start(bf16[128,1024]{1,0:T(8,128)(2,1)S(1)} %copy-done.76), channel_id=1, source_target_pairs={{0,16},{8,24},{16,0},{24,8},{1,17},{9,25},{17,1},{25,9},{2,18},{10... | collective-permute-start | bytes 786440 | tf_op jit(solution)/shard_map/ppermute | solution.py:672
  114.1 23.6 %collective-permute-start.25 = (bf16[128,1024]{1,0:T(8,128)(2,1)S(1)}, bf16[128,1024]{1,0:T(8,128)(2,1)S(1)}, u32[]{:S(2)}, u32[]{:S(2)}) collective-permute-start(bf16[128,1024]{1,0:T(8,128)(2,1)S(1)} %copy-done.76), channel_id=1, source_target_pairs={{0,24},{8,0},{16,8},{24,16},{1,25},{9,1},{17,9},{25,17},{2,26},{10... | collective-permute-start | bytes 786440 | tf_op jit(solution)/shard_map/ppermute | solution.py:672
  129.0 50.7 %collective-permute-start.5 = (bf16[128,2048]{1,0:T(8,128)(2,1)S(1)}, bf16[128,2048]{1,0:T(8,128)(2,1)S(1)}, u32[]{:S(2)}, u32[]{:S(2)}) collective-permute-start(bf16[128,2048]{1,0:T(8,128)(2,1)S(1)} %copy-done.65), channel_id=1, source_target_pairs={{0,4},{4,0},{1,5},{5,1},{2,6},{6,2},{3,7},{7,3},{8,12},{12,8},{9,1... | collective-permute-start | bytes 1572872 | tf_op jit(solution)/shard_map/ppermute | solution.py:583
  130.6 50.6 %collective-permute-start.6 = (bf16[128,2048]{1,0:T(8,128)(2,1)S(1)}, bf16[128,2048]{1,0:T(8,128)(2,1)S(1)}, u32[]{:S(2)}, u32[]{:S(2)}) collective-permute-start(bf16[128,2048]{1,0:T(8,128)(2,1)S(1)} %copy-done.65), channel_id=1, source_target_pairs={{0,8},{8,16},{16,24},{24,0},{1,9},{9,17},{17,25},{25,1},{2,10},{10... | collective-permute-start | bytes 1572872 | tf_op jit(solution)/shard_map/ppermute | solution.py:672
  134.6 30.7 %collective-permute-start.24 = (bf16[128,1024]{1,0:T(8,128)(2,1)S(1)}, bf16[128,1024]{1,0:T(8,128)(2,1)S(1)}, u32[]{:S(2)}, u32[]{:S(2)}) collective-permute-start(bf16[128,1024]{1,0:T(8,128)(2,1)S(1)} %collective-permute-done.23), channel_id=1, source_target_pairs={{0,4},{4,0},{1,5},{5,1},{2,6},{6,2},{3,7},{7,3},{8,12},{12,8},{9,1... | collective-permute-start | bytes 786440 | tf_op jit(solution)/shard_map/ppermute | solution.py:583
  137.6 56.5 %collective-permute-start.8 = (bf16[128,2048]{1,0:T(8,128)(2,1)S(1)}, bf16[128,2048]{1,0:T(8,128)(2,1)S(1)}, u32[]{:S(2)}, u32[]{:S(2)}) collective-permute-start(bf16[128,2048]{1,0:T(8,128)(2,1)S(1)} %copy-done.65), channel_id=1, source_target_pairs={{0,16},{8,24},{16,0},{24,8},{1,17},{9,25},{17,1},{25,9},{2,18},{10... | collective-permute-start | bytes 1572872 | tf_op jit(solution)/shard_map/ppermute | solution.py:672
  178.7 32.9 %collective-permute-start.10 = (bf16[128,2048]{1,0:T(8,128)(2,1)S(1)}, bf16[128,2048]{1,0:T(8,128)(2,1)S(1)}, u32[]{:S(2)}, u32[]{:S(2)}) collective-permute-start(bf16[128,2048]{1,0:T(8,128)(2,1)S(1)} %copy-done.65), channel_id=1, source_target_pairs={{0,24},{8,0},{16,8},{24,16},{1,25},{9,1},{17,9},{25,17},{2,26},{10... | collective-permute-start | bytes 1572872 | tf_op jit(solution)/shard_map/ppermute | solution.py:672
  179.6 89.6 %collective-permute-start.20 = (bf16[1024,1024]{1,0:T(8,128)(2,1)S(1)}, bf16[1024,1024]{1,0:T(8,128)(2,1)}, u32[]{:S(2)}, u32[]{:S(2)}) collective-permute-start(bf16[1024,1024]{1,0:T(8,128)(2,1)S(1)} %bitcast.256), channel_id=1, source_target_pairs={{0,1},{1,0},{2,3},{3,2},{4,5},{5,4},{6,7},{7,6},{8,9},{9,8},{10,11... | collective-permute-start | bytes 6291464 | tf_op jit(solution)/shard_map/ppermute | solution.py:583
  181.2 31.9 %collective-permute-start.7 = (bf16[128,2048]{1,0:T(8,128)(2,1)S(1)}, bf16[128,2048]{1,0:T(8,128)(2,1)S(1)}, u32[]{:S(2)}, u32[]{:S(2)}) collective-permute-start(bf16[128,2048]{1,0:T(8,128)(2,1)S(1)} %collective-permute-done.6), channel_id=1, source_target_pairs={{0,4},{4,0},{1,5},{5,1},{2,6},{6,2},{3,7},{7,3},{8,12},{12,8},{9,1... | collective-permute-start | bytes 1572872 | tf_op jit(solution)/shard_map/ppermute | solution.py:583
  194.1 75.1 %collective-permute-start.27 = (bf16[1024,1024]{1,0:T(8,128)(2,1)}, bf16[1024,1024]{1,0:T(8,128)(2,1)}, u32[]{:S(2)}, u32[]{:S(2)}) collective-permute-start(bf16[1024,1024]{1,0:T(8,128)(2,1)} %bitcast.34), channel_id=1, source_target_pairs={{0,1},{1,0},{2,3},{3,2},{4,5},{5,4},{6,7},{7,6},{8,9},{9,8},{10,11... | collective-permute-start | bytes 6291464 | tf_op jit(solution)/shard_map/ppermute | solution.py:583
  211.6 26.0 %collective-permute-start.9 = (bf16[128,2048]{1,0:T(8,128)(2,1)S(1)}, bf16[128,2048]{1,0:T(8,128)(2,1)S(1)}, u32[]{:S(2)}, u32[]{:S(2)}) collective-permute-start(bf16[128,2048]{1,0:T(8,128)(2,1)S(1)} %collective-permute-done.8), channel_id=1, source_target_pairs={{0,4},{4,0},{1,5},{5,1},{2,6},{6,2},{3,7},{7,3},{8,12},{12,8},{9,1... | collective-permute-start | bytes 1572872 | tf_op jit(solution)/shard_map/ppermute | solution.py:583
  213.1 41.9 %collective-permute-start.11 = (bf16[128,2048]{1,0:T(8,128)(2,1)S(1)}, bf16[128,2048]{1,0:T(8,128)(2,1)S(1)}, u32[]{:S(2)}, u32[]{:S(2)}) collective-permute-start(bf16[128,2048]{1,0:T(8,128)(2,1)S(1)} %collective-permute-done.10), channel_id=1, source_target_pairs={{0,4},{4,0},{1,5},{5,1},{2,6},{6,2},{3,7},{7,3},{8,12},{12,8},{9,1... | collective-permute-start | bytes 1572872 | tf_op jit(solution)/shard_map/ppermute | solution.py:583
  286.9 26.3 %collective-permute-start.31 = (bf16[256,1536]{1,0:T(8,128)(2,1)}, bf16[256,1536]{1,0:T(8,128)(2,1)}, u32[]{:S(2)}, u32[]{:S(2)}) collective-permute-start(bf16[256,1536]{1,0:T(8,128)(2,1)} %pad_maximum_fusion.10.refs_0_), channel_id=1, source_target_pairs={{0,1},{1,0},{2,3},{3,2},{4,5},{5,4},{6,7},{7,6},{8,9},{9,8},{10,11... | collective-permute-start | bytes 2359304 | tf_op jit(solution)/shard_map/ppermute | solution.py:583
  289.3 29.9 %collective-permute-start.32 = (bf16[256,1024]{1,0:T(8,128)(2,1)}, bf16[256,1024]{1,0:T(8,128)(2,1)}, u32[]{:S(2)}, u32[]{:S(2)}) collective-permute-start(bf16[256,1024]{1,0:T(8,128)(2,1)} %add_convert_fusion.4.refs_0_), channel_id=1, source_target_pairs={{0,1},{1,0},{2,3},{3,2},{4,5},{5,4},{6,7},{7,6},{8,9},{9,8},{10,11... | collective-permute-start | bytes 1572872 | tf_op jit(solution)/shard_map/ppermute | solution.py:583
  306.7 36.1 %collective-permute-start.37 = (bf16[256,1536]{1,0:T(8,128)(2,1)}, bf16[256,1536]{1,0:T(8,128)(2,1)}, u32[]{:S(2)}, u32[]{:S(2)}) collective-permute-start(bf16[256,1536]{1,0:T(8,128)(2,1)} %pad_maximum_fusion.11.refs_0_), channel_id=1, source_target_pairs={{0,1},{1,0},{2,3},{3,2},{4,5},{5,4},{6,7},{7,6},{8,9},{9,8},{10,11... | collective-permute-start | bytes 2359304 | tf_op jit(solution)/shard_map/ppermute | solution.py:583
  338.5 32.8 %collective-permute-start.41 = (bf16[256,2048]{1,0:T(8,128)(2,1)}, bf16[256,2048]{1,0:T(8,128)(2,1)}, u32[]{:S(2)}, u32[]{:S(2)}) collective-permute-start(bf16[256,2048]{1,0:T(8,128)(2,1)} %pad_maximum_fusion.7), channel_id=1, source_target_pairs={{0,1},{1,0},{2,3},{3,2},{4,5},{5,4},{6,7},{7,6},{8,9},{9,8},{10,11... | collective-permute-start | bytes 3145736 | tf_op jit(solution)/shard_map/ppermute | solution.py:583
  352.2 35.0 %collective-permute-start.40 = (bf16[256,1536]{1,0:T(8,128)(2,1)}, bf16[256,1536]{1,0:T(8,128)(2,1)}, u32[]{:S(2)}, u32[]{:S(2)}) collective-permute-start(bf16[256,1536]{1,0:T(8,128)(2,1)} %pad_maximum_fusion.12), channel_id=1, source_target_pairs={{0,1},{1,0},{2,3},{3,2},{4,5},{5,4},{6,7},{7,6},{8,9},{9,8},{10,11... | collective-permute-start | bytes 2359304 | tf_op jit(solution)/shard_map/ppermute | solution.py:583
  399.6 19.0 %collective-permute-start.44 = (bf16[256,1280]{1,0:T(8,128)(2,1)}, bf16[256,1280]{1,0:T(8,128)(2,1)}, u32[]{:S(2)}, u32[]{:S(2)}) collective-permute-start(bf16[256,1280]{1,0:T(8,128)(2,1)} %pad_maximum_fusion.21), channel_id=1, source_target_pairs={{0,1},{1,0},{2,3},{3,2},{4,5},{5,4},{6,7},{7,6},{8,9},{9,8},{10,11... | collective-permute-start | bytes 1966088 | tf_op jit(solution)/shard_map/ppermute | solution.py:583
  415.1 42.5 %collective-permute-start.47 = (bf16[256,2048]{1,0:T(8,128)(2,1)}, bf16[256,2048]{1,0:T(8,128)(2,1)}, u32[]{:S(2)}, u32[]{:S(2)}) collective-permute-start(bf16[256,2048]{1,0:T(8,128)(2,1)} %pad_maximum_fusion.8), channel_id=1, source_target_pairs={{0,1},{1,0},{2,3},{3,2},{4,5},{5,4},{6,7},{7,6},{8,9},{9,8},{10,11... | collective-permute-start | bytes 3145736 | tf_op jit(solution)/shard_map/ppermute | solution.py:583
  431.1 26.5 %collective-permute-start.46 = (bf16[256,1536]{1,0:T(8,128)(2,1)}, bf16[256,1536]{1,0:T(8,128)(2,1)}, u32[]{:S(2)}, u32[]{:S(2)}) collective-permute-start(bf16[256,1536]{1,0:T(8,128)(2,1)} %pad_maximum_fusion.14), channel_id=1, source_target_pairs={{0,1},{1,0},{2,3},{3,2},{4,5},{5,4},{6,7},{7,6},{8,9},{9,8},{10,11... | collective-permute-start | bytes 2359304 | tf_op jit(solution)/shard_map/ppermute | solution.py:583
  450.3 43.9 %collective-permute-start.52 = (bf16[4,128,1024]{2,1,0:T(8,128)(2,1)}, bf16[4,128,1024]{2,1,0:T(8,128)(2,1)}, u32[]{:S(2)}, u32[]{:S(2)}) collective-permute-start(bf16[4,128,1024]{2,1,0:T(8,128)(2,1)} %dynamic-slice_bitcast_fusion.2), channel_id=1, source_target_pairs={{0,4},{4,0},{1,5},{5,1},{2,6},{6,2},{3,7},{7,3},{8,12},{12,8},{9,1... | collective-permute-start | bytes 3145736 | tf_op jit(solution)/shard_map/ppermute | solution.py:583
  462.6 20.7 %collective-permute-start.48 = (bf16[256,1280]{1,0:T(8,128)(2,1)}, bf16[256,1280]{1,0:T(8,128)(2,1)S(1)}, u32[]{:S(2)}, u32[]{:S(2)}) collective-permute-start(bf16[256,1280]{1,0:T(8,128)(2,1)} %pad_maximum_fusion.24), channel_id=1, source_target_pairs={{0,1},{1,0},{2,3},{3,2},{4,5},{5,4},{6,7},{7,6},{8,9},{9,8},{10,11... | collective-permute-start | bytes 1966088 | tf_op jit(solution)/shard_map/ppermute | solution.py:583
  493.5 38.7 %collective-permute-start.49 = (bf16[4,128,1024]{2,1,0:T(8,128)(2,1)}, bf16[4,128,1024]{2,1,0:T(8,128)(2,1)}, u32[]{:S(2)}, u32[]{:S(2)}) collective-permute-start(bf16[4,128,1024]{2,1,0:T(8,128)(2,1)} %fusion.80), channel_id=1, source_target_pairs={{0,4},{4,0},{1,5},{5,1},{2,6},{6,2},{3,7},{7,3},{8,12},{12,8},{9,1... | collective-permute-start | bytes 3145736 | tf_op jit(solution)/shard_map/ppermute | solution.py:583
  496.4 30.0 %collective-permute-start.71 = (bf16[128,1024]{1,0:T(8,128)(2,1)S(1)}, bf16[128,1024]{1,0:T(8,128)(2,1)S(1)}, u32[]{:S(2)}, u32[]{:S(2)}) collective-permute-start(bf16[128,1024]{1,0:T(8,128)(2,1)S(1)} %get-tuple-element.157), channel_id=1, source_target_pairs={{0,24},{8,0},{16,8},{24,16},{1,25},{9,1},{17,9},{25,17},{2,26},{10... | collective-permute-start | bytes 786440 | tf_op jit(solution)/shard_map/ppermute | solution.py:661
  500.5 17.9 %collective-permute-start.74 = (f32[2,10368]{1,0:T(2,128)S(1)}, f32[2,10368]{1,0:T(2,128)S(1)}, u32[]{:S(2)}, u32[]{:S(2)}) collective-permute-start(f32[2,10368]{1,0:T(2,128)S(1)} %fusion.199), channel_id=1, source_target_pairs={{0,16},{8,24},{16,0},{24,8},{1,17},{9,25},{17,1},{25,9},{2,18},{10... | collective-permute-start | bytes 248840 | tf_op jit(solution)/shard_map/ppermute | solution.py:672
  501.6 16.8 %collective-permute-start.73 = (f32[2,10368]{1,0:T(2,128)S(1)}, f32[2,10368]{1,0:T(2,128)S(1)}, u32[]{:S(2)}, u32[]{:S(2)}) collective-permute-start(f32[2,10368]{1,0:T(2,128)S(1)} %fusion.199), channel_id=1, source_target_pairs={{0,8},{8,16},{16,24},{24,0},{1,9},{9,17},{17,25},{25,1},{2,10},{10... | collective-permute-start | bytes 248840 | tf_op jit(solution)/shard_map/ppermute | solution.py:672
  507.6 23.4 %collective-permute-start.70 = (bf16[128,1024]{1,0:T(8,128)(2,1)S(1)}, bf16[128,1024]{1,0:T(8,128)(2,1)S(1)}, u32[]{:S(2)}, u32[]{:S(2)}) collective-permute-start(bf16[128,1024]{1,0:T(8,128)(2,1)S(1)} %get-tuple-element.158), channel_id=1, source_target_pairs={{0,16},{8,24},{16,0},{24,8},{1,17},{9,25},{17,1},{25,9},{2,18},{10... | collective-permute-start | bytes 786440 | tf_op jit(solution)/shard_map/ppermute | solution.py:661
  519.8 26.3 %collective-permute-start.60 = (bf16[4,128,1024]{2,1,0:T(8,128)(2,1)}, bf16[4,128,1024]{2,1,0:T(8,128)(2,1)}, u32[]{:S(2)}, u32[]{:S(2)}) collective-permute-start(bf16[4,128,1024]{2,1,0:T(8,128)(2,1)} %dynamic-slice_bitcast_fusion.1), channel_id=1, source_target_pairs={{0,4},{4,0},{1,5},{5,1},{2,6},{6,2},{3,7},{7,3},{8,12},{12,8},{9,1... | collective-permute-start | bytes 3145736 | tf_op jit(solution)/shard_map/ppermute | solution.py:583
  526.4 41.5 %collective-permute-start.64 = (bf16[4,128,1024]{2,1,0:T(8,128)(2,1)}, bf16[4,128,1024]{2,1,0:T(8,128)(2,1)S(1)}, u32[]{:S(2)}, u32[]{:S(2)}) collective-permute-start(bf16[4,128,1024]{2,1,0:T(8,128)(2,1)} %dynamic-slice_bitcast_fusion), channel_id=1, source_target_pairs={{0,4},{4,0},{1,5},{5,1},{2,6},{6,2},{3,7},{7,3},{8,12},{12,8},{9,1... | collective-permute-start | bytes 3145736 | tf_op jit(solution)/shard_map/ppermute | solution.py:583
  534.0 39.8 %collective-permute-start.53 = (bf16[128,1024]{1,0:T(8,128)(2,1)S(1)}, bf16[128,1024]{1,0:T(8,128)(2,1)S(1)}, u32[]{:S(2)}, u32[]{:S(2)}) collective-permute-start(bf16[128,1024]{1,0:T(8,128)(2,1)S(1)} %copy-done.75), channel_id=1, source_target_pairs={{0,0},{1,2},{2,1},{3,3},{4,4},{5,6},{6,5},{7,7},{8,8},{9,10},{10,9... | collective-permute-start | bytes 786440 | tf_op jit(solution)/shard_map/ppermute | solution.py:587
  535.0 37.2 %collective-permute-start.57 = (bf16[128,1024]{1,0:T(8,128)(2,1)S(1)}, bf16[128,1024]{1,0:T(8,128)(2,1)S(1)}, u32[]{:S(2)}, u32[]{:S(2)}) collective-permute-start(bf16[128,1024]{1,0:T(8,128)(2,1)S(1)} %get-tuple-element.166), channel_id=1, source_target_pairs={{0,24},{8,0},{16,8},{24,16},{1,25},{9,1},{17,9},{25,17},{2,26},{10... | collective-permute-start | bytes 786440 | tf_op jit(solution)/shard_map/ppermute | solution.py:661
  535.4 36.8 %collective-permute-start.56 = (bf16[128,1024]{1,0:T(8,128)(2,1)S(1)}, bf16[128,1024]{1,0:T(8,128)(2,1)S(1)}, u32[]{:S(2)}, u32[]{:S(2)}) collective-permute-start(bf16[128,1024]{1,0:T(8,128)(2,1)S(1)} %get-tuple-element.167), channel_id=1, source_target_pairs={{0,16},{8,24},{16,0},{24,8},{1,17},{9,25},{17,1},{25,9},{2,18},{10... | collective-permute-start | bytes 786440 | tf_op jit(solution)/shard_map/ppermute | solution.py:661
  546.1 26.8 %collective-permute-start.55 = (bf16[128,1024]{1,0:T(8,128)(2,1)S(1)}, bf16[128,1024]{1,0:T(8,128)(2,1)S(1)}, u32[]{:S(2)}, u32[]{:S(2)}) collective-permute-start(bf16[128,1024]{1,0:T(8,128)(2,1)S(1)} %get-tuple-element.165), channel_id=1, source_target_pairs={{0,8},{8,16},{16,24},{24,0},{1,9},{9,17},{17,25},{25,1},{2,10},{10... | collective-permute-start | bytes 786440 | tf_op jit(solution)/shard_map/ppermute | solution.py:661
  572.2 21.4 %collective-permute-start.62 = (bf16[128,1024]{1,0:T(8,128)(2,1)S(1)}, bf16[128,1024]{1,0:T(8,128)(2,1)S(1)}, u32[]{:S(2)}, u32[]{:S(2)}) collective-permute-start(bf16[128,1024]{1,0:T(8,128)(2,1)S(1)} %get-tuple-element.161), channel_id=1, source_target_pairs={{0,16},{8,24},{16,0},{24,8},{1,17},{9,25},{17,1},{25,9},{2,18},{10... | collective-permute-start | bytes 786440 | tf_op jit(solution)/shard_map/ppermute | solution.py:661
  572.3 21.3 %collective-permute-start.61 = (bf16[128,1024]{1,0:T(8,128)(2,1)S(1)}, bf16[128,1024]{1,0:T(8,128)(2,1)S(1)}, u32[]{:S(2)}, u32[]{:S(2)}) collective-permute-start(bf16[128,1024]{1,0:T(8,128)(2,1)S(1)} %get-tuple-element.159), channel_id=1, source_target_pairs={{0,8},{8,16},{16,24},{24,0},{1,9},{9,17},{17,25},{25,1},{2,10},{10... | collective-permute-start | bytes 786440 | tf_op jit(solution)/shard_map/ppermute | solution.py:661
  572.9 44.5 %collective-permute-start.54 = (f32[128,1024]{1,0:T(8,128)S(1)}, f32[128,1024]{1,0:T(8,128)S(1)}, u32[]{:S(2)}, u32[]{:S(2)}) collective-permute-start(f32[128,1024]{1,0:T(8,128)S(1)} %constant_dynamic-slice_fusion.3), channel_id=1, source_target_pairs={{0,0},{1,2},{2,1},{3,3},{4,4},{5,6},{6,5},{7,7},{8,8},{9,10},{10,9... | collective-permute-start | bytes 1572872 | tf_op jit(solution)/shard_map/ppermute | solution.py:587
  573.8 21.6 %collective-permute-start.67 = (bf16[128,1024]{1,0:T(8,128)(2,1)S(1)}, bf16[128,1024]{1,0:T(8,128)(2,1)S(1)}, u32[]{:S(2)}, u32[]{:S(2)}) collective-permute-start(bf16[128,1024]{1,0:T(8,128)(2,1)S(1)} %get-tuple-element.163), channel_id=1, source_target_pairs={{0,24},{8,0},{16,8},{24,16},{1,25},{9,1},{17,9},{25,17},{2,26},{10... | collective-permute-start | bytes 786440 | tf_op jit(solution)/shard_map/ppermute | solution.py:661
  578.5 36.5 %collective-permute-start.66 = (bf16[128,1024]{1,0:T(8,128)(2,1)S(1)}, bf16[128,1024]{1,0:T(8,128)(2,1)S(1)}, u32[]{:S(2)}, u32[]{:S(2)}) collective-permute-start(bf16[128,1024]{1,0:T(8,128)(2,1)S(1)} %get-tuple-element.164), channel_id=1, source_target_pairs={{0,16},{8,24},{16,0},{24,8},{1,17},{9,25},{17,1},{25,9},{2,18},{10... | collective-permute-start | bytes 786440 | tf_op jit(solution)/shard_map/ppermute | solution.py:661
  593.5 21.5 %collective-permute-start.65 = (bf16[128,1024]{1,0:T(8,128)(2,1)S(1)}, bf16[128,1024]{1,0:T(8,128)(2,1)S(1)}, u32[]{:S(2)}, u32[]{:S(2)}) collective-permute-start(bf16[128,1024]{1,0:T(8,128)(2,1)S(1)} %get-tuple-element.162), channel_id=1, source_target_pairs={{0,8},{8,16},{16,24},{24,0},{1,9},{9,17},{17,25},{25,1},{2,10},{10... | collective-permute-start | bytes 786440 | tf_op jit(solution)/shard_map/ppermute | solution.py:661
  593.7 24.8 %collective-permute-start.68 = (bf16[64,1792]{1,0:T(8,128)(2,1)S(1)}, bf16[64,1792]{1,0:T(8,128)(2,1)S(1)}, u32[]{:S(2)}, u32[]{:S(2)}) collective-permute-start(bf16[64,1792]{1,0:T(8,128)(2,1)S(1)} %fusion.109), channel_id=1, source_target_pairs={{0,2},{2,0},{1,3},{3,1},{4,6},{6,4},{5,7},{7,5},{8,10},{10,8},{9,1... | collective-permute-start | bytes 688136 | tf_op jit(solution)/shard_map/ppermute | solution.py:583
  (135 other events, 1140.2 us)
Sparse Core Ops, SparseCore 0:
  20.1 266.0 all-gather.1
  401.5 97.5 reduce-scatter.1

commit v5 on v4

--- a/solution.py
+++ b/solution.py
@@ -631,6 +631,10 @@
         second = jnp.where(ic == 0, other, own)
         return jnp.concatenate([first, second], axis=axis)
 
+    def across(values):
+        there = swap(lax.dynamic_slice_in_dim(values, ic * rows, rows, 0), "y")
+        return cores(there, swap(there, "c"))
+
     def both_cores(partial_sum):
         low = lax.optimization_barrier(partial_sum.astype(bf16))
         return low.astype(f32) + swap(low, "c").astype(f32)
@@ -739,8 +743,8 @@
         )
         branch = both_cores(product(scaled, out_mat))
         if which == 1:
-            branch, *there = tie(branch, *kept[0][-1][:2])
-            kept[0] = kept[0][:-1] + ((*there, kept[0][-1][2]),)
+            branch, *there = tie(branch, *kept[0][-1][:3])
+            kept[0] = kept[0][:-1] + ((*there, kept[0][-1][3]),)
         else:
             branch, far_up, far_down = tie(branch, up_mat[1], down_mat[1])
             up_mat, down_mat = (up_mat[0], far_up), (down_mat[0], far_down)
@@ -765,15 +769,14 @@
         mixed_low = (norm_m * gain_m + bias_m).astype(bf16)
         near, far = mixed_low[:, :half_units], mixed_low[:, half_units:]
         hidden = middle + both_cores(product(near, down_mat[0]) + product(far, down_mat[1]))
-        attention_in = jnp.concatenate([a_low, scaled], axis=1)
         mixed_there = jnp.concatenate([far, near], axis=1)
         if which == 1:
             mixed_there = swap(mixed_there, "y")
-        ins_there = (swap(attention_in, "y"), swap(b_low, "y"), mixed_there)
+        ins_there = (across(a_low), swap(scaled, "y"), across(b_low), mixed_there)
         kept.append(
             (
                 norm_a, inv_a, project, scale_here, norm_z, inv_z, norm_b, inv_b, pre_act, below, norm_m, inv_m, gain_m,
-                attention_in, b_low, mixed_low, ins_there,
+                a_low, scaled, b_low, mixed_low, ins_there,
             )
         )
     output = lax.dynamic_slice_in_dim(hidden.astype(bf16), ic * rows, rows, 0)
@@ -788,9 +791,9 @@
         qkv_mat, out_mat, up_mat, down_mat = mats[which]
         (
             norm_a, inv_a, project, scale_here, norm_z, inv_z, norm_b, inv_b, pre_act, below, norm_m, inv_m, gain_m,
-            attention_in, b_low, mixed_low, ins_there,
+            a_low, scaled, b_low, mixed_low, ins_there,
         ) = kept[which]
-        attention_there, b_there, mixed_there = ins_there
+        a_there, scaled_there, b_there, mixed_there = ins_there
         if which == 0:
             grad_hidden, mixed_there = tie(grad_hidden, mixed_there)
             mixed_there = swap(mixed_there, "y")
@@ -805,7 +808,9 @@
         slope = below + pre_act * jnp.exp(-0.5 * pre_act * pre_act) * (1.0 / math.sqrt(2 * math.pi))
         grad_pre = (grad_act * slope).astype(bf16)
         if which == 1:
-            grad_pre, attention_there, b_there = tie(grad_pre, attention_there, b_there)
+            grad_pre, a_there, scaled_there, b_there = tie(
+                grad_pre, a_there, scaled_there, b_there
+            )
         else:
             grad_pre, at_there = tie(grad_pre, at_there)
             later = finish_attention(at_there)
@@ -872,15 +877,17 @@
         at_there = swap(at_there, "y")
         grad_hidden = grad_middle + grad_input
 
-        def attention_term(there, here=at_out, ins=attention_in, ins_there=attention_there):
+        def attention_term(
+            there, here=at_out, ins=(a_low, scaled), ins_there=(a_there, scaled_there)
+        ):
             split = half // 2
             rights = (here, there)
             out_term = term_product(
-                (ins,), (ins_there,), rights, ((0, width, wide, half, 0),), (head_width, half)
+                ins[1:], ins_there[1:], rights, ((0, 0, wide, half, 0),), (head_width, half)
             ).reshape(chips, shard, half)
             out_term = jnp.concatenate([out_term[..., :split], out_term[..., split:]], axis=1)
             qkv_term = term_product(
-                (ins,), (ins_there,), rights, ((0, 0, 0, wide, 0),), (width, wide)
+                ins[:1], ins_there[:1], rights, ((0, 0, 0, wide, 0),), (width, wide)
             )
             return jnp.concatenate([qkv_term, out_term.reshape(-1, split)], axis=1)
 

time: 639 us -> 633 us (level)
  waiting for transfers between devices: 270 us -> 253 us
  starting transfers between devices: 118 us -> 132 us
    ppermute x49 -> x55, waiting for transfers between devices: 168 us -> 137 us  [swap(): return lax.ppermute(array, axis, SWAP)]
    ppermute x12, waiting for transfers between devices: 62.2 us -> 76.9 us  [z_pieces(): lax.ppermute(array, 'z', [(i, (i + step) % nz) for i in range(nz)])]
    ppermute x12, starting transfers between devices: 42 us -> 54.9 us  [z_pieces(): lax.ppermute(array, 'z', [(i, (i + step) % nz) for i in range(nz)])]
    ppermute x49 -> x55, starting transfers between devices: 53.3 us -> 47.8 us  [swap(): return lax.ppermute(array, axis, SWAP)]
    unnamed x222 -> x218, local copies, waits for them, and re-layouts: 13.8 us -> 11.9 us
  transfers between devices with their start and end apart: 79 -> 85, of which waited for: 30 -> 29; matrix products, arithmetic and copies ran while one was open for 23% -> 23% of each run, Pallas kernels for 7% -> 8%
where the time goes in v5:
time: 633 us; the launch traced here: 626 us
  waiting for transfers between devices  253 us (40%)
  starting transfers between devices  132 us (21%)
  other arithmetic  65.2 us (10%)
  Pallas kernels  63.5 us (10%)
  matrix products  49.9 us (8%)
  local copies, waits for them, and re-layouts  46.4 us (7%)
  between operations  16.8 us (3%)
    ppermute x55, waiting for transfers between devices, swap(): return lax.ppermute(array, axis, SWAP)  137 us
    ppermute x12, waiting for transfers between devices, z_pieces(): lax.ppermute(array, 'z', [(i, (i + step) % nz) for i in range(nz)])  76.9 us
    ppermute x12, starting transfers between devices, z_pieces(): lax.ppermute(array, 'z', [(i, (i + step) % nz) for i in range(nz)])  54.9 us
    dot_general x24, matrix products, product(): return jnp.dot(left, right, preferred_element_type=jnp.float32)  49.9 us
    ppermute x55, starting transfers between devices, swap(): return lax.ppermute(array, axis, SWAP)  47.8 us
    ppermute x12, waiting for transfers between devices, step_z(): total = total + lax.ppermute(there, 'z', ring).astype(f32)  38.5 us
    pallas_call x7, Pallas kernels, run_small(): pl.pallas_call(body, out_shape=[jax.ShapeDtypeStruct(*out) for out in out...  36.5 us
    pallas_call x6, Pallas kernels, term_product(): pl.pallas_call(body, out_shape=jax.ShapeDtypeStruct(shape, jnp.bfloat16),...  27 us
  transfers between devices with their start and end apart: 85, of which 29 were waited for; matrix products, arithmetic and copies ran while one was open for 23% of the time, Pallas kernels for 8%

profile of v5, /device:TPU:0, one launch (start us, length us, event | category | flops | bytes accessed | tf_op | source)
XLA Modules:
  0.0 626.0 jit_solution(9446874613437048634)
XLA Ops:
  7.8 4.8 shard_map.203
  14.8 2.9 collective-permute-start.12
  17.7 3.6 collective-permute-start.36
  22.3 3.5 shard_map.204
  36.3 3.4 collective-permute-done.3
  39.7 3.7 collective-permute-start.4
  47.4 24.7 %collective-permute-done.4 = bf16[128,1024]{1,0:T(8,128)(2,1)S(1)} collective-permute-done((bf16[128,1024]{1,0:T(8,128)(2,1)S(1)}, bf16[128,1024]{1,0:T(8,128)(2,1)S(1)}, u32[]{:S(2)}, u32[]{:S(2)}) %collective-permute-start.4) | collective-permute-done | bytes 262176 | tf_op jit(solution)/shard_map/ppermute | solution.py:676
  74.8 4.5 collective-permute-done.21
  79.2 20.7 %collective-permute-start.23 = (bf16[128,1024]{1,0:T(8,128)(2,1)S(1)}, bf16[128,1024]{1,0:T(8,128)(2,1)S(1)}, u32[]{:S(2)}, u32[]{:S(2)}) collective-permute-start(bf16[128,1024]{1,0:T(8,128)(2,1)S(1)} %copy-done.77), channel_id=1, source_target_pairs={{0,16},{8,24},{16,0},{24,8},{1,17},{9,25},{17,1},{25,9},{2,18},{10... | collective-permute-start | bytes 786440 | tf_op jit(solution)/shard_map/ppermute | solution.py:676
  103.6 7.1 %collective-permute-done.17 = bf16[128,1024]{1,0:T(8,128)(2,1)S(1)} collective-permute-done((bf16[128,1024]{1,0:T(8,128)(2,1)S(1)}, bf16[128,1024]{1,0:T(8,128)(2,1)S(1)}, u32[]{:S(2)}, u32[]{:S(2)}) %collective-permute-start.17) | collective-permute-done | bytes 262176 | tf_op jit(solution)/shard_map/ppermute | solution.py:583
  112.0 4.3 collective-permute-done.19
  119.5 4.5 collective-permute-start.6
  126.4 13.9 %collective-permute-start.8 = (bf16[128,2048]{1,0:T(8,128)(2,1)S(1)}, bf16[128,2048]{1,0:T(8,128)(2,1)S(1)}, u32[]{:S(2)}, u32[]{:S(2)}) collective-permute-start(bf16[128,2048]{1,0:T(8,128)(2,1)S(1)} %copy-done.67), channel_id=1, source_target_pairs={{0,16},{8,24},{16,0},{24,8},{1,17},{9,25},{17,1},{25,9},{2,18},{10... | collective-permute-start | bytes 1572872 | tf_op jit(solution)/shard_map/ppermute | solution.py:676
  143.2 8.6 %collective-permute-done.26 = bf16[128,1024]{1,0:T(8,128)(2,1)S(1)} collective-permute-done((bf16[128,1024]{1,0:T(8,128)(2,1)S(1)}, bf16[128,1024]{1,0:T(8,128)(2,1)S(1)}, u32[]{:S(2)}, u32[]{:S(2)}) %collective-permute-start.26) | collective-permute-done | bytes 262176 | tf_op jit(solution)/shard_map/ppermute | solution.py:583
  151.8 4.5 collective-permute-start.10
  159.7 27.1 %collective-permute-done.8 = bf16[128,2048]{1,0:T(8,128)(2,1)S(1)} collective-permute-done((bf16[128,2048]{1,0:T(8,128)(2,1)S(1)}, bf16[128,2048]{1,0:T(8,128)(2,1)S(1)}, u32[]{:S(2)}, u32[]{:S(2)}) %collective-permute-start.8) | collective-permute-done | bytes 524320 | tf_op jit(solution)/shard_map/ppermute | solution.py:676
  187.9 8.4 %collective-permute-done.10 = bf16[128,2048]{1,0:T(8,128)(2,1)S(1)} collective-permute-done((bf16[128,2048]{1,0:T(8,128)(2,1)S(1)}, bf16[128,2048]{1,0:T(8,128)(2,1)S(1)}, u32[]{:S(2)}, u32[]{:S(2)}) %collective-permute-start.10) | collective-permute-done | bytes 524320 | tf_op jit(solution)/shard_map/ppermute | solution.py:676
  199.3 23.9 %collective-permute-done.9 = bf16[128,2048]{1,0:T(8,128)(2,1)S(1)} collective-permute-done((bf16[128,2048]{1,0:T(8,128)(2,1)S(1)}, bf16[128,2048]{1,0:T(8,128)(2,1)S(1)}, u32[]{:S(2)}, u32[]{:S(2)}) %collective-permute-start.9) | collective-permute-done | bytes 524320 | tf_op jit(solution)/shard_map/ppermute | solution.py:583
  223.3 19.0 %collective-permute-done.11 = bf16[128,2048]{1,0:T(8,128)(2,1)S(1)} collective-permute-done((bf16[128,2048]{1,0:T(8,128)(2,1)S(1)}, bf16[128,2048]{1,0:T(8,128)(2,1)S(1)}, u32[]{:S(2)}, u32[]{:S(2)}) %collective-permute-start.11) | collective-permute-done | bytes 524320 | tf_op jit(solution)/shard_map/ppermute | solution.py:583
  246.2 4.8 shard_map.205.refs_0_
  274.8 5.2 collective-permute-done.34
  283.9 6.7 %collective-permute-done.40 = bf16[128,1024]{1,0:T(8,128)(2,1)S(1)} collective-permute-done((bf16[128,1024]{1,0:T(8,128)(2,1)S(1)}, bf16[128,1024]{1,0:T(8,128)(2,1)S(1)}, u32[]{:S(2)}, u32[]{:S(2)}) %collective-permute-start.40) | collective-permute-done | bytes 262176 | tf_op jit(solution)/shard_map/ppermute | solution.py:583
  295.3 3.8 fusion.11.project_ref
  299.1 5.0 shard_map.206.refs_0_
  306.8 3.3 fusion.28
  310.1 3.3 fusion.32
  350.0 7.3 %shard_map.207 = (bf16[256,1536]{1,0:T(8,128)(2,1)}, f32[4,128]{1,0:T(4,128)}) custom-call(f32[8]{0:T(128)} %fusion.128.scale_ref, bf16[256,1536]{1,0:T(8,128)(2,1)} %fusion.11.project_ref, s32[256,1]{1,0:T(8,128)} %copy.28.starts_ref, bf16[256,512]{1,0:T(8,128)(2,1)} %convolution_convert_fusion.3.grad_ref), custom_call_target="tpu_custom_call" | custom-call | tf_op jit(solution)/shard_map/pallas_call | solution.py:571
  360.1 14.2 %collective-permute-done.46.refs_5_ = bf16[256,1536]{1,0:T(8,128)(2,1)} collective-permute-done((bf16[256,1536]{1,0:T(8,128)(2,1)}, bf16[256,1536]{1,0:T(8,128)(2,1)}, u32[]{:S(2)}, u32[]{:S(2)}) %collective-permute-start.46) | collective-permute-done | bytes 786464 | tf_op jit(solution)/shard_map/ppermute | solution.py:583
  374.3 6.7 %shard_map.208 = bf16[1024,2048]{1,0:T(8,128)(2,1)} custom-call(bf16[256,1024]{1,0:T(8,128)(2,1)} %copy-done.38, bf16[256,2048]{1,0:T(8,128)(2,1)} %copy-done.19, bf16[256,1024]{1,0:T(8,128)(2,1)} %pad_maximum_fusion.27.refs_2_, bf16[256,2048]{1,0:T(8,128)(2,1)} %collective-permute-done.47.refs_3_, bf16[256,1536]{1,0:T(8,128)(2,1)} %pad_maximum_fusion.11.refs_4_, ...), custom_call_target="tpu_custom_call" | custom-call | tf_op jit(solution)/shard_map/pallas_call | solution.py:561
  381.0 4.0 fusion.53
  413.9 3.9 shard_map.209
  428.5 7.2 %shard_map.211 = (bf16[256,1536]{1,0:T(8,128)(2,1)}, f32[4,128]{1,0:T(4,128)}) custom-call(f32[8]{0:T(128)} %fusion.129.scale_ref, bf16[256,1536]{1,0:T(8,128)(2,1)} %fusion.8.project_ref, s32[256,1]{1,0:T(8,128)} %copy.28.starts_ref, bf16[256,512]{1,0:T(8,128)(2,1)} %convolution_convert_fusion.2.grad_ref), custom_call_target="tpu_custom_call" | custom-call | tf_op jit(solution)/shard_map/pallas_call | solution.py:571
  440.8 2.9 collective-permute-done.52.refs_5_
  443.7 3.2 fusion.50
  449.6 7.0 %shard_map.214 = bf16[1024,2048]{1,0:T(8,128)(2,1)} custom-call(bf16[256,1024]{1,0:T(8,128)(2,1)} %copy-done.13, bf16[256,2048]{1,0:T(8,128)(2,1)} %copy-done.9, bf16[256,1024]{1,0:T(8,128)(2,1)} %get-tuple-element.100.refs_2_, bf16[256,2048]{1,0:T(8,128)(2,1)} %collective-permute-done.53.refs_3_, bf16[256,1536]{1,0:T(8,128)(2,1)} %pad_maximum_fusion.13.refs_4_, ...), custom_call_target="tpu_custom_call" | custom-call | tf_op jit(solution)/shard_map/pallas_call | solution.py:561
  463.0 4.9 collective-permute-done.64
  471.4 3.9 shard_map.212
  483.3 8.8 %collective-permute-start.77 = (bf16[128,1024]{1,0:T(8,128)(2,1)S(1)}, bf16[128,1024]{1,0:T(8,128)(2,1)S(1)}, u32[]{:S(2)}, u32[]{:S(2)}) collective-permute-start(bf16[128,1024]{1,0:T(8,128)(2,1)S(1)} %get-tuple-element.161), channel_id=1, source_target_pairs={{0,24},{8,0},{16,8},{24,16},{1,25},{9,1},{17,9},{25,17},{2,26},{10... | collective-permute-start | bytes 786440 | tf_op jit(solution)/shard_map/ppermute | solution.py:665
  496.1 4.5 collective-permute-done.81
  501.6 6.7 %collective-permute-done.80 = f32[2,10368]{1,0:T(2,128)S(1)} collective-permute-done((f32[2,10368]{1,0:T(2,128)S(1)}, f32[2,10368]{1,0:T(2,128)S(1)}, u32[]{:S(2)}, u32[]{:S(2)}) %collective-permute-start.80) | collective-permute-done | bytes 82976 | tf_op jit(solution)/shard_map/ppermute | solution.py:676
  509.7 6.2 collective-permute-start.66
  529.1 11.1 %collective-permute-done.66 = bf16[4,128,1024]{2,1,0:T(8,128)(2,1)} collective-permute-done((bf16[4,128,1024]{2,1,0:T(8,128)(2,1)}, bf16[4,128,1024]{2,1,0:T(8,128)(2,1)}, u32[]{:S(2)}, u32[]{:S(2)}) %collective-permute-start.66) | collective-permute-done | bytes 1048608 | tf_op jit(solution)/shard_map/ppermute | solution.py:583
  542.2 20.1 %collective-permute-done.70 = bf16[4,128,1024]{2,1,0:T(8,128)(2,1)S(1)} collective-permute-done((bf16[4,128,1024]{2,1,0:T(8,128)(2,1)}, bf16[4,128,1024]{2,1,0:T(8,128)(2,1)S(1)}, u32[]{:S(2)}, u32[]{:S(2)}) %collective-permute-start.70) | collective-permute-done | bytes 1048608 | tf_op jit(solution)/shard_map/ppermute | solution.py:583
  562.3 3.8 collective-permute-start.69
  568.2 3.4 collective-permute-start.73
  573.8 14.2 %collective-permute-done.68 = bf16[128,1024]{1,0:T(8,128)(2,1)S(1)} collective-permute-done((bf16[128,1024]{1,0:T(8,128)(2,1)S(1)}, bf16[128,1024]{1,0:T(8,128)(2,1)S(1)}, u32[]{:S(2)}, u32[]{:S(2)}) %collective-permute-start.68) | collective-permute-done | bytes 262176 | tf_op jit(solution)/shard_map/ppermute | solution.py:665
  589.8 19.5 %collective-permute-done.72 = bf16[128,1024]{1,0:T(8,128)(2,1)S(1)} collective-permute-done((bf16[128,1024]{1,0:T(8,128)(2,1)S(1)}, bf16[128,1024]{1,0:T(8,128)(2,1)S(1)}, u32[]{:S(2)}, u32[]{:S(2)}) %collective-permute-start.72) | collective-permute-done | bytes 262176 | tf_op jit(solution)/shard_map/ppermute | solution.py:665
  613.5 3.9 shard_map.215
  (619 shorter events, 216.7 us)
Async XLA Ops:
  7.2 285.8 %all-gather.2.cloned.1.call-start = ((), (), s32[]{:S(2)}) async-start(), calls=%async_computation.1 | async-start | bytes 14155776 | tf_op jit(solution)/shard_map/all_gather | solution.py:648
  17.7 245.5 %collective-permute-start.36 = (bf16[128,1024]{1,0:T(8,128)(2,1)}, bf16[128,1024]{1,0:T(8,128)(2,1)}, u32[]{:S(2)}, u32[]{:S(2)}) collective-permute-start(bf16[128,1024]{1,0:T(8,128)(2,1)} %param.23), channel_id=1, source_target_pairs={{0,0},{1,2},{2,1},{3,3},{4,4},{5,6},{6,5},{7,7},{8,8},{9,10},{10,9... | collective-permute-start | bytes 786440 | tf_op jit(solution)/shard_map/ppermute | solution.py:587
  25.8 583.7 %reduce-scatter.2.cloned.1.call-start = ((), (), s32[]{:S(2)}) async-start(), calls=%async_computation.2 | async-start | bytes 4718592 | tf_op jit(solution)/shard_map/reduce_scatter | solution.py:651
  30.5 15.3 %collective-permute-start.14 = (bf16[128,1024]{1,0:T(8,128)(2,1)S(1)}, bf16[128,1024]{1,0:T(8,128)(2,1)S(1)}, u32[]{:S(2)}, u32[]{:S(2)}) collective-permute-start(bf16[128,1024]{1,0:T(8,128)(2,1)S(1)} %copy-done.78), channel_id=1, source_target_pairs={{0,4},{4,0},{1,5},{5,1},{2,6},{6,2},{3,7},{7,3},{8,12},{12,8},{9,1... | collective-permute-start | bytes 786440 | tf_op jit(solution)/shard_map/ppermute | solution.py:583
  32.0 69.4 %collective-permute-start.16 = (bf16[128,1024]{1,0:T(8,128)(2,1)S(1)}, bf16[128,1024]{1,0:T(8,128)(2,1)S(1)}, u32[]{:S(2)}, u32[]{:S(2)}) collective-permute-start(bf16[128,1024]{1,0:T(8,128)(2,1)S(1)} %copy-done.78), channel_id=1, source_target_pairs={{0,16},{8,24},{16,0},{24,8},{1,17},{9,25},{17,1},{25,9},{2,18},{10... | collective-permute-start | bytes 786440 | tf_op jit(solution)/shard_map/ppermute | solution.py:676
  34.6 66.8 %collective-permute-start.18 = (bf16[128,1024]{1,0:T(8,128)(2,1)S(1)}, bf16[128,1024]{1,0:T(8,128)(2,1)S(1)}, u32[]{:S(2)}, u32[]{:S(2)}) collective-permute-start(bf16[128,1024]{1,0:T(8,128)(2,1)S(1)} %copy-done.78), channel_id=1, source_target_pairs={{0,24},{8,0},{16,8},{24,16},{1,25},{9,1},{17,9},{25,17},{2,26},{10... | collective-permute-start | bytes 786440 | tf_op jit(solution)/shard_map/ppermute | solution.py:676
  39.7 32.5 %collective-permute-start.4 = (bf16[128,1024]{1,0:T(8,128)(2,1)S(1)}, bf16[128,1024]{1,0:T(8,128)(2,1)S(1)}, u32[]{:S(2)}, u32[]{:S(2)}) collective-permute-start(bf16[128,1024]{1,0:T(8,128)(2,1)S(1)} %copy-done.77), channel_id=1, source_target_pairs={{0,8},{8,16},{16,24},{24,0},{1,9},{9,17},{17,25},{25,1},{2,10},{10... | collective-permute-start | bytes 786440 | tf_op jit(solution)/shard_map/ppermute | solution.py:676
  45.8 57.0 %collective-permute-start.15 = (bf16[128,1024]{1,0:T(8,128)(2,1)S(1)}, bf16[128,1024]{1,0:T(8,128)(2,1)S(1)}, u32[]{:S(2)}, u32[]{:S(2)}) collective-permute-start(bf16[128,1024]{1,0:T(8,128)(2,1)S(1)} %collective-permute-done.3), channel_id=1, source_target_pairs={{0,4},{4,0},{1,5},{5,1},{2,6},{6,2},{3,7},{7,3},{8,12},{12,8},{9,1... | collective-permute-start | bytes 786440 | tf_op jit(solution)/shard_map/ppermute | solution.py:583
  79.2 40.3 %collective-permute-start.23 = (bf16[128,1024]{1,0:T(8,128)(2,1)S(1)}, bf16[128,1024]{1,0:T(8,128)(2,1)S(1)}, u32[]{:S(2)}, u32[]{:S(2)}) collective-permute-start(bf16[128,1024]{1,0:T(8,128)(2,1)S(1)} %copy-done.77), channel_id=1, source_target_pairs={{0,16},{8,24},{16,0},{24,8},{1,17},{9,25},{17,1},{25,9},{2,18},{10... | collective-permute-start | bytes 786440 | tf_op jit(solution)/shard_map/ppermute | solution.py:676
  101.4 25.0 %collective-permute-start.25 = (bf16[128,1024]{1,0:T(8,128)(2,1)S(1)}, bf16[128,1024]{1,0:T(8,128)(2,1)S(1)}, u32[]{:S(2)}, u32[]{:S(2)}) collective-permute-start(bf16[128,1024]{1,0:T(8,128)(2,1)S(1)} %copy-done.77), channel_id=1, source_target_pairs={{0,24},{8,0},{16,8},{24,16},{1,25},{9,1},{17,9},{25,17},{2,26},{10... | collective-permute-start | bytes 786440 | tf_op jit(solution)/shard_map/ppermute | solution.py:676
  116.3 40.8 %collective-permute-start.5 = (bf16[128,2048]{1,0:T(8,128)(2,1)S(1)}, bf16[128,2048]{1,0:T(8,128)(2,1)S(1)}, u32[]{:S(2)}, u32[]{:S(2)}) collective-permute-start(bf16[128,2048]{1,0:T(8,128)(2,1)S(1)} %copy-done.67), channel_id=1, source_target_pairs={{0,4},{4,0},{1,5},{5,1},{2,6},{6,2},{3,7},{7,3},{8,12},{12,8},{9,1... | collective-permute-start | bytes 1572872 | tf_op jit(solution)/shard_map/ppermute | solution.py:583
  119.5 37.5 %collective-permute-start.6 = (bf16[128,2048]{1,0:T(8,128)(2,1)S(1)}, bf16[128,2048]{1,0:T(8,128)(2,1)S(1)}, u32[]{:S(2)}, u32[]{:S(2)}) collective-permute-start(bf16[128,2048]{1,0:T(8,128)(2,1)S(1)} %copy-done.67), channel_id=1, source_target_pairs={{0,8},{8,16},{16,24},{24,0},{1,9},{9,17},{17,25},{25,1},{2,10},{10... | collective-permute-start | bytes 1572872 | tf_op jit(solution)/shard_map/ppermute | solution.py:676
  124.0 16.3 %collective-permute-start.24 = (bf16[128,1024]{1,0:T(8,128)(2,1)S(1)}, bf16[128,1024]{1,0:T(8,128)(2,1)S(1)}, u32[]{:S(2)}, u32[]{:S(2)}) collective-permute-start(bf16[128,1024]{1,0:T(8,128)(2,1)S(1)} %collective-permute-done.23), channel_id=1, source_target_pairs={{0,4},{4,0},{1,5},{5,1},{2,6},{6,2},{3,7},{7,3},{8,12},{12,8},{9,1... | collective-permute-start | bytes 786440 | tf_op jit(solution)/shard_map/ppermute | solution.py:583
  126.4 60.5 %collective-permute-start.8 = (bf16[128,2048]{1,0:T(8,128)(2,1)S(1)}, bf16[128,2048]{1,0:T(8,128)(2,1)S(1)}, u32[]{:S(2)}, u32[]{:S(2)}) collective-permute-start(bf16[128,2048]{1,0:T(8,128)(2,1)S(1)} %copy-done.67), channel_id=1, source_target_pairs={{0,16},{8,24},{16,0},{24,8},{1,17},{9,25},{17,1},{25,9},{2,18},{10... | collective-permute-start | bytes 1572872 | tf_op jit(solution)/shard_map/ppermute | solution.py:676
  151.8 44.5 %collective-permute-start.10 = (bf16[128,2048]{1,0:T(8,128)(2,1)S(1)}, bf16[128,2048]{1,0:T(8,128)(2,1)S(1)}, u32[]{:S(2)}, u32[]{:S(2)}) collective-permute-start(bf16[128,2048]{1,0:T(8,128)(2,1)S(1)} %copy-done.67), channel_id=1, source_target_pairs={{0,24},{8,0},{16,8},{24,16},{1,25},{9,1},{17,9},{25,17},{2,26},{10... | collective-permute-start | bytes 1572872 | tf_op jit(solution)/shard_map/ppermute | solution.py:676
  157.0 98.0 %collective-permute-start.20 = (bf16[1024,1024]{1,0:T(8,128)(2,1)S(1)}, bf16[1024,1024]{1,0:T(8,128)(2,1)}, u32[]{:S(2)}, u32[]{:S(2)}) collective-permute-start(bf16[1024,1024]{1,0:T(8,128)(2,1)S(1)} %bitcast.256), channel_id=1, source_target_pairs={{0,1},{1,0},{2,3},{3,2},{4,5},{5,4},{6,7},{7,6},{8,9},{9,8},{10,11... | collective-permute-start | bytes 6291464 | tf_op jit(solution)/shard_map/ppermute | solution.py:583
  157.0 42.1 %collective-permute-start.7 = (bf16[128,2048]{1,0:T(8,128)(2,1)S(1)}, bf16[128,2048]{1,0:T(8,128)(2,1)S(1)}, u32[]{:S(2)}, u32[]{:S(2)}) collective-permute-start(bf16[128,2048]{1,0:T(8,128)(2,1)S(1)} %collective-permute-done.6), channel_id=1, source_target_pairs={{0,4},{4,0},{1,5},{5,1},{2,6},{6,2},{3,7},{7,3},{8,12},{12,8},{9,1... | collective-permute-start | bytes 1572872 | tf_op jit(solution)/shard_map/ppermute | solution.py:583
  186.8 68.2 %collective-permute-start.27 = (bf16[1024,1024]{1,0:T(8,128)(2,1)}, bf16[1024,1024]{1,0:T(8,128)(2,1)}, u32[]{:S(2)}, u32[]{:S(2)}) collective-permute-start(bf16[1024,1024]{1,0:T(8,128)(2,1)} %bitcast.34), channel_id=1, source_target_pairs={{0,1},{1,0},{2,3},{3,2},{4,5},{5,4},{6,7},{7,6},{8,9},{9,8},{10,11... | collective-permute-start | bytes 6291464 | tf_op jit(solution)/shard_map/ppermute | solution.py:583
  196.3 26.9 %collective-permute-start.9 = (bf16[128,2048]{1,0:T(8,128)(2,1)S(1)}, bf16[128,2048]{1,0:T(8,128)(2,1)S(1)}, u32[]{:S(2)}, u32[]{:S(2)}) collective-permute-start(bf16[128,2048]{1,0:T(8,128)(2,1)S(1)} %collective-permute-done.8), channel_id=1, source_target_pairs={{0,4},{4,0},{1,5},{5,1},{2,6},{6,2},{3,7},{7,3},{8,12},{12,8},{9,1... | collective-permute-start | bytes 1572872 | tf_op jit(solution)/shard_map/ppermute | solution.py:583
  199.2 43.1 %collective-permute-start.11 = (bf16[128,2048]{1,0:T(8,128)(2,1)S(1)}, bf16[128,2048]{1,0:T(8,128)(2,1)S(1)}, u32[]{:S(2)}, u32[]{:S(2)}) collective-permute-start(bf16[128,2048]{1,0:T(8,128)(2,1)S(1)} %collective-permute-done.10), channel_id=1, source_target_pairs={{0,4},{4,0},{1,5},{5,1},{2,6},{6,2},{3,7},{7,3},{8,12},{12,8},{9,1... | collective-permute-start | bytes 1572872 | tf_op jit(solution)/shard_map/ppermute | solution.py:583
  273.6 40.9 %collective-permute-start.33 = (bf16[256,512]{1,0:T(8,128)(2,1)}, bf16[256,512]{1,0:T(8,128)(2,1)}, u32[]{:S(2)}, u32[]{:S(2)}) collective-permute-start(bf16[256,512]{1,0:T(8,128)(2,1)} %shard_map.205.refs_0_), channel_id=1, source_target_pairs={{0,1},{1,0},{2,3},{3,2},{4,5},{5,4},{6,7},{7,6},{8,9},{9,8},{10,11... | collective-permute-start | bytes 786440 | tf_op jit(solution)/shard_map/ppermute | solution.py:583
  304.1 34.9 %collective-permute-start.42 = (bf16[256,512]{1,0:T(8,128)(2,1)}, bf16[256,512]{1,0:T(8,128)(2,1)}, u32[]{:S(2)}, u32[]{:S(2)}) collective-permute-start(bf16[256,512]{1,0:T(8,128)(2,1)} %shard_map.206.refs_0_), channel_id=1, source_target_pairs={{0,1},{1,0},{2,3},{3,2},{4,5},{5,4},{6,7},{7,6},{8,9},{9,8},{10,11... | collective-permute-start | bytes 786440 | tf_op jit(solution)/shard_map/ppermute | solution.py:583
  330.3 29.8 %collective-permute-start.47 = (bf16[256,2048]{1,0:T(8,128)(2,1)}, bf16[256,2048]{1,0:T(8,128)(2,1)}, u32[]{:S(2)}, u32[]{:S(2)}) collective-permute-start(bf16[256,2048]{1,0:T(8,128)(2,1)} %pad_maximum_fusion.7), channel_id=1, source_target_pairs={{0,1},{1,0},{2,3},{3,2},{4,5},{5,4},{6,7},{7,6},{8,9},{9,8},{10,11... | collective-permute-start | bytes 3145736 | tf_op jit(solution)/shard_map/ppermute | solution.py:583
  342.4 31.9 %collective-permute-start.46 = (bf16[256,1536]{1,0:T(8,128)(2,1)}, bf16[256,1536]{1,0:T(8,128)(2,1)}, u32[]{:S(2)}, u32[]{:S(2)}) collective-permute-start(bf16[256,1536]{1,0:T(8,128)(2,1)} %pad_maximum_fusion.10), channel_id=1, source_target_pairs={{0,1},{1,0},{2,3},{3,2},{4,5},{5,4},{6,7},{7,6},{8,9},{9,8},{10,11... | collective-permute-start | bytes 2359304 | tf_op jit(solution)/shard_map/ppermute | solution.py:583
  386.7 18.0 %collective-permute-start.50 = (bf16[256,1280]{1,0:T(8,128)(2,1)}, bf16[256,1280]{1,0:T(8,128)(2,1)}, u32[]{:S(2)}, u32[]{:S(2)}) collective-permute-start(bf16[256,1280]{1,0:T(8,128)(2,1)} %pad_maximum_fusion.19), channel_id=1, source_target_pairs={{0,1},{1,0},{2,3},{3,2},{4,5},{5,4},{6,7},{7,6},{8,9},{9,8},{10,11... | collective-permute-start | bytes 1966088 | tf_op jit(solution)/shard_map/ppermute | solution.py:583
  401.2 42.5 %collective-permute-start.53 = (bf16[256,2048]{1,0:T(8,128)(2,1)}, bf16[256,2048]{1,0:T(8,128)(2,1)}, u32[]{:S(2)}, u32[]{:S(2)}) collective-permute-start(bf16[256,2048]{1,0:T(8,128)(2,1)} %pad_maximum_fusion.8), channel_id=1, source_target_pairs={{0,1},{1,0},{2,3},{3,2},{4,5},{5,4},{6,7},{7,6},{8,9},{9,8},{10,11... | collective-permute-start | bytes 3145736 | tf_op jit(solution)/shard_map/ppermute | solution.py:583
  419.7 24.1 %collective-permute-start.52 = (bf16[256,1536]{1,0:T(8,128)(2,1)}, bf16[256,1536]{1,0:T(8,128)(2,1)}, u32[]{:S(2)}, u32[]{:S(2)}) collective-permute-start(bf16[256,1536]{1,0:T(8,128)(2,1)} %pad_maximum_fusion.12), channel_id=1, source_target_pairs={{0,1},{1,0},{2,3},{3,2},{4,5},{5,4},{6,7},{7,6},{8,9},{9,8},{10,11... | collective-permute-start | bytes 2359304 | tf_op jit(solution)/shard_map/ppermute | solution.py:583
  438.1 42.4 %collective-permute-start.58 = (bf16[4,128,1024]{2,1,0:T(8,128)(2,1)}, bf16[4,128,1024]{2,1,0:T(8,128)(2,1)}, u32[]{:S(2)}, u32[]{:S(2)}) collective-permute-start(bf16[4,128,1024]{2,1,0:T(8,128)(2,1)} %dynamic-slice_bitcast_fusion.2), channel_id=1, source_target_pairs={{0,4},{4,0},{1,5},{5,1},{2,6},{6,2},{3,7},{7,3},{8,12},{12,8},{9,1... | collective-permute-start | bytes 3145736 | tf_op jit(solution)/shard_map/ppermute | solution.py:583
  448.8 21.8 %collective-permute-start.54 = (bf16[256,1280]{1,0:T(8,128)(2,1)}, bf16[256,1280]{1,0:T(8,128)(2,1)S(1)}, u32[]{:S(2)}, u32[]{:S(2)}) collective-permute-start(bf16[256,1280]{1,0:T(8,128)(2,1)} %pad_maximum_fusion.22), channel_id=1, source_target_pairs={{0,1},{1,0},{2,3},{3,2},{4,5},{5,4},{6,7},{7,6},{8,9},{9,8},{10,11... | collective-permute-start | bytes 1966088 | tf_op jit(solution)/shard_map/ppermute | solution.py:583
  468.6 23.5 %collective-permute-start.65 = (f32[2,10368]{1,0:T(2,128)}, f32[2,10368]{1,0:T(2,128)S(1)}, u32[]{:S(2)}, u32[]{:S(2)}) collective-permute-start(f32[2,10368]{1,0:T(2,128)} %fusion.136), channel_id=1, source_target_pairs={{0,4},{4,0},{1,5},{5,1},{2,6},{6,2},{3,7},{7,3},{8,12},{12,8},{9,1... | collective-permute-start | bytes 248840 | tf_op jit(solution)/shard_map/ppermute | solution.py:583
  480.4 42.5 %collective-permute-start.55 = (bf16[4,128,1024]{2,1,0:T(8,128)(2,1)}, bf16[4,128,1024]{2,1,0:T(8,128)(2,1)}, u32[]{:S(2)}, u32[]{:S(2)}) collective-permute-start(bf16[4,128,1024]{2,1,0:T(8,128)(2,1)} %fusion.80), channel_id=1, source_target_pairs={{0,4},{4,0},{1,5},{5,1},{2,6},{6,2},{3,7},{7,3},{8,12},{12,8},{9,1... | collective-permute-start | bytes 3145736 | tf_op jit(solution)/shard_map/ppermute | solution.py:583
  483.3 35.5 %collective-permute-start.77 = (bf16[128,1024]{1,0:T(8,128)(2,1)S(1)}, bf16[128,1024]{1,0:T(8,128)(2,1)S(1)}, u32[]{:S(2)}, u32[]{:S(2)}) collective-permute-start(bf16[128,1024]{1,0:T(8,128)(2,1)S(1)} %get-tuple-element.161), channel_id=1, source_target_pairs={{0,24},{8,0},{16,8},{24,16},{1,25},{9,1},{17,9},{25,17},{2,26},{10... | collective-permute-start | bytes 786440 | tf_op jit(solution)/shard_map/ppermute | solution.py:665
  492.3 16.0 %collective-permute-start.80 = (f32[2,10368]{1,0:T(2,128)S(1)}, f32[2,10368]{1,0:T(2,128)S(1)}, u32[]{:S(2)}, u32[]{:S(2)}) collective-permute-start(f32[2,10368]{1,0:T(2,128)S(1)} %fusion.199), channel_id=1, source_target_pairs={{0,16},{8,24},{16,0},{24,8},{1,17},{9,25},{17,1},{25,9},{2,18},{10... | collective-permute-start | bytes 248840 | tf_op jit(solution)/shard_map/ppermute | solution.py:676
  492.4 15.9 %collective-permute-start.79 = (f32[2,10368]{1,0:T(2,128)S(1)}, f32[2,10368]{1,0:T(2,128)S(1)}, u32[]{:S(2)}, u32[]{:S(2)}) collective-permute-start(f32[2,10368]{1,0:T(2,128)S(1)} %fusion.199), channel_id=1, source_target_pairs={{0,8},{8,16},{16,24},{24,0},{1,9},{9,17},{17,25},{25,1},{2,10},{10... | collective-permute-start | bytes 248840 | tf_op jit(solution)/shard_map/ppermute | solution.py:676
  500.6 20.8 %collective-permute-start.76 = (bf16[128,1024]{1,0:T(8,128)(2,1)S(1)}, bf16[128,1024]{1,0:T(8,128)(2,1)}, u32[]{:S(2)}, u32[]{:S(2)}) collective-permute-start(bf16[128,1024]{1,0:T(8,128)(2,1)S(1)} %get-tuple-element.162), channel_id=1, source_target_pairs={{0,16},{8,24},{16,0},{24,8},{1,17},{9,25},{17,1},{25,9},{2,18},{10... | collective-permute-start | bytes 786440 | tf_op jit(solution)/shard_map/ppermute | solution.py:665
  509.7 30.5 %collective-permute-start.66 = (bf16[4,128,1024]{2,1,0:T(8,128)(2,1)}, bf16[4,128,1024]{2,1,0:T(8,128)(2,1)}, u32[]{:S(2)}, u32[]{:S(2)}) collective-permute-start(bf16[4,128,1024]{2,1,0:T(8,128)(2,1)} %dynamic-slice_bitcast_fusion.1), channel_id=1, source_target_pairs={{0,4},{4,0},{1,5},{5,1},{2,6},{6,2},{3,7},{7,3},{8,12},{12,8},{9,1... | collective-permute-start | bytes 3145736 | tf_op jit(solution)/shard_map/ppermute | solution.py:583
  518.8 43.5 %collective-permute-start.70 = (bf16[4,128,1024]{2,1,0:T(8,128)(2,1)}, bf16[4,128,1024]{2,1,0:T(8,128)(2,1)S(1)}, u32[]{:S(2)}, u32[]{:S(2)}) collective-permute-start(bf16[4,128,1024]{2,1,0:T(8,128)(2,1)} %dynamic-slice_bitcast_fusion), channel_id=1, source_target_pairs={{0,4},{4,0},{1,5},{5,1},{2,6},{6,2},{3,7},{7,3},{8,12},{12,8},{9,1... | collective-permute-start | bytes 3145736 | tf_op jit(solution)/shard_map/ppermute | solution.py:583
  524.6 43.6 %collective-permute-start.59 = (bf16[128,1024]{1,0:T(8,128)(2,1)S(1)}, bf16[128,1024]{1,0:T(8,128)(2,1)S(1)}, u32[]{:S(2)}, u32[]{:S(2)}) collective-permute-start(bf16[128,1024]{1,0:T(8,128)(2,1)S(1)} %copy-done.76), channel_id=1, source_target_pairs={{0,0},{1,2},{2,1},{3,3},{4,4},{5,6},{6,5},{7,7},{8,8},{9,10},{10,9... | collective-permute-start | bytes 786440 | tf_op jit(solution)/shard_map/ppermute | solution.py:587
  525.5 41.0 %collective-permute-start.63 = (bf16[128,1024]{1,0:T(8,128)(2,1)S(1)}, bf16[128,1024]{1,0:T(8,128)(2,1)S(1)}, u32[]{:S(2)}, u32[]{:S(2)}) collective-permute-start(bf16[128,1024]{1,0:T(8,128)(2,1)S(1)} %get-tuple-element.170), channel_id=1, source_target_pairs={{0,24},{8,0},{16,8},{24,16},{1,25},{9,1},{17,9},{25,17},{2,26},{10... | collective-permute-start | bytes 786440 | tf_op jit(solution)/shard_map/ppermute | solution.py:665
  527.0 39.6 %collective-permute-start.62 = (bf16[128,1024]{1,0:T(8,128)(2,1)S(1)}, bf16[128,1024]{1,0:T(8,128)(2,1)S(1)}, u32[]{:S(2)}, u32[]{:S(2)}) collective-permute-start(bf16[128,1024]{1,0:T(8,128)(2,1)S(1)} %get-tuple-element.171), channel_id=1, source_target_pairs={{0,16},{8,24},{16,0},{24,8},{1,17},{9,25},{17,1},{25,9},{2,18},{10... | collective-permute-start | bytes 786440 | tf_op jit(solution)/shard_map/ppermute | solution.py:665
  540.2 27.1 %collective-permute-start.61 = (bf16[128,1024]{1,0:T(8,128)(2,1)S(1)}, bf16[128,1024]{1,0:T(8,128)(2,1)S(1)}, u32[]{:S(2)}, u32[]{:S(2)}) collective-permute-start(bf16[128,1024]{1,0:T(8,128)(2,1)S(1)} %get-tuple-element.169), channel_id=1, source_target_pairs={{0,8},{8,16},{16,24},{24,0},{1,9},{9,17},{17,25},{25,1},{2,10},{10... | collective-permute-start | bytes 786440 | tf_op jit(solution)/shard_map/ppermute | solution.py:665
  566.5 21.5 %collective-permute-start.68 = (bf16[128,1024]{1,0:T(8,128)(2,1)S(1)}, bf16[128,1024]{1,0:T(8,128)(2,1)S(1)}, u32[]{:S(2)}, u32[]{:S(2)}) collective-permute-start(bf16[128,1024]{1,0:T(8,128)(2,1)S(1)} %get-tuple-element.165), channel_id=1, source_target_pairs={{0,16},{8,24},{16,0},{24,8},{1,17},{9,25},{17,1},{25,9},{2,18},{10... | collective-permute-start | bytes 786440 | tf_op jit(solution)/shard_map/ppermute | solution.py:665
  566.6 21.4 %collective-permute-start.67 = (bf16[128,1024]{1,0:T(8,128)(2,1)S(1)}, bf16[128,1024]{1,0:T(8,128)(2,1)S(1)}, u32[]{:S(2)}, u32[]{:S(2)}) collective-permute-start(bf16[128,1024]{1,0:T(8,128)(2,1)S(1)} %get-tuple-element.163), channel_id=1, source_target_pairs={{0,8},{8,16},{16,24},{24,0},{1,9},{9,17},{17,25},{25,1},{2,10},{10... | collective-permute-start | bytes 786440 | tf_op jit(solution)/shard_map/ppermute | solution.py:665
  567.3 44.4 %collective-permute-start.60 = (f32[128,1024]{1,0:T(8,128)S(1)}, f32[128,1024]{1,0:T(8,128)S(1)}, u32[]{:S(2)}, u32[]{:S(2)}) collective-permute-start(f32[128,1024]{1,0:T(8,128)S(1)} %constant_dynamic-slice_fusion.3), channel_id=1, source_target_pairs={{0,0},{1,2},{2,1},{3,3},{4,4},{5,6},{6,5},{7,7},{8,8},{9,10},{10,9... | collective-permute-start | bytes 1572872 | tf_op jit(solution)/shard_map/ppermute | solution.py:587
  568.2 21.6 %collective-permute-start.73 = (bf16[128,1024]{1,0:T(8,128)(2,1)S(1)}, bf16[128,1024]{1,0:T(8,128)(2,1)S(1)}, u32[]{:S(2)}, u32[]{:S(2)}) collective-permute-start(bf16[128,1024]{1,0:T(8,128)(2,1)S(1)} %get-tuple-element.167), channel_id=1, source_target_pairs={{0,24},{8,0},{16,8},{24,16},{1,25},{9,1},{17,9},{25,17},{2,26},{10... | collective-permute-start | bytes 786440 | tf_op jit(solution)/shard_map/ppermute | solution.py:665
  572.9 36.4 %collective-permute-start.72 = (bf16[128,1024]{1,0:T(8,128)(2,1)S(1)}, bf16[128,1024]{1,0:T(8,128)(2,1)S(1)}, u32[]{:S(2)}, u32[]{:S(2)}) collective-permute-start(bf16[128,1024]{1,0:T(8,128)(2,1)S(1)} %get-tuple-element.168), channel_id=1, source_target_pairs={{0,16},{8,24},{16,0},{24,8},{1,17},{9,25},{17,1},{25,9},{2,18},{10... | collective-permute-start | bytes 786440 | tf_op jit(solution)/shard_map/ppermute | solution.py:665
  588.0 21.3 %collective-permute-start.71 = (bf16[128,1024]{1,0:T(8,128)(2,1)S(1)}, bf16[128,1024]{1,0:T(8,128)(2,1)S(1)}, u32[]{:S(2)}, u32[]{:S(2)}) collective-permute-start(bf16[128,1024]{1,0:T(8,128)(2,1)S(1)} %get-tuple-element.166), channel_id=1, source_target_pairs={{0,8},{8,16},{16,24},{24,0},{1,9},{9,17},{17,25},{25,1},{2,10},{10... | collective-permute-start | bytes 786440 | tf_op jit(solution)/shard_map/ppermute | solution.py:665
  588.9 23.9 %collective-permute-start.74 = (bf16[64,1792]{1,0:T(8,128)(2,1)}, bf16[64,1792]{1,0:T(8,128)(2,1)}, u32[]{:S(2)}, u32[]{:S(2)}) collective-permute-start(bf16[64,1792]{1,0:T(8,128)(2,1)} %fusion.109), channel_id=1, source_target_pairs={{0,2},{2,0},{1,3},{3,1},{4,6},{6,4},{5,7},{7,5},{8,10},{10,8},{9,1... | collective-permute-start | bytes 688136 | tf_op jit(solution)/shard_map/ppermute | solution.py:583
  (139 other events, 1162.8 us)
Sparse Core Ops, SparseCore 0:
  25.9 256.8 all-gather.1
  388.0 104.8 reduce-scatter.1
